TPU v7x, 128 devices: a whole 4x4x4 slice. The times are simulated.
128 devices in a mesh: src: 32 (over x, z, core), tgt: 4 (over y).
Axes of the slice: x: 4, y: 4, z: 4, core: 2. Of those that a mesh axis runs over, the one named last changes fastest.
Arguments:
- src_pts: float32 [3, 512, 256], P(None, 'src'), may hold values from -8 to 9
- src_mass: float32 [512, 256], P('src'), may hold values from 0.25 to 4
- tgt_pts: float32 [3, 256, 1024], P(None, None, 'tgt'), may hold values from -6 to 6
- tgt_mass: float32 [256, 1024], P(None, 'tgt'), may hold values from 0.25 to 4
- listed: int32 [512, 4, 8], P('src', 'tgt'), may hold values from 0 to 255, all different within a row
- live: int32 [512, 4], P('src', 'tgt'), may hold values from 1 to 8, 16 in all within a row
Outputs:
- fine_f: float32 [512, 256], P('src')
- fine_g: float32 [256, 1024], P('src', 'tgt')
Inputs may be any that keep to these rules, and one draw needn't show every extreme that they name: Within one row listed[c, t, :] the entries are distinct; only the first live[c, t] of them are used. For each source cluster c the counts live[c, :] add up to 16.
All inputs are finite; a program needn't handle non-finite values. No bound on the sum of `live` on one device may be relied on, other than what follows from the above.
Results may differ from a plain program's by a relative error of at most 0.0003.
Values sent between devices are 32-bit elements; how exact they have to be, the bound alone decides.
No kernel may reach another device: no remote copies, remote signals or barrier semaphores. Data moves between devices by JAX's collectives and lax.ppermute only.
A program may use at most 128 MiB of HBM per device.

v0:
```python
import functools
import math

import jax
import jax.numpy as jnp
from jax import lax
from jax.experimental import pallas as pl
from jax.experimental.pallas import tpu as pltpu
from jax.sharding import PartitionSpec as P

EPS = 0.1
NEG = -1e30
ALPHA = math.log2(math.e) / EPS
UNSCALE = EPS * math.log(2.0)
F32, BF16, I32 = jnp.float32, jnp.bfloat16, jnp.int32
CL, SLOTS, PTS, TGT = 16, 8, 256, 256
BLOCKS = CL * SLOTS
UNROLL = 8
AHEAD = 4
PAD = 16
LIST = BLOCKS + 2 * PAD
LIMIT = 16 << 20
VMEM = pl.BlockSpec(memory_space=pltpu.VMEM)
SMEM = pl.BlockSpec(memory_space=pltpu.SMEM)


def iota(shape, dim):
    return lax.broadcasted_iota(I32, shape, dim)


def bf16_part(value):
    big = value * 65537.0
    return big - (big - value)


def split3(value):
    high = bf16_part(value)
    rest = value - high
    mid = bf16_part(rest)
    return high, mid, rest - mid


def centroid_kernel(sp, sm, tp, tm, row_out, own_out, slice_out):
    s, t = lax.axis_index("src"), lax.axis_index("tgt")
    mass = sm[...]
    total = jnp.sum(mass, axis=1, keepdims=True)
    inv = 1.0 / total
    cols = [jnp.sum(sp[d] * mass, axis=1, keepdims=True) * inv for d in range(3)]
    cols.append(jnp.log2(total))
    lane = iota((CL, 128), 1)
    z = jnp.zeros((CL, 128), F32)
    for q in range(4):
        z = jnp.where(lane == q, cols[q], z)
    zt = jnp.concatenate([z, jnp.zeros((128 - CL, 128), F32)], axis=0).T
    lane = iota((1, 128), 1)
    row = jnp.zeros((1, 128), F32)
    for q in range(4):
        piece = pltpu.roll(zt[q : q + 1, :], lax.rem(128 - 4 * t, 128), 1)
        row = row + pltpu.roll(jnp.where(lane < 4, piece, 0.0), 4 * q, 1)
    slice_out[...] = tm[pl.ds(pl.multiple_of(8 * s, 8), 8), :]
    weight = tm[...]
    total = jnp.sum(weight, axis=0, keepdims=True)
    inv = 1.0 / total
    rows = [jnp.sum(tp[d] * weight, axis=0, keepdims=True) * inv for d in range(3)]
    rows.append(jnp.log2(total))
    for q in range(4):
        own_out[q : q + 1, :] = rows[q]
        half = jnp.where(s >= 16, rows[q][:, 128:], rows[q][:, :128])
        piece = pltpu.roll(half, lax.rem(128 - 8 * lax.rem(s, 16), 128), 1)
        row = row + pltpu.roll(jnp.where(lane < 8, piece, 0.0), 16 + 8 * q, 1)
    row_out[...] = jnp.broadcast_to(row, row_out.shape)


def dup(table, r, piece):
    for h in range(2):
        table[h, pl.ds(r, CL, stride=16), :] = piece[:, 128 * h : 128 * h + 128]


def own_terms(tp, tm):
    return jnp.log2(tm[...]) - (0.5 * ALPHA) * (tp[0] * tp[0] + tp[1] * tp[1] + tp[2] * tp[2])


def fill_order(order, listed, live):
    n = 0
    for c in range(CL):
        for k in range(SLOTS):
            order[n + k] = (k * CL + c) * TGT + listed[k, c]
        n = n + live[0, c]
    for u in range(PAD):
        order[n + u] = order[0]
    order[LIST - 1] = n
    return n


def target_tables(tab, tp, base):
    for d in range(3):
        a, b, _ = split3(tp[d].T)
        tab[2 * d] = a
        tab[2 * d + 1] = b
    for r, piece in enumerate(split3(base)):
        tab[6 + r] = piece


def target_factors(tab, at):
    sub = iota((16, PTS), 0)
    stack = jnp.ones((16, PTS), F32)
    for r, q in enumerate((0, 0, 1, 2, 2, 3, 4, 4, 5, 6, 7, 8)):
        stack = jnp.where(sub == r, tab[q, pl.ds(at, 1), :], stack)
    return stack


def source_factors(table, x, own):
    for d in range(3):
        a, b, _ = split3(x[d])
        for r, piece in enumerate((a, b, a)):
            dup(table, 3 * d + r, piece)
    for r in range(9, 12):
        dup(table, r, jnp.ones((CL, PTS), F32))
    for r, piece in enumerate(own):
        dup(table, 12 + r, piece)


def row_kernel(listed, live, sp, tp, tm, r_out, l_out, order, gt, gf, tab, scol, lrow, *sets):
    sets = [sets[3 * u : 3 * u + 3] for u in range(AHEAD)]
    n = fill_order(order, listed, live)
    zero = jnp.zeros((CL, PTS), F32)
    source_factors(gf, [sp[d] * ALPHA for d in range(3)], [zero] * 4)
    for c in range(CL):
        gt[c] = jnp.concatenate([gf[h, 16 * c : 16 * c + 16, :] for h in range(2)], axis=1).astype(BF16)
    target_tables(tab, tp, own_terms(tp, tm).T)

    def prepare(i, lhs):
        at = order[i] & (TGT - 1)
        lhs[...] = target_factors(tab, at).astype(BF16).T
        lrow[pl.ds(order[i] >> 8, 1), :] = jnp.broadcast_to(at.astype(F32), (1, 128))

    for u in range(AHEAD):
        prepare(u, sets[u][0])

    def batch(i, _):
        at = AHEAD * i
        v = [jnp.dot(sets[u][0][...], gt[(order[at + u] >> 8) & (CL - 1)], preferred_element_type=F32) for u in range(AHEAD)]
        for u in range(AHEAD):
            prepare(at + AHEAD + u, sets[u][0])
        for u in range(AHEAD):
            lhs, score, tops = sets[u]
            top_old = tops[...]
            total = jnp.zeros((8, PTS), F32)
            top = jnp.full((8, PTS), NEG, F32)
            for j in range(0, TGT, 8):
                total = total + jnp.exp2(score[j : j + 8, :] - top_old)
                score[j : j + 8, :] = v[u][j : j + 8, :]
                top = jnp.maximum(top, v[u][j : j + 8, :])
            tops[...] = jnp.broadcast_to(jnp.max(top, axis=0, keepdims=True), (8, PTS))
            old = order[jnp.maximum(at - AHEAD + u, 0)] >> 8
            r_out[pl.ds(old, 1), :] = top_old[0:1, :]
            scol[pl.ds(old, 1), :] = jnp.sum(total, axis=0, keepdims=True)
        return 0

    lax.fori_loop(0, (n + AHEAD - 1) // AHEAD + 1, batch, 0)
    xn = (-0.5 * ALPHA) * (sp[0] * sp[0] + sp[1] * sp[1] + sp[2] * sp[2])
    lane = iota((1, 128), 1)
    have = jnp.zeros((1, 128), I32)
    for c in range(CL):
        have = jnp.where((lane & (CL - 1)) == c, live[0, c], have)
    ok = jnp.broadcast_to(jnp.where((lane >> 4) < have, 1.0, 0.0), (128, 128)).T[:, 0:1] > 0.5
    r = r_out[...] + jnp.log2(scol[...])
    r = (r.reshape(SLOTS, CL, PTS) + xn[None]).reshape(BLOCKS, PTS)
    r_out[...] = jnp.where(ok, r, NEG)
    l_out[...] = jnp.where(ok, lrow[...], -1.0)


def coarse_kernel(got, own, r_in, l_in, g_out, l_out, terms, scores):
    turned = got[...].T

    def side(rows):
        norm = rows[0] * rows[0] + rows[1] * rows[1] + rows[2] * rows[2]
        return [rows[0], rows[1], rows[2], rows[3] - (0.5 * ALPHA) * norm]

    tgt = [side([turned[16 + 8 * q + li : 17 + 8 * q + li, :] for q in range(4)]) for li in range(8)]
    mine = side([own[q : q + 1, :] for q in range(4)])
    step = 32
    top_g = jnp.full((8, TGT), NEG, F32)
    for ci in range(4):
        for i in range(0, 128, step):
            x = [jnp.broadcast_to(ALPHA * got[i : i + step, 4 * d + ci : 4 * d + ci + 1], (step, 128)) for d in range(3)]
            peak = None
            for li, y in enumerate(tgt):
                v = (y[3] + x[0] * y[0]) + (x[1] * y[1] + x[2] * y[2])
                scores[li] = v
                peak = v if peak is None else jnp.maximum(peak, v)
            peak = jnp.max(peak, axis=1, keepdims=True)
            total = jnp.exp2(scores[0] - peak)
            for li in range(1, 8):
                total = total + jnp.exp2(scores[li] - peak)
            total = jnp.sum(total, axis=1, keepdims=True)
            const = got[i : i + step, 12 + ci : 13 + ci] - (peak + jnp.log2(total))
            const = jnp.broadcast_to(const, (step, 128))
            for h in (0, 128):
                y = [row[:, h : h + 128] for row in mine]
                v = (const + x[0] * y[0]) + (x[1] * y[1] + x[2] * y[2])
                terms[128 * ci + i : 128 * ci + i + step, h : h + 128] = v
    for i in range(0, 512, 8):
        top_g = jnp.maximum(top_g, terms[i : i + 8, :])
    top = jnp.max(top_g, axis=0, keepdims=True)
    total = jnp.zeros((8, TGT), F32)
    for i in range(0, 512, 8):
        total = total + jnp.exp2(terms[i : i + 8, :] - top)
    g = (mine[3] - own[3:4, :]) + top + jnp.log2(jnp.sum(total, axis=0, keepdims=True))
    g = -g
    g_out[...] = jnp.broadcast_to(g, g_out.shape)
    at = l_in[...]
    lane = iota((128, 128), 1).astype(F32)
    hit = jnp.where(at == lane, g[:, :128], 0.0) + jnp.where(at == lane + 128.0, g[:, 128:], 0.0)
    picked = jnp.sum(hit, axis=1, keepdims=True)
    r = (r_in[...] + picked).reshape(SLOTS, CL, PTS)
    top = jnp.max(r, axis=0)
    l_out[...] = top + jnp.log2(jnp.sum(jnp.exp2(r - top[None]), axis=0))


def column_kernel(order, sp, sm, tp, tm, g, l0, l1, l2, l3, f_out, s_out, gt, gf, tab, st):
    parts = [p[...] for p in (l0, l1, l2, l3)]
    top = functools.reduce(jnp.maximum, parts)
    f = -(top + jnp.log2(sum(jnp.exp2(p - top) for p in parts)))
    f_out[...] = f * UNSCALE
    st[...] = jnp.zeros_like(st)
    own = f + jnp.log2(sm[...]) - (0.5 * ALPHA) * (sp[0] * sp[0] + sp[1] * sp[1] + sp[2] * sp[2])
    zero = jnp.zeros((CL, PTS), F32)
    source_factors(gf, [sp[d] * ALPHA for d in range(3)], (*split3(own), zero))
    for c in range(CL):
        gt[c] = jnp.concatenate([gf[h, 16 * c : 16 * c + 16, :] for h in range(2)], axis=1).astype(BF16).T
    target_tables(tab, tp, (own_terms(tp, tm) + g[0:1, :]).T)
    n = order[LIST - 1]

    def batch(i, _):
        at = i * UNROLL
        v = []
        for u in range(UNROLL):
            left = gt[(order[at + u] >> 8) & (CL - 1)]
            right = target_factors(tab, order[at + u] & (TGT - 1)).astype(BF16)
            v.append(jnp.dot(left, right, preferred_element_type=F32))
        lines = []
        for u in range(UNROLL):
            total = jnp.zeros((8, TGT), F32)
            for o in range(0, PTS, 8):
                total = total + jnp.exp2(v[u][o : o + 8, :])
            line = jnp.sum(total, axis=0, keepdims=True)
            lines.append(jnp.where(at + u < n, line, 0.0))
        for u in range(UNROLL):
            to = pl.ds(order[at + u] & (TGT - 1), 1)
            st[to, :] = st[to, :] + lines[u]
        return 0

    lax.fori_loop(0, (n + UNROLL - 1) // UNROLL, batch, 0)
    s_out[...] = st[...].T.reshape(32, 8, TGT)


def final_kernel(arrived, mass, g, out):
    total = jnp.sum(arrived[...], axis=0)
    out[...] = (g[...] - jnp.log2(1.0 + total / mass[...])) * UNSCALE


def on_device(src_pts, src_mass, tgt_pts, tgt_mass, listed, live):
    shape = jax.ShapeDtypeStruct
    params = pltpu.CompilerParams(vmem_limit_bytes=LIMIT)
    row, own, mass = pl.pallas_call(
        centroid_kernel,
        out_shape=(shape((128, 128), F32), shape((8, 256), F32), shape((8, 256), F32)),
        in_specs=[VMEM] * 4,
        out_specs=(VMEM, VMEM, VMEM),
        name="centroids",
    )(src_pts, src_mass, tgt_pts, tgt_mass)
    got = lax.all_to_all(row, ("src", "tgt"), split_axis=0, concat_axis=0, tiled=True)
    slots = listed.transpose(1, 2, 0).reshape(SLOTS, CL)
    counts = live.transpose(1, 0)
    r, where, order = pl.pallas_call(
        row_kernel,
        out_shape=(shape((BLOCKS, PTS), F32), shape((128, 128), F32), shape((LIST,), I32)),
        in_specs=[SMEM, SMEM, VMEM, VMEM, VMEM],
        out_specs=(VMEM, VMEM, SMEM),
        scratch_shapes=[
            pltpu.VMEM((CL, 16, PTS), BF16),
            pltpu.VMEM((2, CL * 16, 128), F32),
            pltpu.VMEM((9, TGT, PTS), F32),
            pltpu.VMEM((BLOCKS, PTS), F32),
            pltpu.VMEM((BLOCKS, 128), F32),
        ]
        + [pltpu.VMEM((TGT, 16), BF16), pltpu.VMEM((TGT, PTS), F32), pltpu.VMEM((8, PTS), F32)] * AHEAD,
        cost_estimate=pl.CostEstimate(flops=100_000_000, bytes_accessed=10_000_000, transcendentals=5_000_000),
        compiler_params=params,
        name="rows",
    )(slots, counts, src_pts, tgt_pts, tgt_mass)
    g, part = pl.pallas_call(
        coarse_kernel,
        out_shape=(shape((8, 256), F32), shape((CL, PTS), F32)),
        in_specs=[VMEM] * 4,
        out_specs=(VMEM, VMEM),
        scratch_shapes=[pltpu.VMEM((512, 256), F32), pltpu.VMEM((8, 32, 128), F32)],
        compiler_params=params,
        name="coarse",
    )(got, own, r, where)
    parts = [part] + [
        lax.ppermute(part, "tgt", [(i, (i + k) % 4) for i in range(4)]) for k in (1, 2, 3)
    ]
    fine_f, sums = pl.pallas_call(
        column_kernel,
        out_shape=(shape((CL, PTS), F32), shape((32, 8, TGT), F32)),
        in_specs=[SMEM] + [VMEM] * 9,
        out_specs=(VMEM, VMEM),
        scratch_shapes=[
            pltpu.VMEM((CL, PTS, 16), BF16),
            pltpu.VMEM((2, CL * 16, 128), F32),
            pltpu.VMEM((9, TGT, PTS), F32),
            pltpu.VMEM((TGT, PTS), F32),
        ],
        compiler_params=params,
        name="columns",
    )(order, src_pts, src_mass, tgt_pts, tgt_mass, g, *parts)
    arrived = lax.all_to_all(sums, "src", split_axis=0, concat_axis=0, tiled=True)
    fine_g = pl.pallas_call(
        final_kernel,
        out_shape=shape((8, TGT), F32),
        in_specs=[VMEM] * 3,
        out_specs=VMEM,
        compiler_params=params,
        name="final",
    )(arrived, mass, g)
    return fine_f, fine_g


def solution(mesh):
    placed = (
        P(None, "src", None),
        P("src", None),
        P(None, None, "tgt"),
        P(None, "tgt"),
        P("src", "tgt", None),
        P("src", "tgt"),
    )
    return jax.shard_map(
        on_device,
        mesh=mesh,
        in_specs=placed,
        out_specs=(P("src", None), P("src", "tgt")),
        check_vma=False,
    )
```

profile of v0, /device:TPU:1, one launch (start us, length us, event | category | flops | bytes accessed | tf_op | source)
XLA Modules:
  0.0 57.3 jit_solution(10921307016846961854)
XLA Ops:
  0.6 0.0 copy-start.1
  0.6 0.0 copy-start
  0.6 2.2 %centroids.1 = (f32[128,128]{1,0:T(8,128)}, f32[8,256]{1,0:T(8,128)}, f32[8,256]{1,0:T(8,128)}) custom-call(f32[3,16,256]{2,1,0:T(8,128)} %sp.5, f32[16,256]{1,0:T(8,128)} %sm.3, f32[3,256,256]{2,1,0:T(8,128)} %tp.5, f32[256,256]{1,0:T(8,128)} %tm.5), custom_call_target="tpu_custom_call" | custom-call | tf_op jit(solution)/shard_map/centroids/pallas_call | solution.py:266
  2.9 0.0 copy-start.2
  2.9 0.0 copy-start.6
  2.9 11.5 %all-to-all-start = ((f32[128,1,128]{2,1,0:T(1,128)}), f32[128,1,128]{2,1,0:T(1,128)S(1)}, u32[]{:S(2)}, u32[]{:S(2)}) async-start(f32[128,1,128]{2,1,0:T(1,128)} %bitcast.11), calls=%async_computation | async-start | bytes 131072 | tf_op jit(solution)/shard_map/all_to_all | solution.py:273
  14.4 0.0 copy-start.7
  14.4 0.0 copy-done.1
  14.4 0.0 copy-done
  14.4 0.0 copy-done.2
  14.4 0.0 copy-done.6
  14.4 0.6 %copy-done.7 = s32[16,1]{0,1:T(1,128)S(1)} copy-done((s32[16,1]{0,1:T(1,128)S(1)}, s32[16,1]{0,1:T(1,128)}, u32[]{:S(2)}) %copy-start.7) | copy-done | bytes 88
  15.1 0.0 copy-start.5
  15.1 7.5 %rows.1 = (f32[128,256]{1,0:T(8,128)S(1)}, f32[128,128]{1,0:T(8,128)S(1)}, s32[160]{0:T(256)S(1)}) custom-call(s32[8,16]{1,0:T(8,128)S(1)} %bitcast.9, s32[1,16]{1,0:T(1,128)S(1)} %bitcast.10, f32[3,16,256]{2,1,0:T(8,128)S(1)} %copy-done.2, f32[3,256,256]{2,1,0:T(8,128)S(1)} %copy-done, f32[256,256]{1,0:T(8,128)S(1)} %copy-done.1), custom_call_target="tpu_custom_call" | custom-call | flops 100000000 | bytes 10000000 | tf_op jit(solution)/shard_map/rows/pallas_call | solution.py:276
  22.5 1.7 %all-to-all-done = f32[128,1,128]{2,1,0:T(1,128)S(1)} async-done(((f32[128,1,128]{2,1,0:T(1,128)}), f32[128,1,128]{2,1,0:T(1,128)S(1)}, u32[]{:S(2)}, u32[]{:S(2)}) %all-to-all-start) | async-done | bytes 65568 | tf_op jit(solution)/shard_map/all_to_all | solution.py:273
  24.3 0.0 copy-done.5
  24.3 0.0 copy-start.3
  24.3 2.5 %coarse.1 = (f32[8,256]{1,0:T(8,128)S(1)}, f32[16,256]{1,0:T(8,128)S(1)}) custom-call(f32[128,128]{1,0:T(8,128)S(1)} %bitcast.8, f32[8,256]{1,0:T(8,128)S(1)} %copy-done.5, f32[128,256]{1,0:T(8,128)S(1)} %get-tuple-element.15.r_in, f32[128,128]{1,0:T(8,128)S(1)} %get-tuple-element.16.l_in), custom_call_target="tpu_custom_call" | custom-call | tf_op jit(solution)/shard_map/coarse/pallas_call | solution.py:293
  26.8 1.3 %collective-permute-start.2 = (f32[16,256]{1,0:T(8,128)S(1)}, f32[16,256]{1,0:T(8,128)S(1)}, u32[]{:S(2)}, u32[]{:S(2)}) collective-permute-start(f32[16,256]{1,0:T(8,128)S(1)} %get-tuple-element.18.l0), channel_id=1, source_target_pairs={{0,3},{1,0},{2,1},{3,2},{4,7},{5,4},{6,5},{7,6},{8,11},{9,8},{10,9... | collective-permute-start | bytes 49160 | tf_op jit(solution)/shard_map/ppermute | solution.py:303
  28.1 1.0 %collective-permute-start.1 = (f32[16,256]{1,0:T(8,128)S(1)}, f32[16,256]{1,0:T(8,128)S(1)}, u32[]{:S(2)}, u32[]{:S(2)}) collective-permute-start(f32[16,256]{1,0:T(8,128)S(1)} %get-tuple-element.18.l0), channel_id=1, source_target_pairs={{0,2},{1,3},{2,0},{3,1},{4,6},{5,7},{6,4},{7,5},{8,10},{9,11},{10,... | collective-permute-start | bytes 49160 | tf_op jit(solution)/shard_map/ppermute | solution.py:303
  29.0 0.0 collective-permute-start
  29.0 0.4 collective-permute-done.2.l3
  29.5 2.7 %collective-permute-done.1.l2 = f32[16,256]{1,0:T(8,128)S(1)} collective-permute-done((f32[16,256]{1,0:T(8,128)S(1)}, f32[16,256]{1,0:T(8,128)S(1)}, u32[]{:S(2)}, u32[]{:S(2)}) %collective-permute-start.1) | collective-permute-done | bytes 16416 | tf_op jit(solution)/shard_map/ppermute | solution.py:303
  32.2 1.0 %collective-permute-done.l1 = f32[16,256]{1,0:T(8,128)S(1)} collective-permute-done((f32[16,256]{1,0:T(8,128)S(1)}, f32[16,256]{1,0:T(8,128)S(1)}, u32[]{:S(2)}, u32[]{:S(2)}) %collective-permute-start) | collective-permute-done | bytes 16416 | tf_op jit(solution)/shard_map/ppermute | solution.py:303
  33.1 0.0 copy-done.3
  33.1 6.3 %columns.1 = (f32[16,256]{1,0:T(8,128)}, f32[32,8,256]{2,1,0:T(8,128)S(1)}) custom-call(s32[160]{0:T(256)S(1)} %get-tuple-element.12.order, f32[3,16,256]{2,1,0:T(8,128)S(1)} %copy-done.2, f32[16,256]{1,0:T(8,128)S(1)} %copy-done.3, f32[3,256,256]{2,1,0:T(8,128)S(1)} %copy-done, f32[256,256]{1,0:T(8,128)S(1)} %copy-done.1, ...), custom_call_target="tpu_custom_call" | custom-call | tf_op jit(solution)/shard_map/columns/pallas_call | solution.py:305
  39.4 0.0 copy-start.4
  39.4 17.2 %all_to_all.16.arrived = f32[32,8,256]{2,1,0:T(8,128)S(1)} all-to-all(f32[32,8,256]{2,1,0:T(8,128)S(1)} %get-tuple-element.20), channel_id=1, replica_groups=mesh['src'=32,'tgt'=4] {'src'}, dimensions={0} | all-to-all | bytes 524288 | tf_op jit(solution)/shard_map/all_to_all | solution.py:319
  56.7 0.0 copy-done.4
  56.7 0.6 %final.1 = f32[8,256]{1,0:T(8,128)} custom-call(f32[32,8,256]{2,1,0:T(8,128)S(1)} %all_to_all.16.arrived, f32[8,256]{1,0:T(8,128)S(1)} %copy-done.4, f32[8,256]{1,0:T(8,128)S(1)} %get-tuple-element.17.g), custom_call_target="tpu_custom_call" | custom-call | tf_op jit(solution)/shard_map/final/pallas_call | solution.py:320
Async XLA Ops:
  0.6 13.8 %copy-start.1 = (f32[256,256]{1,0:T(8,128)S(1)}, f32[256,256]{1,0:T(8,128)}, u32[]{:S(2)}) copy-start(f32[256,256]{1,0:T(8,128)} %tm.5) | copy-start | bytes 786436
  0.6 13.8 %copy-start = (f32[3,256,256]{2,1,0:T(8,128)S(1)}, f32[3,256,256]{2,1,0:T(8,128)}, u32[]{:S(2)}) copy-start(f32[3,256,256]{2,1,0:T(8,128)} %tp.5) | copy-start | bytes 2359300
  2.9 11.5 %copy-start.2 = (f32[3,16,256]{2,1,0:T(8,128)S(1)}, f32[3,16,256]{2,1,0:T(8,128)}, u32[]{:S(2)}) copy-start(f32[3,16,256]{2,1,0:T(8,128)} %sp.5) | copy-start | bytes 147460
  2.9 11.5 %copy-start.6 = (s32[16,1,8]{0,2,1:T(8,128)S(1)}, s32[16,1,8]{0,2,1:T(8,128)}, u32[]{:S(2)}) copy-start(s32[16,1,8]{0,2,1:T(8,128)} %param.10) | copy-start | bytes 1540
  2.9 21.4 %all-to-all-start = ((f32[128,1,128]{2,1,0:T(1,128)}), f32[128,1,128]{2,1,0:T(1,128)S(1)}, u32[]{:S(2)}, u32[]{:S(2)}) async-start(f32[128,1,128]{2,1,0:T(1,128)} %bitcast.11), calls=%async_computation | async-start | bytes 131072 | tf_op jit(solution)/shard_map/all_to_all | solution.py:273
  14.4 0.7 %copy-start.7 = (s32[16,1]{0,1:T(1,128)S(1)}, s32[16,1]{0,1:T(1,128)}, u32[]{:S(2)}) copy-start(s32[16,1]{0,1:T(1,128)} %param.11) | copy-start | bytes 196
  15.1 9.2 %copy-start.5 = (f32[8,256]{1,0:T(8,128)S(1)}, f32[8,256]{1,0:T(8,128)}, u32[]{:S(2)}) copy-start(f32[8,256]{1,0:T(8,128)} %get-tuple-element.14.own) | copy-start | bytes 24580
  24.3 8.8 %copy-start.3 = (f32[16,256]{1,0:T(8,128)S(1)}, f32[16,256]{1,0:T(8,128)}, u32[]{:S(2)}) copy-start(f32[16,256]{1,0:T(8,128)} %sm.3) | copy-start | bytes 49156
  26.8 2.7 %collective-permute-start.2 = (f32[16,256]{1,0:T(8,128)S(1)}, f32[16,256]{1,0:T(8,128)S(1)}, u32[]{:S(2)}, u32[]{:S(2)}) collective-permute-start(f32[16,256]{1,0:T(8,128)S(1)} %get-tuple-element.18.l0), channel_id=1, source_target_pairs={{0,3},{1,0},{2,1},{3,2},{4,7},{5,4},{6,5},{7,6},{8,11},{9,8},{10,9... | collective-permute-start | bytes 49160 | tf_op jit(solution)/shard_map/ppermute | solution.py:303
  28.1 4.1 %collective-permute-start.1 = (f32[16,256]{1,0:T(8,128)S(1)}, f32[16,256]{1,0:T(8,128)S(1)}, u32[]{:S(2)}, u32[]{:S(2)}) collective-permute-start(f32[16,256]{1,0:T(8,128)S(1)} %get-tuple-element.18.l0), channel_id=1, source_target_pairs={{0,2},{1,3},{2,0},{3,1},{4,6},{5,7},{6,4},{7,5},{8,10},{9,11},{10,... | collective-permute-start | bytes 49160 | tf_op jit(solution)/shard_map/ppermute | solution.py:303
  29.0 4.1 %collective-permute-start = (f32[16,256]{1,0:T(8,128)S(1)}, f32[16,256]{1,0:T(8,128)S(1)}, u32[]{:S(2)}, u32[]{:S(2)}) collective-permute-start(f32[16,256]{1,0:T(8,128)S(1)} %get-tuple-element.18.l0), channel_id=1, source_target_pairs={{0,1},{1,2},{2,3},{3,0},{4,5},{5,6},{6,7},{7,4},{8,9},{9,10},{10,1... | collective-permute-start | bytes 49160 | tf_op jit(solution)/shard_map/ppermute | solution.py:303
  39.4 17.2 %copy-start.4 = (f32[8,256]{1,0:T(8,128)S(1)}, f32[8,256]{1,0:T(8,128)}, u32[]{:S(2)}) copy-start(f32[8,256]{1,0:T(8,128)} %get-tuple-element.21.mass) | copy-start | bytes 24580
where the time goes:
time: 57.5 us; the launch traced here: 57.3 us
  Pallas kernels  19.2 us (33%)
  blocking collectives  17.2 us (30%)
  starting transfers between devices  13.7 us (24%)
  waiting for transfers between devices  5.84 us (10%)
  between operations  0.72 us (1%)
  local copies, waits for them, and re-layouts  0.64 us (1%)
    all_to_all x1, blocking collectives, on_device(): lax.all_to_all(sums, 'src', split_axis=0, concat_axis=0, tiled=True)  17.2 us
    all_to_all x1, starting transfers between devices, on_device(): lax.all_to_all(row, ('src', 'tgt'), split_axis=0, concat_axis=0, tiled=True)  11.5 us
    pallas_call x1, Pallas kernels, on_device(): pl.pallas_call(row_kernel, out_shape=(shape((BLOCKS, PTS), F32), shape((1...  7.48 us
    pallas_call x1, Pallas kernels, on_device(): pl.pallas_call(column_kernel, out_shape=(shape((CL, PTS), F32), shape((32...  6.3 us
    ppermute x3, waiting for transfers between devices, on_device(): lax.ppermute(part, 'tgt', [(i, (i + k) % 4) for i in range(4)])  4.09 us
    pallas_call x1, Pallas kernels, on_device(): pl.pallas_call(coarse_kernel, out_shape=(shape((8, 256), F32), shape((CL,...  2.51 us
    pallas_call x1, Pallas kernels, on_device(): pl.pallas_call(centroid_kernel, out_shape=(shape((128, 128), F32), shape(...  2.25 us
    ppermute x3, starting transfers between devices, on_device(): lax.ppermute(part, 'tgt', [(i, (i + k) % 4) for i in range(4)])  2.23 us
  transfers between devices with their start and end apart: 4, of which 4 were waited for; matrix products, arithmetic and copies ran while one was open for 0% of the time, Pallas kernels for 13%

commit v1 on v0

--- a/solution.py
+++ b/solution.py
@@ -22,6 +22,7 @@
 LIMIT = 16 << 20
 VMEM = pl.BlockSpec(memory_space=pltpu.VMEM)
 SMEM = pl.BlockSpec(memory_space=pltpu.SMEM)
+ANY = pl.BlockSpec(memory_space=pl.ANY)
 
 
 def iota(shape, dim):
@@ -40,8 +41,20 @@
     return high, mid, rest - mid
 
 
-def centroid_kernel(sp, sm, tp, tm, row_out, own_out, slice_out):
+def fill_order(order, listed, live):
+    n = 0
+    for c in range(CL):
+        for k in range(SLOTS):
+            order[n + k] = (k * CL + c) * TGT + listed[k, c]
+        n = n + live[0, c]
+    for u in range(PAD):
+        order[n + u] = order[0]
+    order[LIST - 1] = n
+
+
+def centroid_kernel(listed, live, sp, sm, tp, tm, row_out, own_out, slice_out, order):
     s, t = lax.axis_index("src"), lax.axis_index("tgt")
+    fill_order(order, listed, live)
     mass = sm[...]
     total = jnp.sum(mass, axis=1, keepdims=True)
     inv = 1.0 / total
@@ -80,33 +93,23 @@
     return jnp.log2(tm[...]) - (0.5 * ALPHA) * (tp[0] * tp[0] + tp[1] * tp[1] + tp[2] * tp[2])
 
 
-def fill_order(order, listed, live):
-    n = 0
-    for c in range(CL):
-        for k in range(SLOTS):
-            order[n + k] = (k * CL + c) * TGT + listed[k, c]
-        n = n + live[0, c]
-    for u in range(PAD):
-        order[n + u] = order[0]
-    order[LIST - 1] = n
-    return n
-
-
-def target_tables(tab, tp, base):
+def fill_tables(tab, tp, tm):
     for d in range(3):
-        a, b, _ = split3(tp[d].T)
-        tab[2 * d] = a
-        tab[2 * d + 1] = b
-    for r, piece in enumerate(split3(base)):
-        tab[6 + r] = piece
-
-
-def target_factors(tab, at):
+        y = tp[d].T
+        high = bf16_part(y)
+        tab[2 * d] = high
+        tab[2 * d + 1] = bf16_part(y - high)
+    tab[6] = own_terms(tp, tm).T
+
+
+def target_factors(tab, at, extra):
     sub = iota((16, PTS), 0)
     stack = jnp.ones((16, PTS), F32)
-    for r, q in enumerate((0, 0, 1, 2, 2, 3, 4, 4, 5, 6, 7, 8)):
-        stack = jnp.where(sub == r, tab[q, pl.ds(at, 1), :], stack)
-    return stack
+    rows = [tab[q, pl.ds(at, 1), :] for q in (0, 0, 1, 2, 2, 3, 4, 4, 5)]
+    own = tab[6, pl.ds(at, 1), :]
+    for r, row in enumerate((*rows, *split3(own if extra is None else own + extra))):
+        stack = jnp.where(sub == r, row, stack)
+    return stack.astype(BF16)
 
 
 def source_factors(table, x, own):
@@ -120,18 +123,19 @@
         dup(table, 12 + r, piece)
 
 
-def row_kernel(listed, live, sp, tp, tm, r_out, l_out, order, gt, gf, tab, scol, lrow, *sets):
+def row_kernel(order, sp, tp, tm, r_out, l_out, tab, gt, gf, scol, lrow, *sets):
     sets = [sets[3 * u : 3 * u + 3] for u in range(AHEAD)]
-    n = fill_order(order, listed, live)
+    n = order[LIST - 1]
     zero = jnp.zeros((CL, PTS), F32)
     source_factors(gf, [sp[d] * ALPHA for d in range(3)], [zero] * 4)
     for c in range(CL):
         gt[c] = jnp.concatenate([gf[h, 16 * c : 16 * c + 16, :] for h in range(2)], axis=1).astype(BF16)
-    target_tables(tab, tp, own_terms(tp, tm).T)
+    fill_tables(tab, tp, tm)
+    lrow[...] = jnp.full((BLOCKS, 128), -1.0, F32)
 
     def prepare(i, lhs):
         at = order[i] & (TGT - 1)
-        lhs[...] = target_factors(tab, at).astype(BF16).T
+        lhs[...] = target_factors(tab, at, None).T
         lrow[pl.ds(order[i] >> 8, 1), :] = jnp.broadcast_to(at.astype(F32), (1, 128))
 
     for u in range(AHEAD):
@@ -159,15 +163,10 @@
 
     lax.fori_loop(0, (n + AHEAD - 1) // AHEAD + 1, batch, 0)
     xn = (-0.5 * ALPHA) * (sp[0] * sp[0] + sp[1] * sp[1] + sp[2] * sp[2])
-    lane = iota((1, 128), 1)
-    have = jnp.zeros((1, 128), I32)
-    for c in range(CL):
-        have = jnp.where((lane & (CL - 1)) == c, live[0, c], have)
-    ok = jnp.broadcast_to(jnp.where((lane >> 4) < have, 1.0, 0.0), (128, 128)).T[:, 0:1] > 0.5
     r = r_out[...] + jnp.log2(scol[...])
     r = (r.reshape(SLOTS, CL, PTS) + xn[None]).reshape(BLOCKS, PTS)
-    r_out[...] = jnp.where(ok, r, NEG)
-    l_out[...] = jnp.where(ok, lrow[...], -1.0)
+    r_out[...] = jnp.where(lrow[:, 0:1] >= 0.0, r, NEG)
+    l_out[...] = lrow[...]
 
 
 def coarse_kernel(got, own, r_in, l_in, g_out, l_out, terms, scores):
@@ -218,18 +217,20 @@
     l_out[...] = top + jnp.log2(jnp.sum(jnp.exp2(r - top[None]), axis=0))
 
 
-def column_kernel(order, sp, sm, tp, tm, g, l0, l1, l2, l3, f_out, s_out, gt, gf, tab, st):
+def column_kernel(order, g, sp, sm, tp, tm, l0, l1, l2, l3, f_out, s_out, tab, gt, gf, st, fbuf, sem):
     parts = [p[...] for p in (l0, l1, l2, l3)]
     top = functools.reduce(jnp.maximum, parts)
     f = -(top + jnp.log2(sum(jnp.exp2(p - top) for p in parts)))
-    f_out[...] = f * UNSCALE
+    fbuf[...] = f * UNSCALE
+    send = pltpu.make_async_copy(fbuf, f_out, sem)
+    send.start()
     st[...] = jnp.zeros_like(st)
+    fill_tables(tab, tp, tm)
     own = f + jnp.log2(sm[...]) - (0.5 * ALPHA) * (sp[0] * sp[0] + sp[1] * sp[1] + sp[2] * sp[2])
     zero = jnp.zeros((CL, PTS), F32)
     source_factors(gf, [sp[d] * ALPHA for d in range(3)], (*split3(own), zero))
     for c in range(CL):
         gt[c] = jnp.concatenate([gf[h, 16 * c : 16 * c + 16, :] for h in range(2)], axis=1).astype(BF16).T
-    target_tables(tab, tp, (own_terms(tp, tm) + g[0:1, :]).T)
     n = order[LIST - 1]
 
     def batch(i, _):
@@ -237,7 +238,8 @@
         v = []
         for u in range(UNROLL):
             left = gt[(order[at + u] >> 8) & (CL - 1)]
-            right = target_factors(tab, order[at + u] & (TGT - 1)).astype(BF16)
+            to = order[at + u] & (TGT - 1)
+            right = target_factors(tab, to, g[0, to])
             v.append(jnp.dot(left, right, preferred_element_type=F32))
         lines = []
         for u in range(UNROLL):
@@ -253,6 +255,7 @@
 
     lax.fori_loop(0, (n + UNROLL - 1) // UNROLL, batch, 0)
     s_out[...] = st[...].T.reshape(32, 8, TGT)
+    send.wait()
 
 
 def final_kernel(arrived, mass, g, out):
@@ -263,25 +266,25 @@
 def on_device(src_pts, src_mass, tgt_pts, tgt_mass, listed, live):
     shape = jax.ShapeDtypeStruct
     params = pltpu.CompilerParams(vmem_limit_bytes=LIMIT)
-    row, own, mass = pl.pallas_call(
-        centroid_kernel,
-        out_shape=(shape((128, 128), F32), shape((8, 256), F32), shape((8, 256), F32)),
-        in_specs=[VMEM] * 4,
-        out_specs=(VMEM, VMEM, VMEM),
-        name="centroids",
-    )(src_pts, src_mass, tgt_pts, tgt_mass)
-    got = lax.all_to_all(row, ("src", "tgt"), split_axis=0, concat_axis=0, tiled=True)
     slots = listed.transpose(1, 2, 0).reshape(SLOTS, CL)
     counts = live.transpose(1, 0)
-    r, where, order = pl.pallas_call(
+    row, own, mass, order = pl.pallas_call(
+        centroid_kernel,
+        out_shape=(shape((128, 128), F32), shape((8, 256), F32), shape((8, 256), F32), shape((LIST,), I32)),
+        in_specs=[SMEM, SMEM] + [VMEM] * 4,
+        out_specs=(VMEM, VMEM, VMEM, SMEM),
+        name="centroids",
+    )(slots, counts, src_pts, src_mass, tgt_pts, tgt_mass)
+    got = lax.all_to_all(row, ("src", "tgt"), split_axis=0, concat_axis=0, tiled=True)
+    r, where = pl.pallas_call(
         row_kernel,
-        out_shape=(shape((BLOCKS, PTS), F32), shape((128, 128), F32), shape((LIST,), I32)),
-        in_specs=[SMEM, SMEM, VMEM, VMEM, VMEM],
-        out_specs=(VMEM, VMEM, SMEM),
+        out_shape=(shape((BLOCKS, PTS), F32), shape((128, 128), F32)),
+        in_specs=[SMEM, VMEM, VMEM, VMEM],
+        out_specs=(VMEM, VMEM),
         scratch_shapes=[
+            pltpu.VMEM((7, TGT, PTS), F32),
             pltpu.VMEM((CL, 16, PTS), BF16),
             pltpu.VMEM((2, CL * 16, 128), F32),
-            pltpu.VMEM((9, TGT, PTS), F32),
             pltpu.VMEM((BLOCKS, PTS), F32),
             pltpu.VMEM((BLOCKS, 128), F32),
         ]
@@ -289,7 +292,7 @@
         cost_estimate=pl.CostEstimate(flops=100_000_000, bytes_accessed=10_000_000, transcendentals=5_000_000),
         compiler_params=params,
         name="rows",
-    )(slots, counts, src_pts, tgt_pts, tgt_mass)
+    )(order, src_pts, tgt_pts, tgt_mass)
     g, part = pl.pallas_call(
         coarse_kernel,
         out_shape=(shape((8, 256), F32), shape((CL, PTS), F32)),
@@ -305,17 +308,19 @@
     fine_f, sums = pl.pallas_call(
         column_kernel,
         out_shape=(shape((CL, PTS), F32), shape((32, 8, TGT), F32)),
-        in_specs=[SMEM] + [VMEM] * 9,
-        out_specs=(VMEM, VMEM),
+        in_specs=[SMEM, SMEM] + [VMEM] * 8,
+        out_specs=(ANY, VMEM),
         scratch_shapes=[
+            pltpu.VMEM((7, TGT, PTS), F32),
             pltpu.VMEM((CL, PTS, 16), BF16),
             pltpu.VMEM((2, CL * 16, 128), F32),
-            pltpu.VMEM((9, TGT, PTS), F32),
             pltpu.VMEM((TGT, PTS), F32),
+            pltpu.VMEM((CL, PTS), F32),
+            pltpu.SemaphoreType.DMA,
         ],
         compiler_params=params,
         name="columns",
-    )(order, src_pts, src_mass, tgt_pts, tgt_mass, g, *parts)
+    )(order, g, src_pts, src_mass, tgt_pts, tgt_mass, *parts)
     arrived = lax.all_to_all(sums, "src", split_axis=0, concat_axis=0, tiled=True)
     fine_g = pl.pallas_call(
         final_kernel,

time: 57.5 us -> 56.6 us (0.984)
  Pallas kernels: 19.2 us -> 15.7 us
  waiting for transfers between devices: 5.84 us -> 7.83 us
  blocking collectives: 17.2 us -> 17.9 us
    all_to_all x1, waiting for transfers between devices: 1.75 us -> 3.74 us  [on_device(): lax.all_to_all(row, ('src', 'tgt'), split_axis=0, concat_axis=0, tiled=True)]
    pallas_call x1, Pallas kernels: 7.48 us -> 5.5 us  [on_device(): pl.pallas_call(row_kernel, out_shape=(shape((BLOCKS, PTS), F32), shape((1...]
    pallas_call x1, Pallas kernels: 6.3 us -> 4.74 us  [on_device(): pl.pallas_call(column_kernel, out_shape=(shape((CL, PTS), F32), shape((32...]
    all_to_all x1, blocking collectives: 17.2 us -> 17.9 us  [on_device(): lax.all_to_all(sums, 'src', split_axis=0, concat_axis=0, tiled=True)]
  transfers between devices with their start and end apart: 4 -> 4, of which waited for: 4 -> 4; matrix products, arithmetic and copies ran while one was open for 0% -> 0% of each run, Pallas kernels for 13% -> 10%
where the time goes in v1:
time: 56.6 us; the launch traced here: 56.4 us
  blocking collectives  17.9 us (32%)
  Pallas kernels  15.7 us (28%)
  starting transfers between devices  13.7 us (24%)
  waiting for transfers between devices  7.83 us (14%)
  between operations  0.74 us (1%)
  local copies, waits for them, and re-layouts  0.67 us (1%)
    all_to_all x1, blocking collectives, on_device(): lax.all_to_all(sums, 'src', split_axis=0, concat_axis=0, tiled=True)  17.9 us
    all_to_all x1, starting transfers between devices, on_device(): lax.all_to_all(row, ('src', 'tgt'), split_axis=0, concat_axis=0, tiled=True)  11.5 us
    pallas_call x1, Pallas kernels, on_device(): pl.pallas_call(row_kernel, out_shape=(shape((BLOCKS, PTS), F32), shape((1...  5.5 us
    pallas_call x1, Pallas kernels, on_device(): pl.pallas_call(column_kernel, out_shape=(shape((CL, PTS), F32), shape((32...  4.74 us
    ppermute x3, waiting for transfers between devices, on_device(): lax.ppermute(part, 'tgt', [(i, (i + k) % 4) for i in range(4)])  4.09 us
    all_to_all x1, waiting for transfers between devices, on_device(): lax.all_to_all(row, ('src', 'tgt'), split_axis=0, concat_axis=0, tiled=True)  3.74 us
    pallas_call x1, Pallas kernels, on_device(): pl.pallas_call(coarse_kernel, out_shape=(shape((8, 256), F32), shape((CL,...  2.51 us
    pallas_call x1, Pallas kernels, on_device(): pl.pallas_call(centroid_kernel, out_shape=(shape((128, 128), F32), shape(...  2.26 us
  transfers between devices with their start and end apart: 4, of which 4 were waited for; matrix products, arithmetic and copies ran while one was open for 0% of the time, Pallas kernels for 10%

profile of v1, /device:TPU:1, one launch (start us, length us, event | category | flops | bytes accessed | tf_op | source)
XLA Modules:
  0.0 56.4 jit_solution(4921576672481187037)
XLA Ops:
  0.6 0.0 copy-start
  0.6 0.0 copy-start.1
  0.7 2.3 %centroids.1 = (f32[128,128]{1,0:T(8,128)}, f32[8,256]{1,0:T(8,128)}, f32[8,256]{1,0:T(8,128)}, s32[160]{0:T(256)}) custom-call(s32[8,16]{1,0:T(8,128)} %bitcast.10, s32[1,16]{1,0:T(1,128)} %bitcast.11, f32[3,16,256]{2,1,0:T(8,128)} %sp.5, f32[16,256]{1,0:T(8,128)} %sm.3, f32[3,256,256]{2,1,0:T(8,128)} %tp.5, f32[256,256]{1,0:T(8,128)} %tm.5), custom_call_target="tpu_custom_call" | custom-call | tf_op jit(solution)/shard_map/centroids/pallas_call | solution.py:271
  2.9 0.0 copy-start.2
  2.9 11.5 %all-to-all-start = ((f32[128,1,128]{2,1,0:T(1,128)}), f32[128,1,128]{2,1,0:T(1,128)S(1)}, u32[]{:S(2)}, u32[]{:S(2)}) async-start(f32[128,1,128]{2,1,0:T(1,128)} %bitcast.9), calls=%async_computation | async-start | bytes 131072 | tf_op jit(solution)/shard_map/all_to_all | solution.py:278
  14.4 0.0 copy-start.6
  14.4 0.0 copy-done
  14.5 0.0 copy-done.1
  14.5 0.0 copy-done.2
  14.5 0.6 %copy-done.6 = s32[160]{0:T(256)S(1)} copy-done((s32[160]{0:T(256)S(1)}, s32[160]{0:T(256)}, u32[]{:S(2)}) %copy-start.6) | copy-done | bytes 664
  15.1 0.0 copy-start.5
  15.1 5.5 %rows.1 = (f32[128,256]{1,0:T(8,128)S(1)}, f32[128,128]{1,0:T(8,128)S(1)}) custom-call(s32[160]{0:T(256)S(1)} %copy-done.6, f32[3,16,256]{2,1,0:T(8,128)S(1)} %copy-done.2, f32[3,256,256]{2,1,0:T(8,128)S(1)} %copy-done, f32[256,256]{1,0:T(8,128)S(1)} %copy-done.1), custom_call_target="tpu_custom_call" | custom-call | flops 100000000 | bytes 10000000 | tf_op jit(solution)/shard_map/rows/pallas_call | solution.py:279
  20.6 3.7 %all-to-all-done = f32[128,1,128]{2,1,0:T(1,128)S(1)} async-done(((f32[128,1,128]{2,1,0:T(1,128)}), f32[128,1,128]{2,1,0:T(1,128)S(1)}, u32[]{:S(2)}, u32[]{:S(2)}) %all-to-all-start) | async-done | bytes 65568 | tf_op jit(solution)/shard_map/all_to_all | solution.py:278
  24.4 0.0 copy-done.5
  24.4 0.0 copy-start.3
  24.4 2.5 %coarse.1 = (f32[8,256]{1,0:T(8,128)S(1)}, f32[16,256]{1,0:T(8,128)S(1)}) custom-call(f32[128,128]{1,0:T(8,128)S(1)} %bitcast.8, f32[8,256]{1,0:T(8,128)S(1)} %copy-done.5, f32[128,256]{1,0:T(8,128)S(1)} %get-tuple-element.15.r_in, f32[128,128]{1,0:T(8,128)S(1)} %get-tuple-element.16.l_in), custom_call_target="tpu_custom_call" | custom-call | tf_op jit(solution)/shard_map/coarse/pallas_call | solution.py:296
  26.9 0.9 %collective-permute-start.2 = (f32[16,256]{1,0:T(8,128)S(1)}, f32[16,256]{1,0:T(8,128)S(1)}, u32[]{:S(2)}, u32[]{:S(2)}) collective-permute-start(f32[16,256]{1,0:T(8,128)S(1)} %get-tuple-element.18.l0), channel_id=1, source_target_pairs={{0,3},{1,0},{2,1},{3,2},{4,7},{5,4},{6,5},{7,6},{8,11},{9,8},{10,9... | collective-permute-start | bytes 49160 | tf_op jit(solution)/shard_map/ppermute | solution.py:306
  27.7 1.3 %collective-permute-start.1 = (f32[16,256]{1,0:T(8,128)S(1)}, f32[16,256]{1,0:T(8,128)S(1)}, u32[]{:S(2)}, u32[]{:S(2)}) collective-permute-start(f32[16,256]{1,0:T(8,128)S(1)} %get-tuple-element.18.l0), channel_id=1, source_target_pairs={{0,2},{1,3},{2,0},{3,1},{4,6},{5,7},{6,4},{7,5},{8,10},{9,11},{10,... | collective-permute-start | bytes 49160 | tf_op jit(solution)/shard_map/ppermute | solution.py:306
  29.0 0.0 collective-permute-start
  29.1 0.5 collective-permute-done.2.l3
  29.5 2.3 %collective-permute-done.1.l2 = f32[16,256]{1,0:T(8,128)S(1)} collective-permute-done((f32[16,256]{1,0:T(8,128)S(1)}, f32[16,256]{1,0:T(8,128)S(1)}, u32[]{:S(2)}, u32[]{:S(2)}) %collective-permute-start.1) | collective-permute-done | bytes 16416 | tf_op jit(solution)/shard_map/ppermute | solution.py:306
  31.8 1.3 %collective-permute-done.l1 = f32[16,256]{1,0:T(8,128)S(1)} collective-permute-done((f32[16,256]{1,0:T(8,128)S(1)}, f32[16,256]{1,0:T(8,128)S(1)}, u32[]{:S(2)}, u32[]{:S(2)}) %collective-permute-start) | collective-permute-done | bytes 16416 | tf_op jit(solution)/shard_map/ppermute | solution.py:306
  33.1 0.0 copy-done.3
  33.1 4.7 %columns.1 = (f32[16,256]{1,0:T(8,128)}, f32[32,8,256]{2,1,0:T(8,128)S(1)}) custom-call(s32[160]{0:T(256)S(1)} %copy-done.6, f32[8,256]{1,0:T(8,128)S(1)} %get-tuple-element.17.g, f32[3,16,256]{2,1,0:T(8,128)S(1)} %copy-done.2, f32[16,256]{1,0:T(8,128)S(1)} %copy-done.3, f32[3,256,256]{2,1,0:T(8,128)S(1)} %copy-done, f32[256,256]{1,0:T(8,128)S(1)} %copy-done.1, ...), custom_call_target="tpu_custom_call" | custom-call | tf_op jit(solution)/shard_map/columns/pallas_call | solution.py:308
  37.9 0.0 copy-start.4
  37.9 17.9 %all_to_all.16.arrived = f32[32,8,256]{2,1,0:T(8,128)S(1)} all-to-all(f32[32,8,256]{2,1,0:T(8,128)S(1)} %get-tuple-element.20), channel_id=1, replica_groups=mesh['src'=32,'tgt'=4] {'src'}, dimensions={0} | all-to-all | bytes 524288 | tf_op jit(solution)/shard_map/all_to_all | solution.py:324
  55.8 0.0 copy-done.4
  55.8 0.6 %final.1 = f32[8,256]{1,0:T(8,128)} custom-call(f32[32,8,256]{2,1,0:T(8,128)S(1)} %all_to_all.16.arrived, f32[8,256]{1,0:T(8,128)S(1)} %copy-done.4, f32[8,256]{1,0:T(8,128)S(1)} %get-tuple-element.17.g), custom_call_target="tpu_custom_call" | custom-call | tf_op jit(solution)/shard_map/final/pallas_call | solution.py:325
Async XLA Ops:
  0.6 13.8 %copy-start = (f32[3,256,256]{2,1,0:T(8,128)S(1)}, f32[3,256,256]{2,1,0:T(8,128)}, u32[]{:S(2)}) copy-start(f32[3,256,256]{2,1,0:T(8,128)} %tp.5) | copy-start | bytes 2359300
  0.6 13.8 %copy-start.1 = (f32[256,256]{1,0:T(8,128)S(1)}, f32[256,256]{1,0:T(8,128)}, u32[]{:S(2)}) copy-start(f32[256,256]{1,0:T(8,128)} %tm.5) | copy-start | bytes 786436
  2.9 11.5 %copy-start.2 = (f32[3,16,256]{2,1,0:T(8,128)S(1)}, f32[3,16,256]{2,1,0:T(8,128)}, u32[]{:S(2)}) copy-start(f32[3,16,256]{2,1,0:T(8,128)} %sp.5) | copy-start | bytes 147460
  2.9 21.4 %all-to-all-start = ((f32[128,1,128]{2,1,0:T(1,128)}), f32[128,1,128]{2,1,0:T(1,128)S(1)}, u32[]{:S(2)}, u32[]{:S(2)}) async-start(f32[128,1,128]{2,1,0:T(1,128)} %bitcast.9), calls=%async_computation | async-start | bytes 131072 | tf_op jit(solution)/shard_map/all_to_all | solution.py:278
  14.4 0.7 %copy-start.6 = (s32[160]{0:T(256)S(1)}, s32[160]{0:T(256)}, u32[]{:S(2)}) copy-start(s32[160]{0:T(256)} %get-tuple-element.12.order) | copy-start | bytes 1924
  15.1 9.2 %copy-start.5 = (f32[8,256]{1,0:T(8,128)S(1)}, f32[8,256]{1,0:T(8,128)}, u32[]{:S(2)}) copy-start(f32[8,256]{1,0:T(8,128)} %get-tuple-element.14.own) | copy-start | bytes 24580
  24.4 8.8 %copy-start.3 = (f32[16,256]{1,0:T(8,128)S(1)}, f32[16,256]{1,0:T(8,128)}, u32[]{:S(2)}) copy-start(f32[16,256]{1,0:T(8,128)} %sm.3) | copy-start | bytes 49156
  26.9 2.7 %collective-permute-start.2 = (f32[16,256]{1,0:T(8,128)S(1)}, f32[16,256]{1,0:T(8,128)S(1)}, u32[]{:S(2)}, u32[]{:S(2)}) collective-permute-start(f32[16,256]{1,0:T(8,128)S(1)} %get-tuple-element.18.l0), channel_id=1, source_target_pairs={{0,3},{1,0},{2,1},{3,2},{4,7},{5,4},{6,5},{7,6},{8,11},{9,8},{10,9... | collective-permute-start | bytes 49160 | tf_op jit(solution)/shard_map/ppermute | solution.py:306
  27.7 4.1 %collective-permute-start.1 = (f32[16,256]{1,0:T(8,128)S(1)}, f32[16,256]{1,0:T(8,128)S(1)}, u32[]{:S(2)}, u32[]{:S(2)}) collective-permute-start(f32[16,256]{1,0:T(8,128)S(1)} %get-tuple-element.18.l0), channel_id=1, source_target_pairs={{0,2},{1,3},{2,0},{3,1},{4,6},{5,7},{6,4},{7,5},{8,10},{9,11},{10,... | collective-permute-start | bytes 49160 | tf_op jit(solution)/shard_map/ppermute | solution.py:306
  29.0 4.1 %collective-permute-start = (f32[16,256]{1,0:T(8,128)S(1)}, f32[16,256]{1,0:T(8,128)S(1)}, u32[]{:S(2)}, u32[]{:S(2)}) collective-permute-start(f32[16,256]{1,0:T(8,128)S(1)} %get-tuple-element.18.l0), channel_id=1, source_target_pairs={{0,1},{1,2},{2,3},{3,0},{4,5},{5,6},{6,7},{7,4},{8,9},{9,10},{10,1... | collective-permute-start | bytes 49160 | tf_op jit(solution)/shard_map/ppermute | solution.py:306
  37.9 17.9 %copy-start.4 = (f32[8,256]{1,0:T(8,128)S(1)}, f32[8,256]{1,0:T(8,128)}, u32[]{:S(2)}) copy-start(f32[8,256]{1,0:T(8,128)} %get-tuple-element.21.mass) | copy-start | bytes 24580

commit v2 on v1

--- a/solution.py
+++ b/solution.py
@@ -53,7 +53,7 @@
 
 
 def centroid_kernel(listed, live, sp, sm, tp, tm, row_out, own_out, slice_out, order):
-    s, t = lax.axis_index("src"), lax.axis_index("tgt")
+    s = lax.axis_index("src")
     fill_order(order, listed, live)
     mass = sm[...]
     total = jnp.sum(mass, axis=1, keepdims=True)
@@ -65,11 +65,10 @@
     for q in range(4):
         z = jnp.where(lane == q, cols[q], z)
     zt = jnp.concatenate([z, jnp.zeros((128 - CL, 128), F32)], axis=0).T
-    lane = iota((1, 128), 1)
-    row = jnp.zeros((1, 128), F32)
-    for q in range(4):
-        piece = pltpu.roll(zt[q : q + 1, :], lax.rem(128 - 4 * t, 128), 1)
-        row = row + pltpu.roll(jnp.where(lane < 4, piece, 0.0), 4 * q, 1)
+    row = zt[0:1, :]
+    for q in range(1, 4):
+        row = row + pltpu.roll(zt[q : q + 1, :], CL * q, 1)
+    row_out[...] = jnp.broadcast_to(row, row_out.shape)
     slice_out[...] = tm[pl.ds(pl.multiple_of(8 * s, 8), 8), :]
     weight = tm[...]
     total = jnp.sum(weight, axis=0, keepdims=True)
@@ -78,10 +77,6 @@
     rows.append(jnp.log2(total))
     for q in range(4):
         own_out[q : q + 1, :] = rows[q]
-        half = jnp.where(s >= 16, rows[q][:, 128:], rows[q][:, :128])
-        piece = pltpu.roll(half, lax.rem(128 - 8 * lax.rem(s, 16), 128), 1)
-        row = row + pltpu.roll(jnp.where(lane < 8, piece, 0.0), 16 + 8 * q, 1)
-    row_out[...] = jnp.broadcast_to(row, row_out.shape)
 
 
 def dup(table, r, piece):
@@ -169,44 +164,39 @@
     l_out[...] = lrow[...]
 
 
-def coarse_kernel(got, own, r_in, l_in, g_out, l_out, terms, scores):
-    turned = got[...].T
-
-    def side(rows):
+def coarse_kernel(got, own, own1, own2, own3, r_in, l_in, g_out, l_out, terms, scores):
+    def side(table, h):
+        rows = [table[q : q + 1, h : h + 128] for q in range(4)]
         norm = rows[0] * rows[0] + rows[1] * rows[1] + rows[2] * rows[2]
         return [rows[0], rows[1], rows[2], rows[3] - (0.5 * ALPHA) * norm]
 
-    tgt = [side([turned[16 + 8 * q + li : 17 + 8 * q + li, :] for q in range(4)]) for li in range(8)]
-    mine = side([own[q : q + 1, :] for q in range(4)])
-    step = 32
+    tgt = [side(table, h) for table in (own, own1, own2, own3) for h in (0, 128)]
+    size = got.shape[0]
+    for c in range(CL):
+        x = [jnp.broadcast_to(ALPHA * got[:, CL * d + c : CL * d + c + 1], (size, 128)) for d in range(3)]
+        peak = None
+        for li, y in enumerate(tgt):
+            v = (y[3] + x[0] * y[0]) + (x[1] * y[1] + x[2] * y[2])
+            scores[li] = v
+            peak = v if peak is None else jnp.maximum(peak, v)
+            if li < 2:
+                terms[size * c : size * (c + 1), 128 * li : 128 * li + 128] = v
+        peak = jnp.max(peak, axis=1, keepdims=True)
+        total = jnp.exp2(scores[0] - peak)
+        for li in range(1, 8):
+            total = total + jnp.exp2(scores[li] - peak)
+        total = jnp.sum(total, axis=1, keepdims=True)
+        const = got[:, 3 * CL + c : 3 * CL + c + 1] - (peak + jnp.log2(total))
+        for h in (0, 128):
+            terms[size * c : size * (c + 1), h : h + 128] += jnp.broadcast_to(const, (size, 128))
     top_g = jnp.full((8, TGT), NEG, F32)
-    for ci in range(4):
-        for i in range(0, 128, step):
-            x = [jnp.broadcast_to(ALPHA * got[i : i + step, 4 * d + ci : 4 * d + ci + 1], (step, 128)) for d in range(3)]
-            peak = None
-            for li, y in enumerate(tgt):
-                v = (y[3] + x[0] * y[0]) + (x[1] * y[1] + x[2] * y[2])
-                scores[li] = v
-                peak = v if peak is None else jnp.maximum(peak, v)
-            peak = jnp.max(peak, axis=1, keepdims=True)
-            total = jnp.exp2(scores[0] - peak)
-            for li in range(1, 8):
-                total = total + jnp.exp2(scores[li] - peak)
-            total = jnp.sum(total, axis=1, keepdims=True)
-            const = got[i : i + step, 12 + ci : 13 + ci] - (peak + jnp.log2(total))
-            const = jnp.broadcast_to(const, (step, 128))
-            for h in (0, 128):
-                y = [row[:, h : h + 128] for row in mine]
-                v = (const + x[0] * y[0]) + (x[1] * y[1] + x[2] * y[2])
-                terms[128 * ci + i : 128 * ci + i + step, h : h + 128] = v
-    for i in range(0, 512, 8):
+    for i in range(0, size * CL, 8):
         top_g = jnp.maximum(top_g, terms[i : i + 8, :])
     top = jnp.max(top_g, axis=0, keepdims=True)
     total = jnp.zeros((8, TGT), F32)
-    for i in range(0, 512, 8):
+    for i in range(0, size * CL, 8):
         total = total + jnp.exp2(terms[i : i + 8, :] - top)
-    g = (mine[3] - own[3:4, :]) + top + jnp.log2(jnp.sum(total, axis=0, keepdims=True))
-    g = -g
+    g = own[3:4, :] - top - jnp.log2(jnp.sum(total, axis=0, keepdims=True))
     g_out[...] = jnp.broadcast_to(g, g_out.shape)
     at = l_in[...]
     lane = iota((128, 128), 1).astype(F32)
@@ -263,6 +253,10 @@
     out[...] = (g[...] - jnp.log2(1.0 + total / mass[...])) * UNSCALE
 
 
+def over_tgt(part):
+    return [part] + [lax.ppermute(part, "tgt", [(i, (i + k) % 4) for i in range(4)]) for k in (1, 2, 3)]
+
+
 def on_device(src_pts, src_mass, tgt_pts, tgt_mass, listed, live):
     shape = jax.ShapeDtypeStruct
     params = pltpu.CompilerParams(vmem_limit_bytes=LIMIT)
@@ -270,12 +264,13 @@
     counts = live.transpose(1, 0)
     row, own, mass, order = pl.pallas_call(
         centroid_kernel,
-        out_shape=(shape((128, 128), F32), shape((8, 256), F32), shape((8, 256), F32), shape((LIST,), I32)),
+        out_shape=(shape((32, 128), F32), shape((8, 256), F32), shape((8, 256), F32), shape((LIST,), I32)),
         in_specs=[SMEM, SMEM] + [VMEM] * 4,
         out_specs=(VMEM, VMEM, VMEM, SMEM),
         name="centroids",
     )(slots, counts, src_pts, src_mass, tgt_pts, tgt_mass)
-    got = lax.all_to_all(row, ("src", "tgt"), split_axis=0, concat_axis=0, tiled=True)
+    got = lax.all_to_all(row, "src", split_axis=0, concat_axis=0, tiled=True)
+    owns = over_tgt(own)
     r, where = pl.pallas_call(
         row_kernel,
         out_shape=(shape((BLOCKS, PTS), F32), shape((128, 128), F32)),
@@ -296,15 +291,13 @@
     g, part = pl.pallas_call(
         coarse_kernel,
         out_shape=(shape((8, 256), F32), shape((CL, PTS), F32)),
-        in_specs=[VMEM] * 4,
+        in_specs=[VMEM] * 7,
         out_specs=(VMEM, VMEM),
         scratch_shapes=[pltpu.VMEM((512, 256), F32), pltpu.VMEM((8, 32, 128), F32)],
         compiler_params=params,
         name="coarse",
-    )(got, own, r, where)
-    parts = [part] + [
-        lax.ppermute(part, "tgt", [(i, (i + k) % 4) for i in range(4)]) for k in (1, 2, 3)
-    ]
+    )(got, *owns, r, where)
+    parts = over_tgt(part)
     fine_f, sums = pl.pallas_call(
         column_kernel,
         out_shape=(shape((CL, PTS), F32), shape((32, 8, TGT), F32)),

time: 56.6 us -> 58.4 us (1.032)
  waiting for transfers between devices: 7.83 us -> 4.11 us
  starting transfers between devices: 13.7 us -> 17 us
  Pallas kernels: 15.7 us -> 17.1 us
  blocking collectives: 17.9 us -> 19.1 us
  local copies, waits for them, and re-layouts: 0.67 us -> 0.03 us
    ppermute x3 -> x6, starting transfers between devices: 2.18 us -> 7.6 us  [over_tgt(): lax.ppermute(part, 'tgt', [(i, (i + k) % 4) for i in range(4)])]
    all_to_all x1, waiting for transfers between devices: 3.74 us -> 0.01 us  [on_device(): got = lax.all_to_all(row, 'src', split_axis=0, concat_axis=0, tiled=True)]
    all_to_all x1, starting transfers between devices: 11.5 us -> 9.43 us  [on_device(): got = lax.all_to_all(row, 'src', split_axis=0, concat_axis=0, tiled=True)]
    all_to_all x1, blocking collectives: 17.9 us -> 19.1 us  [on_device(): lax.all_to_all(sums, 'src', split_axis=0, concat_axis=0, tiled=True)]
    unnamed x14, local copies, waits for them, and re-layouts: 0.67 us -> 0.03 us
    ppermute x3 -> x6, waiting for transfers between devices: 4.09 us -> 4.11 us  [over_tgt(): lax.ppermute(part, 'tgt', [(i, (i + k) % 4) for i in range(4)])]
  transfers between devices with their start and end apart: 4 -> 7, of which waited for: 4 -> 2; matrix products, arithmetic and copies ran while one was open for 0% -> 0% of each run, Pallas kernels for 10% -> 10%
where the time goes in v2:
time: 58.4 us; the launch traced here: 58.1 us
  blocking collectives  19.1 us (33%)
  Pallas kernels  17.1 us (29%)
  starting transfers between devices  17 us (29%)
  waiting for transfers between devices  4.11 us (7%)
  between operations  0.77 us (1%)
    all_to_all x1, blocking collectives, on_device(): lax.all_to_all(sums, 'src', split_axis=0, concat_axis=0, tiled=True)  19.1 us
    all_to_all x1, starting transfers between devices, on_device(): got = lax.all_to_all(row, 'src', split_axis=0, concat_axis=0, tiled=True)  9.43 us
    ppermute x6, starting transfers between devices, over_tgt(): lax.ppermute(part, 'tgt', [(i, (i + k) % 4) for i in range(4)])  7.6 us
    pallas_call x1, Pallas kernels, on_device(): pl.pallas_call(row_kernel, out_shape=(shape((BLOCKS, PTS), F32), shape((1...  6.07 us
    pallas_call x1, Pallas kernels, on_device(): pl.pallas_call(column_kernel, out_shape=(shape((CL, PTS), F32), shape((32...  5.19 us
    ppermute x6, waiting for transfers between devices, over_tgt(): lax.ppermute(part, 'tgt', [(i, (i + k) % 4) for i in range(4)])  4.11 us
    pallas_call x1, Pallas kernels, on_device(): pl.pallas_call(coarse_kernel, out_shape=(shape((8, 256), F32), shape((CL,...  3.03 us
    pallas_call x1, Pallas kernels, on_device(): pl.pallas_call(centroid_kernel, out_shape=(shape((32, 128), F32), shape((...  2.19 us
  transfers between devices with their start and end apart: 7, of which 2 were waited for; matrix products, arithmetic and copies ran while one was open for 0% of the time, Pallas kernels for 10%

profile of v2, /device:TPU:1, one launch (start us, length us, event | category | flops | bytes accessed | tf_op | source)
XLA Modules:
  0.0 58.1 jit_solution(13423185218696464556)
XLA Ops:
  0.6 0.0 copy-start
  0.6 0.0 copy-start.1
  0.7 0.0 copy-start.2
  0.7 2.2 %centroids.1 = (f32[32,128]{1,0:T(8,128)}, f32[8,256]{1,0:T(8,128)}, f32[8,256]{1,0:T(8,128)}, s32[160]{0:T(256)}) custom-call(s32[8,16]{1,0:T(8,128)} %bitcast.10, s32[1,16]{1,0:T(1,128)} %bitcast.11, f32[3,16,256]{2,1,0:T(8,128)} %sp.5, f32[16,256]{1,0:T(8,128)} %sm.3, f32[3,256,256]{2,1,0:T(8,128)} %tp.5, f32[256,256]{1,0:T(8,128)} %tm.5), custom_call_target="tpu_custom_call" | custom-call | tf_op jit(solution)/shard_map/centroids/pallas_call | solution.py:265
  2.9 0.0 copy-start.5
  2.9 9.4 %all-to-all-start = ((f32[32,1,128]{2,1,0:T(1,128)}), f32[32,1,128]{2,1,0:T(1,128)S(1)}, u32[]{:S(2)}, u32[]{:S(2)}) async-start(f32[32,1,128]{2,1,0:T(1,128)} %bitcast.9), calls=%async_computation | async-start | bytes 32768 | tf_op jit(solution)/shard_map/all_to_all | solution.py:272
  12.3 0.0 copy-done.5
  12.3 0.0 copy-start.6
  12.3 2.8 %collective-permute-start.2 = (f32[8,256]{1,0:T(8,128)S(1)}, f32[8,256]{1,0:T(8,128)S(1)}, u32[]{:S(2)}, u32[]{:S(2)}) collective-permute-start(f32[8,256]{1,0:T(8,128)S(1)} %copy-done.5), channel_id=1, source_target_pairs={{0,3},{1,0},{2,1},{3,2},{4,7},{5,4},{6,5},{7,6},{8,11},{9,8},{10,9... | collective-permute-start | bytes 24584 | tf_op jit(solution)/shard_map/ppermute | solution.py:257
  15.1 0.3 collective-permute-start.1
  15.5 0.7 %collective-permute-start = (f32[8,256]{1,0:T(8,128)S(1)}, f32[8,256]{1,0:T(8,128)S(1)}, u32[]{:S(2)}, u32[]{:S(2)}) collective-permute-start(f32[8,256]{1,0:T(8,128)S(1)} %copy-done.5), channel_id=1, source_target_pairs={{0,1},{1,2},{2,3},{3,0},{4,5},{5,6},{6,7},{7,4},{8,9},{9,10},{10,1... | collective-permute-start | bytes 24584 | tf_op jit(solution)/shard_map/ppermute | solution.py:257
  16.2 0.0 copy-done
  16.2 0.0 copy-done.1
  16.2 0.0 copy-done.2
  16.2 0.0 copy-done.6
  16.2 6.1 %rows.1 = (f32[128,256]{1,0:T(8,128)S(1)}, f32[128,128]{1,0:T(8,128)S(1)}) custom-call(s32[160]{0:T(256)S(1)} %copy-done.6, f32[3,16,256]{2,1,0:T(8,128)S(1)} %copy-done.2, f32[3,256,256]{2,1,0:T(8,128)S(1)} %copy-done, f32[256,256]{1,0:T(8,128)S(1)} %copy-done.1), custom_call_target="tpu_custom_call" | custom-call | flops 100000000 | bytes 10000000 | tf_op jit(solution)/shard_map/rows/pallas_call | solution.py:274
  22.3 0.0 collective-permute-done.2.own3
  22.3 0.0 collective-permute-done.1.own2
  22.3 0.0 collective-permute-done.own1
  22.3 0.0 all-to-all-done
  22.3 0.0 copy-start.3
  22.3 3.0 %coarse.1 = (f32[8,256]{1,0:T(8,128)S(1)}, f32[16,256]{1,0:T(8,128)S(1)}) custom-call(f32[32,128]{1,0:T(8,128)S(1)} %bitcast.8, f32[8,256]{1,0:T(8,128)S(1)} %copy-done.5, f32[8,256]{1,0:T(8,128)S(1)} %collective-permute-done.own1, f32[8,256]{1,0:T(8,128)S(1)} %collective-permute-done.1.own2, f32[8,256]{1,0:T(8,128)S(1)} %collective-permute-done.2.own3, ...), custom_call_target="tpu_custom_call" | custom-call | tf_op jit(solution)/shard_map/coarse/pallas_call | solution.py:291
  25.4 2.3 %collective-permute-start.5 = (f32[16,256]{1,0:T(8,128)S(1)}, f32[16,256]{1,0:T(8,128)S(1)}, u32[]{:S(2)}, u32[]{:S(2)}) collective-permute-start(f32[16,256]{1,0:T(8,128)S(1)} %get-tuple-element.18.l0), channel_id=1, source_target_pairs={{0,3},{1,0},{2,1},{3,2},{4,7},{5,4},{6,5},{7,6},{8,11},{9,8},{10,9... | collective-permute-start | bytes 49160 | tf_op jit(solution)/shard_map/ppermute | solution.py:257
  27.7 1.4 %collective-permute-start.4 = (f32[16,256]{1,0:T(8,128)S(1)}, f32[16,256]{1,0:T(8,128)S(1)}, u32[]{:S(2)}, u32[]{:S(2)}) collective-permute-start(f32[16,256]{1,0:T(8,128)S(1)} %get-tuple-element.18.l0), channel_id=1, source_target_pairs={{0,2},{1,3},{2,0},{3,1},{4,6},{5,7},{6,4},{7,5},{8,10},{9,11},{10,... | collective-permute-start | bytes 49160 | tf_op jit(solution)/shard_map/ppermute | solution.py:257
  29.1 0.0 collective-permute-start.3
  29.1 0.0 collective-permute-done.5.l3
  29.1 2.7 %collective-permute-done.4.l2 = f32[16,256]{1,0:T(8,128)S(1)} collective-permute-done((f32[16,256]{1,0:T(8,128)S(1)}, f32[16,256]{1,0:T(8,128)S(1)}, u32[]{:S(2)}, u32[]{:S(2)}) %collective-permute-start.4) | collective-permute-done | bytes 16416 | tf_op jit(solution)/shard_map/ppermute | solution.py:257
  31.8 1.4 %collective-permute-done.3.l1 = f32[16,256]{1,0:T(8,128)S(1)} collective-permute-done((f32[16,256]{1,0:T(8,128)S(1)}, f32[16,256]{1,0:T(8,128)S(1)}, u32[]{:S(2)}, u32[]{:S(2)}) %collective-permute-start.3) | collective-permute-done | bytes 16416 | tf_op jit(solution)/shard_map/ppermute | solution.py:257
  33.2 0.0 copy-done.3
  33.2 5.2 %columns.1 = (f32[16,256]{1,0:T(8,128)}, f32[32,8,256]{2,1,0:T(8,128)S(1)}) custom-call(s32[160]{0:T(256)S(1)} %copy-done.6, f32[8,256]{1,0:T(8,128)S(1)} %get-tuple-element.17.g, f32[3,16,256]{2,1,0:T(8,128)S(1)} %copy-done.2, f32[16,256]{1,0:T(8,128)S(1)} %copy-done.3, f32[3,256,256]{2,1,0:T(8,128)S(1)} %copy-done, f32[256,256]{1,0:T(8,128)S(1)} %copy-done.1, ...), custom_call_target="tpu_custom_call" | custom-call | tf_op jit(solution)/shard_map/columns/pallas_call | solution.py:301
  38.4 0.0 copy-start.4
  38.4 19.1 %all_to_all.16.arrived = f32[32,8,256]{2,1,0:T(8,128)S(1)} all-to-all(f32[32,8,256]{2,1,0:T(8,128)S(1)} %get-tuple-element.20), channel_id=1, replica_groups=mesh['src'=32,'tgt'=4] {'src'}, dimensions={0} | all-to-all | bytes 524288 | tf_op jit(solution)/shard_map/all_to_all | solution.py:317
  57.5 0.0 copy-done.4
  57.5 0.6 %final.1 = f32[8,256]{1,0:T(8,128)} custom-call(f32[32,8,256]{2,1,0:T(8,128)S(1)} %all_to_all.16.arrived, f32[8,256]{1,0:T(8,128)S(1)} %copy-done.4, f32[8,256]{1,0:T(8,128)S(1)} %get-tuple-element.17.g), custom_call_target="tpu_custom_call" | custom-call | tf_op jit(solution)/shard_map/final/pallas_call | solution.py:318
Async XLA Ops:
  0.6 15.5 %copy-start = (f32[3,256,256]{2,1,0:T(8,128)S(1)}, f32[3,256,256]{2,1,0:T(8,128)}, u32[]{:S(2)}) copy-start(f32[3,256,256]{2,1,0:T(8,128)} %tp.5) | copy-start | bytes 2359300
  0.6 15.5 %copy-start.1 = (f32[256,256]{1,0:T(8,128)S(1)}, f32[256,256]{1,0:T(8,128)}, u32[]{:S(2)}) copy-start(f32[256,256]{1,0:T(8,128)} %tm.5) | copy-start | bytes 786436
  0.7 15.5 %copy-start.2 = (f32[3,16,256]{2,1,0:T(8,128)S(1)}, f32[3,16,256]{2,1,0:T(8,128)}, u32[]{:S(2)}) copy-start(f32[3,16,256]{2,1,0:T(8,128)} %sp.5) | copy-start | bytes 147460
  2.9 9.5 %copy-start.5 = (f32[8,256]{1,0:T(8,128)S(1)}, f32[8,256]{1,0:T(8,128)}, u32[]{:S(2)}) copy-start(f32[8,256]{1,0:T(8,128)} %get-tuple-element.14.own) | copy-start | bytes 24580
  2.9 19.4 %all-to-all-start = ((f32[32,1,128]{2,1,0:T(1,128)}), f32[32,1,128]{2,1,0:T(1,128)S(1)}, u32[]{:S(2)}, u32[]{:S(2)}) async-start(f32[32,1,128]{2,1,0:T(1,128)} %bitcast.9), calls=%async_computation | async-start | bytes 32768 | tf_op jit(solution)/shard_map/all_to_all | solution.py:272
  12.3 3.9 %copy-start.6 = (s32[160]{0:T(256)S(1)}, s32[160]{0:T(256)}, u32[]{:S(2)}) copy-start(s32[160]{0:T(256)} %get-tuple-element.12.order) | copy-start | bytes 1924
  12.3 9.9 %collective-permute-start.2 = (f32[8,256]{1,0:T(8,128)S(1)}, f32[8,256]{1,0:T(8,128)S(1)}, u32[]{:S(2)}, u32[]{:S(2)}) collective-permute-start(f32[8,256]{1,0:T(8,128)S(1)} %copy-done.5), channel_id=1, source_target_pairs={{0,3},{1,0},{2,1},{3,2},{4,7},{5,4},{6,5},{7,6},{8,11},{9,8},{10,9... | collective-permute-start | bytes 24584 | tf_op jit(solution)/shard_map/ppermute | solution.py:257
  15.1 7.1 %collective-permute-start.1 = (f32[8,256]{1,0:T(8,128)S(1)}, f32[8,256]{1,0:T(8,128)S(1)}, u32[]{:S(2)}, u32[]{:S(2)}) collective-permute-start(f32[8,256]{1,0:T(8,128)S(1)} %copy-done.5), channel_id=1, source_target_pairs={{0,2},{1,3},{2,0},{3,1},{4,6},{5,7},{6,4},{7,5},{8,10},{9,11},{10,... | collective-permute-start | bytes 24584 | tf_op jit(solution)/shard_map/ppermute | solution.py:257
  15.5 6.8 %collective-permute-start = (f32[8,256]{1,0:T(8,128)S(1)}, f32[8,256]{1,0:T(8,128)S(1)}, u32[]{:S(2)}, u32[]{:S(2)}) collective-permute-start(f32[8,256]{1,0:T(8,128)S(1)} %copy-done.5), channel_id=1, source_target_pairs={{0,1},{1,2},{2,3},{3,0},{4,5},{5,6},{6,7},{7,4},{8,9},{9,10},{10,1... | collective-permute-start | bytes 24584 | tf_op jit(solution)/shard_map/ppermute | solution.py:257
  22.3 10.9 %copy-start.3 = (f32[16,256]{1,0:T(8,128)S(1)}, f32[16,256]{1,0:T(8,128)}, u32[]{:S(2)}) copy-start(f32[16,256]{1,0:T(8,128)} %sm.3) | copy-start | bytes 49156
  25.4 3.8 %collective-permute-start.5 = (f32[16,256]{1,0:T(8,128)S(1)}, f32[16,256]{1,0:T(8,128)S(1)}, u32[]{:S(2)}, u32[]{:S(2)}) collective-permute-start(f32[16,256]{1,0:T(8,128)S(1)} %get-tuple-element.18.l0), channel_id=1, source_target_pairs={{0,3},{1,0},{2,1},{3,2},{4,7},{5,4},{6,5},{7,6},{8,11},{9,8},{10,9... | collective-permute-start | bytes 49160 | tf_op jit(solution)/shard_map/ppermute | solution.py:257
  27.7 4.1 %collective-permute-start.4 = (f32[16,256]{1,0:T(8,128)S(1)}, f32[16,256]{1,0:T(8,128)S(1)}, u32[]{:S(2)}, u32[]{:S(2)}) collective-permute-start(f32[16,256]{1,0:T(8,128)S(1)} %get-tuple-element.18.l0), channel_id=1, source_target_pairs={{0,2},{1,3},{2,0},{3,1},{4,6},{5,7},{6,4},{7,5},{8,10},{9,11},{10,... | collective-permute-start | bytes 49160 | tf_op jit(solution)/shard_map/ppermute | solution.py:257
  29.1 4.1 %collective-permute-start.3 = (f32[16,256]{1,0:T(8,128)S(1)}, f32[16,256]{1,0:T(8,128)S(1)}, u32[]{:S(2)}, u32[]{:S(2)}) collective-permute-start(f32[16,256]{1,0:T(8,128)S(1)} %get-tuple-element.18.l0), channel_id=1, source_target_pairs={{0,1},{1,2},{2,3},{3,0},{4,5},{5,6},{6,7},{7,4},{8,9},{9,10},{10,1... | collective-permute-start | bytes 49160 | tf_op jit(solution)/shard_map/ppermute | solution.py:257
  38.4 19.1 %copy-start.4 = (f32[8,256]{1,0:T(8,128)S(1)}, f32[8,256]{1,0:T(8,128)}, u32[]{:S(2)}) copy-start(f32[8,256]{1,0:T(8,128)} %get-tuple-element.21.mass) | copy-start | bytes 24580

commit v3 on v1

--- a/solution.py
+++ b/solution.py
@@ -15,8 +15,12 @@
 F32, BF16, I32 = jnp.float32, jnp.bfloat16, jnp.int32
 CL, SLOTS, PTS, TGT = 16, 8, 256, 256
 BLOCKS = CL * SLOTS
-UNROLL = 8
-AHEAD = 4
+SAMPLE = 32
+MARGIN = 90.0
+HUGE = 1e36
+BATCH = 8
+MANY = 16
+FEW = 4
 PAD = 16
 LIST = BLOCKS + 2 * PAD
 LIMIT = 16 << 20
@@ -123,45 +127,65 @@
         dup(table, 12 + r, piece)
 
 
-def row_kernel(order, sp, tp, tm, r_out, l_out, tab, gt, gf, scol, lrow, *sets):
-    sets = [sets[3 * u : 3 * u + 3] for u in range(AHEAD)]
+def exp_sum(score):
+    total = jnp.zeros((8, PTS), F32)
+    for o in range(0, TGT, 8):
+        total = total + jnp.exp2(score[o : o + 8, :])
+    return jnp.sum(total, axis=0, keepdims=True)
+
+
+def row_kernel(order, sp, tp, tm, r_out, l_out, tab, gt, gf, scol, lrow, *scratch):
+    factors = [scratch[2 * u : 2 * u + 2] for u in range(BATCH)]
     n = order[LIST - 1]
     zero = jnp.zeros((CL, PTS), F32)
     source_factors(gf, [sp[d] * ALPHA for d in range(3)], [zero] * 4)
     for c in range(CL):
-        gt[c] = jnp.concatenate([gf[h, 16 * c : 16 * c + 16, :] for h in range(2)], axis=1).astype(BF16)
+        gt[c] = jnp.concatenate([gf[h, 16 * c : 16 * c + 16, :] for h in range(2)], axis=1)
     fill_tables(tab, tp, tm)
     lrow[...] = jnp.full((BLOCKS, 128), -1.0, F32)
-
-    def prepare(i, lhs):
-        at = order[i] & (TGT - 1)
-        lhs[...] = target_factors(tab, at, None).T
-        lrow[pl.ds(order[i] >> 8, 1), :] = jnp.broadcast_to(at.astype(F32), (1, 128))
-
-    for u in range(AHEAD):
-        prepare(u, sets[u][0])
+    scol[...] = jnp.zeros((BLOCKS, PTS), F32)
+    sub = iota((16, PTS), 0)
+
+    def prepare(i, lhs, rhs):
+        b, at = order[i] >> 8, order[i] & (TGT - 1)
+        left = target_factors(tab, at, None).T
+        right = gt[b & (CL - 1)]
+        seen = jnp.dot(left[:SAMPLE, :], right.astype(BF16), preferred_element_type=F32)
+        shift = jnp.max(seen, axis=0, keepdims=True) + MARGIN
+        for r, piece in enumerate(split3(-shift)):
+            right = jnp.where(sub == 12 + r, piece, right)
+        lhs[...] = left
+        rhs[...] = right.astype(BF16)
+        r_out[pl.ds(b, 1), :] = shift
+        lrow[pl.ds(b, 1), :] = jnp.broadcast_to(at.astype(F32), (1, 128))
+
+    for u in range(BATCH):
+        prepare(u, *factors[u])
 
     def batch(i, _):
-        at = AHEAD * i
-        v = [jnp.dot(sets[u][0][...], gt[(order[at + u] >> 8) & (CL - 1)], preferred_element_type=F32) for u in range(AHEAD)]
-        for u in range(AHEAD):
-            prepare(at + AHEAD + u, sets[u][0])
-        for u in range(AHEAD):
-            lhs, score, tops = sets[u]
-            top_old = tops[...]
-            total = jnp.zeros((8, PTS), F32)
-            top = jnp.full((8, PTS), NEG, F32)
-            for j in range(0, TGT, 8):
-                total = total + jnp.exp2(score[j : j + 8, :] - top_old)
-                score[j : j + 8, :] = v[u][j : j + 8, :]
-                top = jnp.maximum(top, v[u][j : j + 8, :])
-            tops[...] = jnp.broadcast_to(jnp.max(top, axis=0, keepdims=True), (8, PTS))
-            old = order[jnp.maximum(at - AHEAD + u, 0)] >> 8
-            r_out[pl.ds(old, 1), :] = top_old[0:1, :]
-            scol[pl.ds(old, 1), :] = jnp.sum(total, axis=0, keepdims=True)
+        at = BATCH * i
+        scores = [jnp.dot(lhs[...], rhs[...], preferred_element_type=F32) for lhs, rhs in factors]
+        for u in range(BATCH):
+            prepare(at + BATCH + u, *factors[u])
+        for u in range(BATCH):
+            scol[pl.ds(order[at + u] >> 8, 1), :] = exp_sum(scores[u])
         return 0
 
-    lax.fori_loop(0, (n + AHEAD - 1) // AHEAD + 1, batch, 0)
+    lax.fori_loop(0, (n + BATCH - 1) // BATCH, batch, 0)
+
+    @pl.when(jnp.max(scol[...]) > HUGE)
+    def _():
+        def exact(i, _):
+            b = order[i] >> 8
+            left = target_factors(tab, order[i] & (TGT - 1), None).T
+            v = jnp.dot(left, gt[b & (CL - 1)].astype(BF16), preferred_element_type=F32)
+            top = jnp.max(v, axis=0, keepdims=True)
+            r_out[pl.ds(b, 1), :] = top
+            scol[pl.ds(b, 1), :] = jnp.sum(jnp.exp2(v - top), axis=0, keepdims=True)
+            return 0
+
+        lax.fori_loop(0, n, exact, 0)
+
     xn = (-0.5 * ALPHA) * (sp[0] * sp[0] + sp[1] * sp[1] + sp[2] * sp[2])
     r = r_out[...] + jnp.log2(scol[...])
     r = (r.reshape(SLOTS, CL, PTS) + xn[None]).reshape(BLOCKS, PTS)
@@ -233,27 +257,21 @@
         gt[c] = jnp.concatenate([gf[h, 16 * c : 16 * c + 16, :] for h in range(2)], axis=1).astype(BF16).T
     n = order[LIST - 1]
 
-    def batch(i, _):
-        at = i * UNROLL
-        v = []
-        for u in range(UNROLL):
+    def batch(at, size):
+        scores = []
+        for u in range(size):
             left = gt[(order[at + u] >> 8) & (CL - 1)]
             to = order[at + u] & (TGT - 1)
-            right = target_factors(tab, to, g[0, to])
-            v.append(jnp.dot(left, right, preferred_element_type=F32))
-        lines = []
-        for u in range(UNROLL):
-            total = jnp.zeros((8, TGT), F32)
-            for o in range(0, PTS, 8):
-                total = total + jnp.exp2(v[u][o : o + 8, :])
-            line = jnp.sum(total, axis=0, keepdims=True)
-            lines.append(jnp.where(at + u < n, line, 0.0))
-        for u in range(UNROLL):
+            scores.append(jnp.dot(left, target_factors(tab, to, g[0, to]), preferred_element_type=F32))
+        lines = [jnp.where(at + u < n, exp_sum(scores[u]), 0.0) for u in range(size)]
+        for u in range(size):
             to = pl.ds(order[at + u] & (TGT - 1), 1)
             st[to, :] = st[to, :] + lines[u]
         return 0
 
-    lax.fori_loop(0, (n + UNROLL - 1) // UNROLL, batch, 0)
+    whole = n // MANY
+    lax.fori_loop(0, whole, lambda i, _: batch(MANY * i, MANY), 0)
+    lax.fori_loop(0, (n - MANY * whole + FEW - 1) // FEW, lambda i, _: batch(MANY * whole + FEW * i, FEW), 0)
     s_out[...] = st[...].T.reshape(32, 8, TGT)
     send.wait()
 
@@ -266,6 +284,7 @@
 def on_device(src_pts, src_mass, tgt_pts, tgt_mass, listed, live):
     shape = jax.ShapeDtypeStruct
     params = pltpu.CompilerParams(vmem_limit_bytes=LIMIT)
+    stages = [pltpu.VMEM((TGT, 16), BF16), pltpu.VMEM((16, PTS), BF16)] * BATCH
     slots = listed.transpose(1, 2, 0).reshape(SLOTS, CL)
     counts = live.transpose(1, 0)
     row, own, mass, order = pl.pallas_call(
@@ -283,12 +302,12 @@
         out_specs=(VMEM, VMEM),
         scratch_shapes=[
             pltpu.VMEM((7, TGT, PTS), F32),
-            pltpu.VMEM((CL, 16, PTS), BF16),
+            pltpu.VMEM((CL, 16, PTS), F32),
             pltpu.VMEM((2, CL * 16, 128), F32),
             pltpu.VMEM((BLOCKS, PTS), F32),
             pltpu.VMEM((BLOCKS, 128), F32),
         ]
-        + [pltpu.VMEM((TGT, 16), BF16), pltpu.VMEM((TGT, PTS), F32), pltpu.VMEM((8, PTS), F32)] * AHEAD,
+        + stages,
         cost_estimate=pl.CostEstimate(flops=100_000_000, bytes_accessed=10_000_000, transcendentals=5_000_000),
         compiler_params=params,
         name="rows",

time: 56.6 us -> 55 us (0.972); the launches traced: 56.4 us -> 54.2 us
  blocking collectives: 17.9 us -> 15.7 us
    all_to_all x1, blocking collectives: 17.9 us -> 15.7 us  [on_device(): lax.all_to_all(sums, 'src', split_axis=0, concat_axis=0, tiled=True)]
where the time goes in v3:
time: 55 us; the launch traced here: 54.2 us
  Pallas kernels  15.7 us (29%)
  blocking collectives  15.7 us (29%)
  starting transfers between devices  13.7 us (25%)
  waiting for transfers between devices  7.78 us (14%)
  between operations  0.73 us (1%)
  local copies, waits for them, and re-layouts  0.67 us (1%)
    all_to_all x1, blocking collectives, on_device(): lax.all_to_all(sums, 'src', split_axis=0, concat_axis=0, tiled=True)  15.7 us
    all_to_all x1, starting transfers between devices, on_device(): lax.all_to_all(row, ('src', 'tgt'), split_axis=0, concat_axis=0, tiled=True)  11.5 us
    pallas_call x1, Pallas kernels, on_device(): pl.pallas_call(row_kernel, out_shape=(shape((BLOCKS, PTS), F32), shape((1...  5.54 us
    pallas_call x1, Pallas kernels, on_device(): pl.pallas_call(column_kernel, out_shape=(shape((CL, PTS), F32), shape((32...  4.7 us
    ppermute x3, waiting for transfers between devices, on_device(): lax.ppermute(part, 'tgt', [(i, (i + k) % 4) for i in range(4)])  4.09 us
    all_to_all x1, waiting for transfers between devices, on_device(): lax.all_to_all(row, ('src', 'tgt'), split_axis=0, concat_axis=0, tiled=True)  3.69 us
    pallas_call x1, Pallas kernels, on_device(): pl.pallas_call(coarse_kernel, out_shape=(shape((8, 256), F32), shape((CL,...  2.51 us
    pallas_call x1, Pallas kernels, on_device(): pl.pallas_call(centroid_kernel, out_shape=(shape((128, 128), F32), shape(...  2.26 us
  transfers between devices with their start and end apart: 4, of which 4 were waited for; matrix products, arithmetic and copies ran while one was open for 0% of the time, Pallas kernels for 10%

profile of v3, /device:TPU:1, one launch (start us, length us, event | category | flops | bytes accessed | tf_op | source)
XLA Modules:
  0.0 54.2 jit_solution(10286367250803777497)
XLA Ops:
  0.6 0.0 copy-start
  0.6 0.0 copy-start.1
  0.7 2.3 %centroids.1 = (f32[128,128]{1,0:T(8,128)}, f32[8,256]{1,0:T(8,128)}, f32[8,256]{1,0:T(8,128)}, s32[160]{0:T(256)}) custom-call(s32[8,16]{1,0:T(8,128)} %bitcast.10, s32[1,16]{1,0:T(1,128)} %bitcast.11, f32[3,16,256]{2,1,0:T(8,128)} %sp.5, f32[16,256]{1,0:T(8,128)} %sm.3, f32[3,256,256]{2,1,0:T(8,128)} %tp.5, f32[256,256]{1,0:T(8,128)} %tm.5), custom_call_target="tpu_custom_call" | custom-call | tf_op jit(solution)/shard_map/centroids/pallas_call | solution.py:290
  2.9 0.0 copy-start.2
  2.9 11.5 %all-to-all-start = ((f32[128,1,128]{2,1,0:T(1,128)}), f32[128,1,128]{2,1,0:T(1,128)S(1)}, u32[]{:S(2)}, u32[]{:S(2)}) async-start(f32[128,1,128]{2,1,0:T(1,128)} %bitcast.9), calls=%async_computation | async-start | bytes 131072 | tf_op jit(solution)/shard_map/all_to_all | solution.py:297
  14.4 0.0 copy-start.6
  14.4 0.0 copy-done
  14.5 0.0 copy-done.1
  14.5 0.0 copy-done.2
  14.5 0.6 %copy-done.6 = s32[160]{0:T(256)S(1)} copy-done((s32[160]{0:T(256)S(1)}, s32[160]{0:T(256)}, u32[]{:S(2)}) %copy-start.6) | copy-done | bytes 664
  15.1 0.0 copy-start.5
  15.1 5.5 %rows.1 = (f32[128,256]{1,0:T(8,128)S(1)}, f32[128,128]{1,0:T(8,128)S(1)}) custom-call(s32[160]{0:T(256)S(1)} %copy-done.6, f32[3,16,256]{2,1,0:T(8,128)S(1)} %copy-done.2, f32[3,256,256]{2,1,0:T(8,128)S(1)} %copy-done, f32[256,256]{1,0:T(8,128)S(1)} %copy-done.1), custom_call_target="tpu_custom_call" | custom-call | flops 100000000 | bytes 10000000 | tf_op jit(solution)/shard_map/rows/pallas_call | solution.py:298
  20.7 3.7 %all-to-all-done = f32[128,1,128]{2,1,0:T(1,128)S(1)} async-done(((f32[128,1,128]{2,1,0:T(1,128)}), f32[128,1,128]{2,1,0:T(1,128)S(1)}, u32[]{:S(2)}, u32[]{:S(2)}) %all-to-all-start) | async-done | bytes 65568 | tf_op jit(solution)/shard_map/all_to_all | solution.py:297
  24.4 0.0 copy-done.5
  24.4 0.0 copy-start.3
  24.4 2.5 %coarse.1 = (f32[8,256]{1,0:T(8,128)S(1)}, f32[16,256]{1,0:T(8,128)S(1)}) custom-call(f32[128,128]{1,0:T(8,128)S(1)} %bitcast.8, f32[8,256]{1,0:T(8,128)S(1)} %copy-done.5, f32[128,256]{1,0:T(8,128)S(1)} %get-tuple-element.15.r_in, f32[128,128]{1,0:T(8,128)S(1)} %get-tuple-element.16.l_in), custom_call_target="tpu_custom_call" | custom-call | tf_op jit(solution)/shard_map/coarse/pallas_call | solution.py:315
  26.9 0.9 %collective-permute-start.2 = (f32[16,256]{1,0:T(8,128)S(1)}, f32[16,256]{1,0:T(8,128)S(1)}, u32[]{:S(2)}, u32[]{:S(2)}) collective-permute-start(f32[16,256]{1,0:T(8,128)S(1)} %get-tuple-element.18.l0), channel_id=1, source_target_pairs={{0,3},{1,0},{2,1},{3,2},{4,7},{5,4},{6,5},{7,6},{8,11},{9,8},{10,9... | collective-permute-start | bytes 49160 | tf_op jit(solution)/shard_map/ppermute | solution.py:325
  27.7 1.3 %collective-permute-start.1 = (f32[16,256]{1,0:T(8,128)S(1)}, f32[16,256]{1,0:T(8,128)S(1)}, u32[]{:S(2)}, u32[]{:S(2)}) collective-permute-start(f32[16,256]{1,0:T(8,128)S(1)} %get-tuple-element.18.l0), channel_id=1, source_target_pairs={{0,2},{1,3},{2,0},{3,1},{4,6},{5,7},{6,4},{7,5},{8,10},{9,11},{10,... | collective-permute-start | bytes 49160 | tf_op jit(solution)/shard_map/ppermute | solution.py:325
  29.0 0.0 collective-permute-start
  29.1 0.5 collective-permute-done.2.l3
  29.5 2.3 %collective-permute-done.1.l2 = f32[16,256]{1,0:T(8,128)S(1)} collective-permute-done((f32[16,256]{1,0:T(8,128)S(1)}, f32[16,256]{1,0:T(8,128)S(1)}, u32[]{:S(2)}, u32[]{:S(2)}) %collective-permute-start.1) | collective-permute-done | bytes 16416 | tf_op jit(solution)/shard_map/ppermute | solution.py:325
  31.8 1.3 %collective-permute-done.l1 = f32[16,256]{1,0:T(8,128)S(1)} collective-permute-done((f32[16,256]{1,0:T(8,128)S(1)}, f32[16,256]{1,0:T(8,128)S(1)}, u32[]{:S(2)}, u32[]{:S(2)}) %collective-permute-start) | collective-permute-done | bytes 16416 | tf_op jit(solution)/shard_map/ppermute | solution.py:325
  33.1 0.0 copy-done.3
  33.1 4.7 %columns.1 = (f32[16,256]{1,0:T(8,128)}, f32[32,8,256]{2,1,0:T(8,128)S(1)}) custom-call(s32[160]{0:T(256)S(1)} %copy-done.6, f32[8,256]{1,0:T(8,128)S(1)} %get-tuple-element.17.g, f32[3,16,256]{2,1,0:T(8,128)S(1)} %copy-done.2, f32[16,256]{1,0:T(8,128)S(1)} %copy-done.3, f32[3,256,256]{2,1,0:T(8,128)S(1)} %copy-done, f32[256,256]{1,0:T(8,128)S(1)} %copy-done.1, ...), custom_call_target="tpu_custom_call" | custom-call | tf_op jit(solution)/shard_map/columns/pallas_call | solution.py:327
  37.9 0.0 copy-start.4
  37.9 15.7 %all_to_all.16.arrived = f32[32,8,256]{2,1,0:T(8,128)S(1)} all-to-all(f32[32,8,256]{2,1,0:T(8,128)S(1)} %get-tuple-element.20), channel_id=1, replica_groups=mesh['src'=32,'tgt'=4] {'src'}, dimensions={0} | all-to-all | bytes 524288 | tf_op jit(solution)/shard_map/all_to_all | solution.py:343
  53.6 0.0 copy-done.4
  53.6 0.6 %final.1 = f32[8,256]{1,0:T(8,128)} custom-call(f32[32,8,256]{2,1,0:T(8,128)S(1)} %all_to_all.16.arrived, f32[8,256]{1,0:T(8,128)S(1)} %copy-done.4, f32[8,256]{1,0:T(8,128)S(1)} %get-tuple-element.17.g), custom_call_target="tpu_custom_call" | custom-call | tf_op jit(solution)/shard_map/final/pallas_call | solution.py:344
Async XLA Ops:
  0.6 13.8 %copy-start = (f32[3,256,256]{2,1,0:T(8,128)S(1)}, f32[3,256,256]{2,1,0:T(8,128)}, u32[]{:S(2)}) copy-start(f32[3,256,256]{2,1,0:T(8,128)} %tp.5) | copy-start | bytes 2359300
  0.6 13.8 %copy-start.1 = (f32[256,256]{1,0:T(8,128)S(1)}, f32[256,256]{1,0:T(8,128)}, u32[]{:S(2)}) copy-start(f32[256,256]{1,0:T(8,128)} %tm.5) | copy-start | bytes 786436
  2.9 11.5 %copy-start.2 = (f32[3,16,256]{2,1,0:T(8,128)S(1)}, f32[3,16,256]{2,1,0:T(8,128)}, u32[]{:S(2)}) copy-start(f32[3,16,256]{2,1,0:T(8,128)} %sp.5) | copy-start | bytes 147460
  2.9 21.4 %all-to-all-start = ((f32[128,1,128]{2,1,0:T(1,128)}), f32[128,1,128]{2,1,0:T(1,128)S(1)}, u32[]{:S(2)}, u32[]{:S(2)}) async-start(f32[128,1,128]{2,1,0:T(1,128)} %bitcast.9), calls=%async_computation | async-start | bytes 131072 | tf_op jit(solution)/shard_map/all_to_all | solution.py:297
  14.4 0.7 %copy-start.6 = (s32[160]{0:T(256)S(1)}, s32[160]{0:T(256)}, u32[]{:S(2)}) copy-start(s32[160]{0:T(256)} %get-tuple-element.12.order) | copy-start | bytes 1924
  15.1 9.2 %copy-start.5 = (f32[8,256]{1,0:T(8,128)S(1)}, f32[8,256]{1,0:T(8,128)}, u32[]{:S(2)}) copy-start(f32[8,256]{1,0:T(8,128)} %get-tuple-element.14.own) | copy-start | bytes 24580
  24.4 8.8 %copy-start.3 = (f32[16,256]{1,0:T(8,128)S(1)}, f32[16,256]{1,0:T(8,128)}, u32[]{:S(2)}) copy-start(f32[16,256]{1,0:T(8,128)} %sm.3) | copy-start | bytes 49156
  26.9 2.7 %collective-permute-start.2 = (f32[16,256]{1,0:T(8,128)S(1)}, f32[16,256]{1,0:T(8,128)S(1)}, u32[]{:S(2)}, u32[]{:S(2)}) collective-permute-start(f32[16,256]{1,0:T(8,128)S(1)} %get-tuple-element.18.l0), channel_id=1, source_target_pairs={{0,3},{1,0},{2,1},{3,2},{4,7},{5,4},{6,5},{7,6},{8,11},{9,8},{10,9... | collective-permute-start | bytes 49160 | tf_op jit(solution)/shard_map/ppermute | solution.py:325
  27.7 4.1 %collective-permute-start.1 = (f32[16,256]{1,0:T(8,128)S(1)}, f32[16,256]{1,0:T(8,128)S(1)}, u32[]{:S(2)}, u32[]{:S(2)}) collective-permute-start(f32[16,256]{1,0:T(8,128)S(1)} %get-tuple-element.18.l0), channel_id=1, source_target_pairs={{0,2},{1,3},{2,0},{3,1},{4,6},{5,7},{6,4},{7,5},{8,10},{9,11},{10,... | collective-permute-start | bytes 49160 | tf_op jit(solution)/shard_map/ppermute | solution.py:325
  29.0 4.1 %collective-permute-start = (f32[16,256]{1,0:T(8,128)S(1)}, f32[16,256]{1,0:T(8,128)S(1)}, u32[]{:S(2)}, u32[]{:S(2)}) collective-permute-start(f32[16,256]{1,0:T(8,128)S(1)} %get-tuple-element.18.l0), channel_id=1, source_target_pairs={{0,1},{1,2},{2,3},{3,0},{4,5},{5,6},{6,7},{7,4},{8,9},{9,10},{10,1... | collective-permute-start | bytes 49160 | tf_op jit(solution)/shard_map/ppermute | solution.py:325
  37.9 15.7 %copy-start.4 = (f32[8,256]{1,0:T(8,128)S(1)}, f32[8,256]{1,0:T(8,128)}, u32[]{:S(2)}) copy-start(f32[8,256]{1,0:T(8,128)} %get-tuple-element.21.mass) | copy-start | bytes 24580

commit v4 on v3

--- a/solution.py
+++ b/solution.py
@@ -194,43 +194,63 @@
 
 
 def coarse_kernel(got, own, r_in, l_in, g_out, l_out, terms, scores):
-    turned = got[...].T
-
-    def side(rows):
-        norm = rows[0] * rows[0] + rows[1] * rows[1] + rows[2] * rows[2]
-        return [rows[0], rows[1], rows[2], rows[3] - (0.5 * ALPHA) * norm]
-
-    tgt = [side([turned[16 + 8 * q + li : 17 + 8 * q + li, :] for q in range(4)]) for li in range(8)]
-    mine = side([own[q : q + 1, :] for q in range(4)])
-    step = 32
+    table = got[...]
+    turned = table.T
+    high = bf16_part(ALPHA * table)
+    mid = bf16_part(ALPHA * table - high)
+    lane = iota((256, 64), 1)
+    r = lane & 15
+    d = (r >= 3).astype(I32) + (r >= 6).astype(I32)
+    wanted = 4 * d + (lane >> 4) + jnp.where(r - 3 * d == 1, 128, 0)
+    pick = jnp.where((r < 9) & (iota((256, 64), 0) == wanted), 1.0, 0.0).astype(BF16)
+    left = jnp.dot(jnp.concatenate([high, mid], axis=1).astype(BF16), pick, preferred_element_type=F32)
+    r = iota((128, 64), 1) & 15
+    left = jnp.where((r >= 9) & (r < 12), 1.0, left).astype(BF16)
+
+    def target_rows(y, mass):
+        rows = []
+        for v in y:
+            a = bf16_part(v)
+            rows += [a, a, bf16_part(v - a)]
+        return rows + list(split3(mass - (0.5 * ALPHA) * (y[0] * y[0] + y[1] * y[1] + y[2] * y[2])))
+
+    def stacked(rows, at):
+        stack = jnp.zeros((16, rows[0].shape[1]), F32)
+        sub = iota(stack.shape, 0)
+        for q, row in enumerate(rows):
+            stack = jnp.where(sub == q, row[at : at + 1, :], stack)
+        return stack.astype(BF16)
+
+    tiles = target_rows([turned[16 + 8 * d : 24 + 8 * d, :] for d in range(3)], turned[40:48, :])
+    rights = [jnp.concatenate([stacked(tiles, 2 * p), stacked(tiles, 2 * p + 1)], axis=1) for p in range(4)]
+    mine = stacked(target_rows([own[d : d + 1, :] for d in range(3)], own[3:4, :]), 0)
+    zero = jnp.zeros((16, TGT), BF16)
+    for ci in range(4):
+
+        def score(right):
+            placed = jnp.concatenate([right if k == ci else zero for k in range(4)], axis=0)
+            return jnp.dot(left, placed, preferred_element_type=F32)
+
+        peak = None
+        for p, right in enumerate(rights):
+            v = score(right)
+            scores[p] = v
+            peak = v if peak is None else jnp.maximum(peak, v)
+        terms[128 * ci : 128 * ci + 128, :] = score(mine)
+        peak = jnp.max(jnp.maximum(peak[:, :128], peak[:, 128:]), axis=1, keepdims=True)
+        total = jnp.exp2(scores[0] - peak)
+        for p in range(1, 4):
+            total = total + jnp.exp2(scores[p] - peak)
+        total = jnp.sum(total[:, :128] + total[:, 128:], axis=1, keepdims=True)
+        terms[128 * ci : 128 * ci + 128, :] += table[:, 12 + ci : 13 + ci] - (peak + jnp.log2(total))
     top_g = jnp.full((8, TGT), NEG, F32)
-    for ci in range(4):
-        for i in range(0, 128, step):
-            x = [jnp.broadcast_to(ALPHA * got[i : i + step, 4 * d + ci : 4 * d + ci + 1], (step, 128)) for d in range(3)]
-            peak = None
-            for li, y in enumerate(tgt):
-                v = (y[3] + x[0] * y[0]) + (x[1] * y[1] + x[2] * y[2])
-                scores[li] = v
-                peak = v if peak is None else jnp.maximum(peak, v)
-            peak = jnp.max(peak, axis=1, keepdims=True)
-            total = jnp.exp2(scores[0] - peak)
-            for li in range(1, 8):
-                total = total + jnp.exp2(scores[li] - peak)
-            total = jnp.sum(total, axis=1, keepdims=True)
-            const = got[i : i + step, 12 + ci : 13 + ci] - (peak + jnp.log2(total))
-            const = jnp.broadcast_to(const, (step, 128))
-            for h in (0, 128):
-                y = [row[:, h : h + 128] for row in mine]
-                v = (const + x[0] * y[0]) + (x[1] * y[1] + x[2] * y[2])
-                terms[128 * ci + i : 128 * ci + i + step, h : h + 128] = v
     for i in range(0, 512, 8):
         top_g = jnp.maximum(top_g, terms[i : i + 8, :])
     top = jnp.max(top_g, axis=0, keepdims=True)
     total = jnp.zeros((8, TGT), F32)
     for i in range(0, 512, 8):
         total = total + jnp.exp2(terms[i : i + 8, :] - top)
-    g = (mine[3] - own[3:4, :]) + top + jnp.log2(jnp.sum(total, axis=0, keepdims=True))
-    g = -g
+    g = own[3:4, :] - top - jnp.log2(jnp.sum(total, axis=0, keepdims=True))
     g_out[...] = jnp.broadcast_to(g, g_out.shape)
     at = l_in[...]
     lane = iota((128, 128), 1).astype(F32)
@@ -317,12 +337,12 @@
         out_shape=(shape((8, 256), F32), shape((CL, PTS), F32)),
         in_specs=[VMEM] * 4,
         out_specs=(VMEM, VMEM),
-        scratch_shapes=[pltpu.VMEM((512, 256), F32), pltpu.VMEM((8, 32, 128), F32)],
+        scratch_shapes=[pltpu.VMEM((512, 256), F32), pltpu.VMEM((4, 128, 256), F32)],
         compiler_params=params,
         name="coarse",
     )(got, own, r, where)
     parts = [part] + [
-        lax.ppermute(part, "tgt", [(i, (i + k) % 4) for i in range(4)]) for k in (1, 2, 3)
+        lax.ppermute(part, "tgt", [(i, (i + k) % 4) for i in range(4)]) for k in (1, 3, 2)
     ]
     fine_f, sums = pl.pallas_call(
         column_kernel,

time: 55 us -> 54.7 us (level)
  waiting for transfers between devices: 7.78 us -> 6.98 us
  starting transfers between devices: 13.7 us -> 14.3 us
    pallas_call x1, Pallas kernels: 2.51 us -> 1.51 us  [on_device(): pl.pallas_call(coarse_kernel, out_shape=(shape((8, 256), F32), shape((CL,...]
    ppermute x3, starting transfers between devices: 2.18 us -> 2.8 us  [on_device(): lax.ppermute(part, 'tgt', [(i, (i + k) % 4) for i in range(4)])]
  transfers between devices with their start and end apart: 4 -> 4, of which waited for: 4 -> 3; matrix products, arithmetic and copies ran while one was open for 0% -> 0% of each run, Pallas kernels for 10% -> 11%
where the time goes in v4:
time: 54.7 us; the launch traced here: 54.1 us
  blocking collectives  15.8 us (29%)
  Pallas kernels  15.6 us (29%)
  starting transfers between devices  14.3 us (26%)
  waiting for transfers between devices  6.98 us (13%)
  between operations  0.73 us (1%)
  local copies, waits for them, and re-layouts  0.67 us (1%)
    all_to_all x1, blocking collectives, on_device(): lax.all_to_all(sums, 'src', split_axis=0, concat_axis=0, tiled=True)  15.8 us
    all_to_all x1, starting transfers between devices, on_device(): lax.all_to_all(row, ('src', 'tgt'), split_axis=0, concat_axis=0, tiled=True)  11.5 us
    pallas_call x1, Pallas kernels, on_device(): pl.pallas_call(row_kernel, out_shape=(shape((BLOCKS, PTS), F32), shape((1...  6.05 us
    pallas_call x1, Pallas kernels, on_device(): pl.pallas_call(column_kernel, out_shape=(shape((CL, PTS), F32), shape((32...  5.13 us
    ppermute x3, waiting for transfers between devices, on_device(): lax.ppermute(part, 'tgt', [(i, (i + k) % 4) for i in range(4)])  3.8 us
    all_to_all x1, waiting for transfers between devices, on_device(): lax.all_to_all(row, ('src', 'tgt'), split_axis=0, concat_axis=0, tiled=True)  3.19 us
    ppermute x3, starting transfers between devices, on_device(): lax.ppermute(part, 'tgt', [(i, (i + k) % 4) for i in range(4)])  2.8 us
    pallas_call x1, Pallas kernels, on_device(): pl.pallas_call(centroid_kernel, out_shape=(shape((128, 128), F32), shape(...  2.26 us
  transfers between devices with their start and end apart: 4, of which 3 were waited for; matrix products, arithmetic and copies ran while one was open for 0% of the time, Pallas kernels for 11%

profile of v4, /device:TPU:1, one launch (start us, length us, event | category | flops | bytes accessed | tf_op | source)
XLA Modules:
  0.0 54.1 jit_solution(6287021488887289989)
XLA Ops:
  0.6 0.0 copy-start
  0.6 0.0 copy-start.1
  0.7 2.3 %centroids.1 = (f32[128,128]{1,0:T(8,128)}, f32[8,256]{1,0:T(8,128)}, f32[8,256]{1,0:T(8,128)}, s32[160]{0:T(256)}) custom-call(s32[8,16]{1,0:T(8,128)} %bitcast.10, s32[1,16]{1,0:T(1,128)} %bitcast.11, f32[3,16,256]{2,1,0:T(8,128)} %sp.5, f32[16,256]{1,0:T(8,128)} %sm.3, f32[3,256,256]{2,1,0:T(8,128)} %tp.5, f32[256,256]{1,0:T(8,128)} %tm.5), custom_call_target="tpu_custom_call" | custom-call | tf_op jit(solution)/shard_map/centroids/pallas_call | solution.py:310
  2.9 0.0 copy-start.2
  2.9 11.5 %all-to-all-start = ((f32[128,1,128]{2,1,0:T(1,128)}), f32[128,1,128]{2,1,0:T(1,128)S(1)}, u32[]{:S(2)}, u32[]{:S(2)}) async-start(f32[128,1,128]{2,1,0:T(1,128)} %bitcast.9), calls=%async_computation | async-start | bytes 131072 | tf_op jit(solution)/shard_map/all_to_all | solution.py:317
  14.4 0.0 copy-start.6
  14.4 0.0 copy-done
  14.5 0.0 copy-done.1
  14.5 0.0 copy-done.2
  14.5 0.6 %copy-done.6 = s32[160]{0:T(256)S(1)} copy-done((s32[160]{0:T(256)S(1)}, s32[160]{0:T(256)}, u32[]{:S(2)}) %copy-start.6) | copy-done | bytes 664
  15.1 0.0 copy-start.5
  15.1 6.0 %rows.1 = (f32[128,256]{1,0:T(8,128)S(1)}, f32[128,128]{1,0:T(8,128)S(1)}) custom-call(s32[160]{0:T(256)S(1)} %copy-done.6, f32[3,16,256]{2,1,0:T(8,128)S(1)} %copy-done.2, f32[3,256,256]{2,1,0:T(8,128)S(1)} %copy-done, f32[256,256]{1,0:T(8,128)S(1)} %copy-done.1), custom_call_target="tpu_custom_call" | custom-call | flops 100000000 | bytes 10000000 | tf_op jit(solution)/shard_map/rows/pallas_call | solution.py:318
  21.2 3.2 %all-to-all-done = f32[128,1,128]{2,1,0:T(1,128)S(1)} async-done(((f32[128,1,128]{2,1,0:T(1,128)}), f32[128,1,128]{2,1,0:T(1,128)S(1)}, u32[]{:S(2)}, u32[]{:S(2)}) %all-to-all-start) | async-done | bytes 65568 | tf_op jit(solution)/shard_map/all_to_all | solution.py:317
  24.4 0.0 copy-done.5
  24.4 0.0 copy-start.3
  24.4 1.5 %coarse.1 = (f32[8,256]{1,0:T(8,128)S(1)}, f32[16,256]{1,0:T(8,128)S(1)}) custom-call(f32[128,128]{1,0:T(8,128)S(1)} %bitcast.8, f32[8,256]{1,0:T(8,128)S(1)} %copy-done.5, f32[128,256]{1,0:T(8,128)S(1)} %get-tuple-element.15.r_in, f32[128,128]{1,0:T(8,128)S(1)} %get-tuple-element.16.l_in), custom_call_target="tpu_custom_call" | custom-call | tf_op jit(solution)/shard_map/coarse/pallas_call | solution.py:335
  25.9 0.7 %collective-permute-start.2 = (f32[16,256]{1,0:T(8,128)S(1)}, f32[16,256]{1,0:T(8,128)S(1)}, u32[]{:S(2)}, u32[]{:S(2)}) collective-permute-start(f32[16,256]{1,0:T(8,128)S(1)} %get-tuple-element.18.l0), channel_id=1, source_target_pairs={{0,2},{1,3},{2,0},{3,1},{4,6},{5,7},{6,4},{7,5},{8,10},{9,11},{10,... | collective-permute-start | bytes 49160 | tf_op jit(solution)/shard_map/ppermute | solution.py:345
  26.6 2.0 %collective-permute-start.1 = (f32[16,256]{1,0:T(8,128)S(1)}, f32[16,256]{1,0:T(8,128)S(1)}, u32[]{:S(2)}, u32[]{:S(2)}) collective-permute-start(f32[16,256]{1,0:T(8,128)S(1)} %get-tuple-element.18.l0), channel_id=1, source_target_pairs={{0,3},{1,0},{2,1},{3,2},{4,7},{5,4},{6,5},{7,6},{8,11},{9,8},{10,9... | collective-permute-start | bytes 49160 | tf_op jit(solution)/shard_map/ppermute | solution.py:345
  28.7 0.0 collective-permute-start
  28.7 1.4 %collective-permute-done.2.l3 = f32[16,256]{1,0:T(8,128)S(1)} collective-permute-done((f32[16,256]{1,0:T(8,128)S(1)}, f32[16,256]{1,0:T(8,128)S(1)}, u32[]{:S(2)}, u32[]{:S(2)}) %collective-permute-start.2) | collective-permute-done | bytes 16416 | tf_op jit(solution)/shard_map/ppermute | solution.py:345
  30.1 0.0 collective-permute-done.1.l2
  30.1 2.4 %collective-permute-done.l1 = f32[16,256]{1,0:T(8,128)S(1)} collective-permute-done((f32[16,256]{1,0:T(8,128)S(1)}, f32[16,256]{1,0:T(8,128)S(1)}, u32[]{:S(2)}, u32[]{:S(2)}) %collective-permute-start) | collective-permute-done | bytes 16416 | tf_op jit(solution)/shard_map/ppermute | solution.py:345
  32.5 0.0 copy-done.3
  32.5 5.1 %columns.1 = (f32[16,256]{1,0:T(8,128)}, f32[32,8,256]{2,1,0:T(8,128)S(1)}) custom-call(s32[160]{0:T(256)S(1)} %copy-done.6, f32[8,256]{1,0:T(8,128)S(1)} %get-tuple-element.17.g, f32[3,16,256]{2,1,0:T(8,128)S(1)} %copy-done.2, f32[16,256]{1,0:T(8,128)S(1)} %copy-done.3, f32[3,256,256]{2,1,0:T(8,128)S(1)} %copy-done, f32[256,256]{1,0:T(8,128)S(1)} %copy-done.1, ...), custom_call_target="tpu_custom_call" | custom-call | tf_op jit(solution)/shard_map/columns/pallas_call | solution.py:347
  37.6 0.0 copy-start.4
  37.6 15.8 %all_to_all.16.arrived = f32[32,8,256]{2,1,0:T(8,128)S(1)} all-to-all(f32[32,8,256]{2,1,0:T(8,128)S(1)} %get-tuple-element.20), channel_id=1, replica_groups=mesh['src'=32,'tgt'=4] {'src'}, dimensions={0} | all-to-all | bytes 524288 | tf_op jit(solution)/shard_map/all_to_all | solution.py:363
  53.5 0.0 copy-done.4
  53.5 0.6 %final.1 = f32[8,256]{1,0:T(8,128)} custom-call(f32[32,8,256]{2,1,0:T(8,128)S(1)} %all_to_all.16.arrived, f32[8,256]{1,0:T(8,128)S(1)} %copy-done.4, f32[8,256]{1,0:T(8,128)S(1)} %get-tuple-element.17.g), custom_call_target="tpu_custom_call" | custom-call | tf_op jit(solution)/shard_map/final/pallas_call | solution.py:364
Async XLA Ops:
  0.6 13.8 %copy-start = (f32[3,256,256]{2,1,0:T(8,128)S(1)}, f32[3,256,256]{2,1,0:T(8,128)}, u32[]{:S(2)}) copy-start(f32[3,256,256]{2,1,0:T(8,128)} %tp.5) | copy-start | bytes 2359300
  0.6 13.8 %copy-start.1 = (f32[256,256]{1,0:T(8,128)S(1)}, f32[256,256]{1,0:T(8,128)}, u32[]{:S(2)}) copy-start(f32[256,256]{1,0:T(8,128)} %tm.5) | copy-start | bytes 786436
  2.9 11.5 %copy-start.2 = (f32[3,16,256]{2,1,0:T(8,128)S(1)}, f32[3,16,256]{2,1,0:T(8,128)}, u32[]{:S(2)}) copy-start(f32[3,16,256]{2,1,0:T(8,128)} %sp.5) | copy-start | bytes 147460
  2.9 21.4 %all-to-all-start = ((f32[128,1,128]{2,1,0:T(1,128)}), f32[128,1,128]{2,1,0:T(1,128)S(1)}, u32[]{:S(2)}, u32[]{:S(2)}) async-start(f32[128,1,128]{2,1,0:T(1,128)} %bitcast.9), calls=%async_computation | async-start | bytes 131072 | tf_op jit(solution)/shard_map/all_to_all | solution.py:317
  14.4 0.7 %copy-start.6 = (s32[160]{0:T(256)S(1)}, s32[160]{0:T(256)}, u32[]{:S(2)}) copy-start(s32[160]{0:T(256)} %get-tuple-element.12.order) | copy-start | bytes 1924
  15.1 9.2 %copy-start.5 = (f32[8,256]{1,0:T(8,128)S(1)}, f32[8,256]{1,0:T(8,128)}, u32[]{:S(2)}) copy-start(f32[8,256]{1,0:T(8,128)} %get-tuple-element.14.own) | copy-start | bytes 24580
  24.4 8.1 %copy-start.3 = (f32[16,256]{1,0:T(8,128)S(1)}, f32[16,256]{1,0:T(8,128)}, u32[]{:S(2)}) copy-start(f32[16,256]{1,0:T(8,128)} %sm.3) | copy-start | bytes 49156
  25.9 4.2 %collective-permute-start.2 = (f32[16,256]{1,0:T(8,128)S(1)}, f32[16,256]{1,0:T(8,128)S(1)}, u32[]{:S(2)}, u32[]{:S(2)}) collective-permute-start(f32[16,256]{1,0:T(8,128)S(1)} %get-tuple-element.18.l0), channel_id=1, source_target_pairs={{0,2},{1,3},{2,0},{3,1},{4,6},{5,7},{6,4},{7,5},{8,10},{9,11},{10,... | collective-permute-start | bytes 49160 | tf_op jit(solution)/shard_map/ppermute | solution.py:345
  26.6 3.4 %collective-permute-start.1 = (f32[16,256]{1,0:T(8,128)S(1)}, f32[16,256]{1,0:T(8,128)S(1)}, u32[]{:S(2)}, u32[]{:S(2)}) collective-permute-start(f32[16,256]{1,0:T(8,128)S(1)} %get-tuple-element.18.l0), channel_id=1, source_target_pairs={{0,3},{1,0},{2,1},{3,2},{4,7},{5,4},{6,5},{7,6},{8,11},{9,8},{10,9... | collective-permute-start | bytes 49160 | tf_op jit(solution)/shard_map/ppermute | solution.py:345
  28.7 3.8 %collective-permute-start = (f32[16,256]{1,0:T(8,128)S(1)}, f32[16,256]{1,0:T(8,128)S(1)}, u32[]{:S(2)}, u32[]{:S(2)}) collective-permute-start(f32[16,256]{1,0:T(8,128)S(1)} %get-tuple-element.18.l0), channel_id=1, source_target_pairs={{0,1},{1,2},{2,3},{3,0},{4,5},{5,6},{6,7},{7,4},{8,9},{9,10},{10,1... | collective-permute-start | bytes 49160 | tf_op jit(solution)/shard_map/ppermute | solution.py:345
  37.6 15.8 %copy-start.4 = (f32[8,256]{1,0:T(8,128)S(1)}, f32[8,256]{1,0:T(8,128)}, u32[]{:S(2)}) copy-start(f32[8,256]{1,0:T(8,128)} %get-tuple-element.21.mass) | copy-start | bytes 24580

commit v5 on v4

--- a/solution.py
+++ b/solution.py
@@ -57,7 +57,7 @@
 
 
 def centroid_kernel(listed, live, sp, sm, tp, tm, row_out, own_out, slice_out, order):
-    s, t = lax.axis_index("src"), lax.axis_index("tgt")
+    s = lax.axis_index("src")
     fill_order(order, listed, live)
     mass = sm[...]
     total = jnp.sum(mass, axis=1, keepdims=True)
@@ -69,11 +69,10 @@
     for q in range(4):
         z = jnp.where(lane == q, cols[q], z)
     zt = jnp.concatenate([z, jnp.zeros((128 - CL, 128), F32)], axis=0).T
-    lane = iota((1, 128), 1)
-    row = jnp.zeros((1, 128), F32)
-    for q in range(4):
-        piece = pltpu.roll(zt[q : q + 1, :], lax.rem(128 - 4 * t, 128), 1)
-        row = row + pltpu.roll(jnp.where(lane < 4, piece, 0.0), 4 * q, 1)
+    row = zt[0:1, :]
+    for q in range(1, 4):
+        row = row + pltpu.roll(zt[q : q + 1, :], CL * q, 1)
+    row_out[...] = jnp.broadcast_to(row, row_out.shape)
     slice_out[...] = tm[pl.ds(pl.multiple_of(8 * s, 8), 8), :]
     weight = tm[...]
     total = jnp.sum(weight, axis=0, keepdims=True)
@@ -82,10 +81,6 @@
     rows.append(jnp.log2(total))
     for q in range(4):
         own_out[q : q + 1, :] = rows[q]
-        half = jnp.where(s >= 16, rows[q][:, 128:], rows[q][:, :128])
-        piece = pltpu.roll(half, lax.rem(128 - 8 * lax.rem(s, 16), 128), 1)
-        row = row + pltpu.roll(jnp.where(lane < 8, piece, 0.0), 16 + 8 * q, 1)
-    row_out[...] = jnp.broadcast_to(row, row_out.shape)
 
 
 def dup(table, r, piece):
@@ -193,62 +188,59 @@
     l_out[...] = lrow[...]
 
 
-def coarse_kernel(got, own, r_in, l_in, g_out, l_out, terms, scores):
+def coarse_kernel(got, own, own1, own2, own3, r_in, l_in, g_out, l_out, terms, scores):
     table = got[...]
-    turned = table.T
+    size = table.shape[0]
     high = bf16_part(ALPHA * table)
     mid = bf16_part(ALPHA * table - high)
-    lane = iota((256, 64), 1)
+    lane = iota((256, 256), 1)
     r = lane & 15
     d = (r >= 3).astype(I32) + (r >= 6).astype(I32)
-    wanted = 4 * d + (lane >> 4) + jnp.where(r - 3 * d == 1, 128, 0)
-    pick = jnp.where((r < 9) & (iota((256, 64), 0) == wanted), 1.0, 0.0).astype(BF16)
-    left = jnp.dot(jnp.concatenate([high, mid], axis=1).astype(BF16), pick, preferred_element_type=F32)
-    r = iota((128, 64), 1) & 15
-    left = jnp.where((r >= 9) & (r < 12), 1.0, left).astype(BF16)
-
-    def target_rows(y, mass):
+    wanted = CL * d + (lane >> 4) + jnp.where(r - 3 * d == 1, 128, 0)
+    pick = jnp.where((r < 9) & (iota((256, 256), 0) == wanted), 1.0, 0.0).astype(BF16)
+    picked = jnp.dot(jnp.concatenate([high, mid], axis=1).astype(BF16), pick, preferred_element_type=F32)
+    r = iota((size, 256), 1) & 15
+    picked = jnp.where((r >= 9) & (r < 12), 1.0, picked)
+
+    def source_side(c):
+        half = picked[:, 128 * (c // 8) : 128 * (c // 8) + 128]
+        return pltpu.roll(half, (128 - 16 * (c % 8)) % 128, 1)[:, :16]
+
+    def target_side(own):
+        y = [own[d : d + 1, :] for d in range(3)]
         rows = []
         for v in y:
             a = bf16_part(v)
             rows += [a, a, bf16_part(v - a)]
-        return rows + list(split3(mass - (0.5 * ALPHA) * (y[0] * y[0] + y[1] * y[1] + y[2] * y[2])))
-
-    def stacked(rows, at):
-        stack = jnp.zeros((16, rows[0].shape[1]), F32)
+        rows += split3(own[3:4, :] - (0.5 * ALPHA) * (y[0] * y[0] + y[1] * y[1] + y[2] * y[2]))
+        stack = jnp.zeros((16, TGT), F32)
         sub = iota(stack.shape, 0)
         for q, row in enumerate(rows):
-            stack = jnp.where(sub == q, row[at : at + 1, :], stack)
+            stack = jnp.where(sub == q, row, stack)
         return stack.astype(BF16)
 
-    tiles = target_rows([turned[16 + 8 * d : 24 + 8 * d, :] for d in range(3)], turned[40:48, :])
-    rights = [jnp.concatenate([stacked(tiles, 2 * p), stacked(tiles, 2 * p + 1)], axis=1) for p in range(4)]
-    mine = stacked(target_rows([own[d : d + 1, :] for d in range(3)], own[3:4, :]), 0)
-    zero = jnp.zeros((16, TGT), BF16)
-    for ci in range(4):
-
-        def score(right):
-            placed = jnp.concatenate([right if k == ci else zero for k in range(4)], axis=0)
-            return jnp.dot(left, placed, preferred_element_type=F32)
-
+    rights = [target_side(table) for table in (own, own1, own2, own3)]
+    many = 4 * size
+    for k in range(4):
+        left = jnp.concatenate([source_side(4 * k + c) for c in range(4)], axis=0).astype(BF16)
+        mass = jnp.concatenate([table[:, 3 * CL + 4 * k + c : 3 * CL + 4 * k + c + 1] for c in range(4)], axis=0)
         peak = None
         for p, right in enumerate(rights):
-            v = score(right)
-            scores[p] = v
+            v = jnp.dot(left, right, preferred_element_type=F32)
+            scores[4 * k + p] = v
             peak = v if peak is None else jnp.maximum(peak, v)
-        terms[128 * ci : 128 * ci + 128, :] = score(mine)
         peak = jnp.max(jnp.maximum(peak[:, :128], peak[:, 128:]), axis=1, keepdims=True)
-        total = jnp.exp2(scores[0] - peak)
+        total = jnp.exp2(scores[4 * k] - peak)
         for p in range(1, 4):
-            total = total + jnp.exp2(scores[p] - peak)
+            total = total + jnp.exp2(scores[4 * k + p] - peak)
         total = jnp.sum(total[:, :128] + total[:, 128:], axis=1, keepdims=True)
-        terms[128 * ci : 128 * ci + 128, :] += table[:, 12 + ci : 13 + ci] - (peak + jnp.log2(total))
+        terms[many * k : many * (k + 1), :] = scores[4 * k] + (mass - (peak + jnp.log2(total)))
     top_g = jnp.full((8, TGT), NEG, F32)
-    for i in range(0, 512, 8):
+    for i in range(0, 4 * many, 8):
         top_g = jnp.maximum(top_g, terms[i : i + 8, :])
     top = jnp.max(top_g, axis=0, keepdims=True)
     total = jnp.zeros((8, TGT), F32)
-    for i in range(0, 512, 8):
+    for i in range(0, 4 * many, 8):
         total = total + jnp.exp2(terms[i : i + 8, :] - top)
     g = own[3:4, :] - top - jnp.log2(jnp.sum(total, axis=0, keepdims=True))
     g_out[...] = jnp.broadcast_to(g, g_out.shape)
@@ -301,7 +293,11 @@
     out[...] = (g[...] - jnp.log2(1.0 + total / mass[...])) * UNSCALE
 
 
-def on_device(src_pts, src_mass, tgt_pts, tgt_mass, listed, live):
+def over_tgt(part):
+    return [part] + [lax.ppermute(part, "tgt", [(i, (i + k) % 4) for i in range(4)]) for k in (1, 2, 3)]
+
+
+def program(src_pts, src_mass, tgt_pts, tgt_mass, listed, live):
     shape = jax.ShapeDtypeStruct
     params = pltpu.CompilerParams(vmem_limit_bytes=LIMIT)
     stages = [pltpu.VMEM((TGT, 16), BF16), pltpu.VMEM((16, PTS), BF16)] * BATCH
@@ -309,12 +305,13 @@
     counts = live.transpose(1, 0)
     row, own, mass, order = pl.pallas_call(
         centroid_kernel,
-        out_shape=(shape((128, 128), F32), shape((8, 256), F32), shape((8, 256), F32), shape((LIST,), I32)),
+        out_shape=(shape((32, 128), F32), shape((8, 256), F32), shape((8, 256), F32), shape((LIST,), I32)),
         in_specs=[SMEM, SMEM] + [VMEM] * 4,
         out_specs=(VMEM, VMEM, VMEM, SMEM),
         name="centroids",
     )(slots, counts, src_pts, src_mass, tgt_pts, tgt_mass)
-    got = lax.all_to_all(row, ("src", "tgt"), split_axis=0, concat_axis=0, tiled=True)
+    owns = over_tgt(own)
+    got = lax.all_to_all(row, "src", split_axis=0, concat_axis=0, tiled=True)
     r, where = pl.pallas_call(
         row_kernel,
         out_shape=(shape((BLOCKS, PTS), F32), shape((128, 128), F32)),
@@ -335,15 +332,13 @@
     g, part = pl.pallas_call(
         coarse_kernel,
         out_shape=(shape((8, 256), F32), shape((CL, PTS), F32)),
-        in_specs=[VMEM] * 4,
+        in_specs=[VMEM] * 7,
         out_specs=(VMEM, VMEM),
-        scratch_shapes=[pltpu.VMEM((512, 256), F32), pltpu.VMEM((4, 128, 256), F32)],
+        scratch_shapes=[pltpu.VMEM((512, 256), F32), pltpu.VMEM((16, 128, 256), F32)],
         compiler_params=params,
         name="coarse",
-    )(got, own, r, where)
-    parts = [part] + [
-        lax.ppermute(part, "tgt", [(i, (i + k) % 4) for i in range(4)]) for k in (1, 3, 2)
-    ]
+    )(got, *owns, r, where)
+    parts = over_tgt(part)
     fine_f, sums = pl.pallas_call(
         column_kernel,
         out_shape=(shape((CL, PTS), F32), shape((32, 8, TGT), F32)),
@@ -382,7 +377,7 @@
         P("src", "tgt"),
     )
     return jax.shard_map(
-        on_device,
+        program,
         mesh=mesh,
         in_specs=placed,
         out_specs=(P("src", None), P("src", "tgt")),

time: 54.7 us -> 55.8 us (1.020)
  blocking collectives: 15.8 us -> 18.8 us
  waiting for transfers between devices: 6.98 us -> 4.1 us
  starting transfers between devices: 14.3 us -> 16.7 us
  local copies, waits for them, and re-layouts: 0.67 us -> 0.03 us
    ppermute x3 -> x6, starting transfers between devices: 2.8 us -> 7.31 us  [over_tgt(): lax.ppermute(part, 'tgt', [(i, (i + k) % 4) for i in range(4)])]
    all_to_all x1, waiting for transfers between devices: 3.19 us -> 0.01 us  [program(): got = lax.all_to_all(row, 'src', split_axis=0, concat_axis=0, tiled=True)]
    all_to_all x1, blocking collectives: 15.8 us -> 18.8 us  [program(): lax.all_to_all(sums, 'src', split_axis=0, concat_axis=0, tiled=True)]
    all_to_all x1, starting transfers between devices: 11.5 us -> 9.43 us  [program(): got = lax.all_to_all(row, 'src', split_axis=0, concat_axis=0, tiled=True)]
    unnamed x14, local copies, waits for them, and re-layouts: 0.67 us -> 0.03 us
    ppermute x3 -> x6, waiting for transfers between devices: 3.8 us -> 4.1 us  [over_tgt(): lax.ppermute(part, 'tgt', [(i, (i + k) % 4) for i in range(4)])]
  transfers between devices with their start and end apart: 4 -> 7, of which waited for: 3 -> 2; matrix products, arithmetic and copies ran while one was open for 0% -> 0% of each run, Pallas kernels for 11% -> 11%
where the time goes in v5:
time: 55.8 us; the launch traced here: 55.5 us
  blocking collectives  18.8 us (34%)
  starting transfers between devices  16.7 us (30%)
  Pallas kernels  15.1 us (27%)
  waiting for transfers between devices  4.1 us (7%)
  between operations  0.77 us (1%)
    all_to_all x1, blocking collectives, program(): lax.all_to_all(sums, 'src', split_axis=0, concat_axis=0, tiled=True)  18.8 us
    all_to_all x1, starting transfers between devices, program(): got = lax.all_to_all(row, 'src', split_axis=0, concat_axis=0, tiled=True)  9.43 us
    ppermute x6, starting transfers between devices, over_tgt(): lax.ppermute(part, 'tgt', [(i, (i + k) % 4) for i in range(4)])  7.31 us
    pallas_call x1, Pallas kernels, program(): pl.pallas_call(row_kernel, out_shape=(shape((BLOCKS, PTS), F32), shape((1...  6.06 us
    pallas_call x1, Pallas kernels, program(): pl.pallas_call(column_kernel, out_shape=(shape((CL, PTS), F32), shape((32...  4.82 us
    ppermute x6, waiting for transfers between devices, over_tgt(): lax.ppermute(part, 'tgt', [(i, (i + k) % 4) for i in range(4)])  4.1 us
    pallas_call x1, Pallas kernels, program(): pl.pallas_call(centroid_kernel, out_shape=(shape((32, 128), F32), shape((...  2.19 us
    pallas_call x1, Pallas kernels, program(): pl.pallas_call(coarse_kernel, out_shape=(shape((8, 256), F32), shape((CL,...  1.34 us
  transfers between devices with their start and end apart: 7, of which 2 were waited for; matrix products, arithmetic and copies ran while one was open for 0% of the time, Pallas kernels for 11%

profile of v5, /device:TPU:1, one launch (start us, length us, event | category | flops | bytes accessed | tf_op | source)
XLA Modules:
  0.0 55.5 jit_solution(2963647581541176274)
XLA Ops:
  0.6 0.0 copy-start
  0.6 0.0 copy-start.1
  0.7 0.0 copy-start.2
  0.7 2.2 %centroids.1 = (f32[32,128]{1,0:T(8,128)}, f32[8,256]{1,0:T(8,128)}, f32[8,256]{1,0:T(8,128)}, s32[160]{0:T(256)}) custom-call(s32[8,16]{1,0:T(8,128)} %bitcast.10, s32[1,16]{1,0:T(1,128)} %bitcast.11, f32[3,16,256]{2,1,0:T(8,128)} %sp.5, f32[16,256]{1,0:T(8,128)} %sm.3, f32[3,256,256]{2,1,0:T(8,128)} %tp.5, f32[256,256]{1,0:T(8,128)} %tm.5), custom_call_target="tpu_custom_call" | custom-call | tf_op jit(solution)/shard_map/centroids/pallas_call | solution.py:306
  2.9 0.0 copy-start.5
  2.9 9.4 %all-to-all-start = ((f32[32,1,128]{2,1,0:T(1,128)}), f32[32,1,128]{2,1,0:T(1,128)S(1)}, u32[]{:S(2)}, u32[]{:S(2)}) async-start(f32[32,1,128]{2,1,0:T(1,128)} %bitcast.9), calls=%async_computation | async-start | bytes 32768 | tf_op jit(solution)/shard_map/all_to_all | solution.py:314
  12.3 0.0 copy-done.5
  12.3 0.0 copy-start.6
  12.3 2.8 %collective-permute-start.2 = (f32[8,256]{1,0:T(8,128)S(1)}, f32[8,256]{1,0:T(8,128)S(1)}, u32[]{:S(2)}, u32[]{:S(2)}) collective-permute-start(f32[8,256]{1,0:T(8,128)S(1)} %copy-done.5), channel_id=1, source_target_pairs={{0,3},{1,0},{2,1},{3,2},{4,7},{5,4},{6,5},{7,6},{8,11},{9,8},{10,9... | collective-permute-start | bytes 24584 | tf_op jit(solution)/shard_map/ppermute | solution.py:297
  15.1 0.3 collective-permute-start.1
  15.5 0.7 %collective-permute-start = (f32[8,256]{1,0:T(8,128)S(1)}, f32[8,256]{1,0:T(8,128)S(1)}, u32[]{:S(2)}, u32[]{:S(2)}) collective-permute-start(f32[8,256]{1,0:T(8,128)S(1)} %copy-done.5), channel_id=1, source_target_pairs={{0,1},{1,2},{2,3},{3,0},{4,5},{5,6},{6,7},{7,4},{8,9},{9,10},{10,1... | collective-permute-start | bytes 24584 | tf_op jit(solution)/shard_map/ppermute | solution.py:297
  16.2 0.0 copy-done
  16.2 0.0 copy-done.1
  16.2 0.0 copy-done.2
  16.2 0.0 copy-done.6
  16.2 6.1 %rows.1 = (f32[128,256]{1,0:T(8,128)S(1)}, f32[128,128]{1,0:T(8,128)S(1)}) custom-call(s32[160]{0:T(256)S(1)} %copy-done.6, f32[3,16,256]{2,1,0:T(8,128)S(1)} %copy-done.2, f32[3,256,256]{2,1,0:T(8,128)S(1)} %copy-done, f32[256,256]{1,0:T(8,128)S(1)} %copy-done.1), custom_call_target="tpu_custom_call" | custom-call | flops 100000000 | bytes 10000000 | tf_op jit(solution)/shard_map/rows/pallas_call | solution.py:315
  22.2 0.0 collective-permute-done.2.own3
  22.3 0.0 collective-permute-done.1.own2
  22.3 0.0 collective-permute-done.own1
  22.3 0.0 all-to-all-done
  22.3 0.0 copy-start.3
  22.3 1.3 %coarse.1 = (f32[8,256]{1,0:T(8,128)S(1)}, f32[16,256]{1,0:T(8,128)S(1)}) custom-call(f32[32,128]{1,0:T(8,128)S(1)} %bitcast.8, f32[8,256]{1,0:T(8,128)S(1)} %copy-done.5, f32[8,256]{1,0:T(8,128)S(1)} %collective-permute-done.own1, f32[8,256]{1,0:T(8,128)S(1)} %collective-permute-done.1.own2, f32[8,256]{1,0:T(8,128)S(1)} %collective-permute-done.2.own3, ...), custom_call_target="tpu_custom_call" | custom-call | tf_op jit(solution)/shard_map/coarse/pallas_call | solution.py:332
  23.6 2.1 %collective-permute-start.5 = (f32[16,256]{1,0:T(8,128)S(1)}, f32[16,256]{1,0:T(8,128)S(1)}, u32[]{:S(2)}, u32[]{:S(2)}) collective-permute-start(f32[16,256]{1,0:T(8,128)S(1)} %get-tuple-element.18.l0), channel_id=1, source_target_pairs={{0,3},{1,0},{2,1},{3,2},{4,7},{5,4},{6,5},{7,6},{8,11},{9,8},{10,9... | collective-permute-start | bytes 49160 | tf_op jit(solution)/shard_map/ppermute | solution.py:297
  25.7 1.4 %collective-permute-start.4 = (f32[16,256]{1,0:T(8,128)S(1)}, f32[16,256]{1,0:T(8,128)S(1)}, u32[]{:S(2)}, u32[]{:S(2)}) collective-permute-start(f32[16,256]{1,0:T(8,128)S(1)} %get-tuple-element.18.l0), channel_id=1, source_target_pairs={{0,2},{1,3},{2,0},{3,1},{4,6},{5,7},{6,4},{7,5},{8,10},{9,11},{10,... | collective-permute-start | bytes 49160 | tf_op jit(solution)/shard_map/ppermute | solution.py:297
  27.1 0.0 collective-permute-start.3
  27.1 0.0 collective-permute-done.5.l3
  27.1 2.7 %collective-permute-done.4.l2 = f32[16,256]{1,0:T(8,128)S(1)} collective-permute-done((f32[16,256]{1,0:T(8,128)S(1)}, f32[16,256]{1,0:T(8,128)S(1)}, u32[]{:S(2)}, u32[]{:S(2)}) %collective-permute-start.4) | collective-permute-done | bytes 16416 | tf_op jit(solution)/shard_map/ppermute | solution.py:297
  29.8 1.4 %collective-permute-done.3.l1 = f32[16,256]{1,0:T(8,128)S(1)} collective-permute-done((f32[16,256]{1,0:T(8,128)S(1)}, f32[16,256]{1,0:T(8,128)S(1)}, u32[]{:S(2)}, u32[]{:S(2)}) %collective-permute-start.3) | collective-permute-done | bytes 16416 | tf_op jit(solution)/shard_map/ppermute | solution.py:297
  31.2 0.0 copy-done.3
  31.2 4.8 %columns.1 = (f32[16,256]{1,0:T(8,128)}, f32[32,8,256]{2,1,0:T(8,128)S(1)}) custom-call(s32[160]{0:T(256)S(1)} %copy-done.6, f32[8,256]{1,0:T(8,128)S(1)} %get-tuple-element.17.g, f32[3,16,256]{2,1,0:T(8,128)S(1)} %copy-done.2, f32[16,256]{1,0:T(8,128)S(1)} %copy-done.3, f32[3,256,256]{2,1,0:T(8,128)S(1)} %copy-done, f32[256,256]{1,0:T(8,128)S(1)} %copy-done.1, ...), custom_call_target="tpu_custom_call" | custom-call | tf_op jit(solution)/shard_map/columns/pallas_call | solution.py:342
  36.0 0.0 copy-start.4
  36.0 18.8 %all_to_all.16.arrived = f32[32,8,256]{2,1,0:T(8,128)S(1)} all-to-all(f32[32,8,256]{2,1,0:T(8,128)S(1)} %get-tuple-element.20), channel_id=1, replica_groups=mesh['src'=32,'tgt'=4] {'src'}, dimensions={0} | all-to-all | bytes 524288 | tf_op jit(solution)/shard_map/all_to_all | solution.py:358
  54.9 0.0 copy-done.4
  54.9 0.6 %final.1 = f32[8,256]{1,0:T(8,128)} custom-call(f32[32,8,256]{2,1,0:T(8,128)S(1)} %all_to_all.16.arrived, f32[8,256]{1,0:T(8,128)S(1)} %copy-done.4, f32[8,256]{1,0:T(8,128)S(1)} %get-tuple-element.17.g), custom_call_target="tpu_custom_call" | custom-call | tf_op jit(solution)/shard_map/final/pallas_call | solution.py:359
Async XLA Ops:
  0.6 15.5 %copy-start = (f32[3,256,256]{2,1,0:T(8,128)S(1)}, f32[3,256,256]{2,1,0:T(8,128)}, u32[]{:S(2)}) copy-start(f32[3,256,256]{2,1,0:T(8,128)} %tp.5) | copy-start | bytes 2359300
  0.6 15.5 %copy-start.1 = (f32[256,256]{1,0:T(8,128)S(1)}, f32[256,256]{1,0:T(8,128)}, u32[]{:S(2)}) copy-start(f32[256,256]{1,0:T(8,128)} %tm.5) | copy-start | bytes 786436
  0.7 15.5 %copy-start.2 = (f32[3,16,256]{2,1,0:T(8,128)S(1)}, f32[3,16,256]{2,1,0:T(8,128)}, u32[]{:S(2)}) copy-start(f32[3,16,256]{2,1,0:T(8,128)} %sp.5) | copy-start | bytes 147460
  2.9 9.5 %copy-start.5 = (f32[8,256]{1,0:T(8,128)S(1)}, f32[8,256]{1,0:T(8,128)}, u32[]{:S(2)}) copy-start(f32[8,256]{1,0:T(8,128)} %get-tuple-element.14.own) | copy-start | bytes 24580
  2.9 19.4 %all-to-all-start = ((f32[32,1,128]{2,1,0:T(1,128)}), f32[32,1,128]{2,1,0:T(1,128)S(1)}, u32[]{:S(2)}, u32[]{:S(2)}) async-start(f32[32,1,128]{2,1,0:T(1,128)} %bitcast.9), calls=%async_computation | async-start | bytes 32768 | tf_op jit(solution)/shard_map/all_to_all | solution.py:314
  12.3 3.9 %copy-start.6 = (s32[160]{0:T(256)S(1)}, s32[160]{0:T(256)}, u32[]{:S(2)}) copy-start(s32[160]{0:T(256)} %get-tuple-element.12.order) | copy-start | bytes 1924
  12.3 9.9 %collective-permute-start.2 = (f32[8,256]{1,0:T(8,128)S(1)}, f32[8,256]{1,0:T(8,128)S(1)}, u32[]{:S(2)}, u32[]{:S(2)}) collective-permute-start(f32[8,256]{1,0:T(8,128)S(1)} %copy-done.5), channel_id=1, source_target_pairs={{0,3},{1,0},{2,1},{3,2},{4,7},{5,4},{6,5},{7,6},{8,11},{9,8},{10,9... | collective-permute-start | bytes 24584 | tf_op jit(solution)/shard_map/ppermute | solution.py:297
  15.1 7.1 %collective-permute-start.1 = (f32[8,256]{1,0:T(8,128)S(1)}, f32[8,256]{1,0:T(8,128)S(1)}, u32[]{:S(2)}, u32[]{:S(2)}) collective-permute-start(f32[8,256]{1,0:T(8,128)S(1)} %copy-done.5), channel_id=1, source_target_pairs={{0,2},{1,3},{2,0},{3,1},{4,6},{5,7},{6,4},{7,5},{8,10},{9,11},{10,... | collective-permute-start | bytes 24584 | tf_op jit(solution)/shard_map/ppermute | solution.py:297
  15.5 6.8 %collective-permute-start = (f32[8,256]{1,0:T(8,128)S(1)}, f32[8,256]{1,0:T(8,128)S(1)}, u32[]{:S(2)}, u32[]{:S(2)}) collective-permute-start(f32[8,256]{1,0:T(8,128)S(1)} %copy-done.5), channel_id=1, source_target_pairs={{0,1},{1,2},{2,3},{3,0},{4,5},{5,6},{6,7},{7,4},{8,9},{9,10},{10,1... | collective-permute-start | bytes 24584 | tf_op jit(solution)/shard_map/ppermute | solution.py:297
  22.3 8.9 %copy-start.3 = (f32[16,256]{1,0:T(8,128)S(1)}, f32[16,256]{1,0:T(8,128)}, u32[]{:S(2)}) copy-start(f32[16,256]{1,0:T(8,128)} %sm.3) | copy-start | bytes 49156
  23.6 3.5 %collective-permute-start.5 = (f32[16,256]{1,0:T(8,128)S(1)}, f32[16,256]{1,0:T(8,128)S(1)}, u32[]{:S(2)}, u32[]{:S(2)}) collective-permute-start(f32[16,256]{1,0:T(8,128)S(1)} %get-tuple-element.18.l0), channel_id=1, source_target_pairs={{0,3},{1,0},{2,1},{3,2},{4,7},{5,4},{6,5},{7,6},{8,11},{9,8},{10,9... | collective-permute-start | bytes 49160 | tf_op jit(solution)/shard_map/ppermute | solution.py:297
  25.7 4.1 %collective-permute-start.4 = (f32[16,256]{1,0:T(8,128)S(1)}, f32[16,256]{1,0:T(8,128)S(1)}, u32[]{:S(2)}, u32[]{:S(2)}) collective-permute-start(f32[16,256]{1,0:T(8,128)S(1)} %get-tuple-element.18.l0), channel_id=1, source_target_pairs={{0,2},{1,3},{2,0},{3,1},{4,6},{5,7},{6,4},{7,5},{8,10},{9,11},{10,... | collective-permute-start | bytes 49160 | tf_op jit(solution)/shard_map/ppermute | solution.py:297
  27.1 4.1 %collective-permute-start.3 = (f32[16,256]{1,0:T(8,128)S(1)}, f32[16,256]{1,0:T(8,128)S(1)}, u32[]{:S(2)}, u32[]{:S(2)}) collective-permute-start(f32[16,256]{1,0:T(8,128)S(1)} %get-tuple-element.18.l0), channel_id=1, source_target_pairs={{0,1},{1,2},{2,3},{3,0},{4,5},{5,6},{6,7},{7,4},{8,9},{9,10},{10,1... | collective-permute-start | bytes 49160 | tf_op jit(solution)/shard_map/ppermute | solution.py:297
  36.0 18.8 %copy-start.4 = (f32[8,256]{1,0:T(8,128)S(1)}, f32[8,256]{1,0:T(8,128)}, u32[]{:S(2)}) copy-start(f32[8,256]{1,0:T(8,128)} %get-tuple-element.21.mass) | copy-start | bytes 24580

commit v6 on v4

--- a/solution.py
+++ b/solution.py
@@ -342,7 +342,7 @@
         name="coarse",
     )(got, own, r, where)
     parts = [part] + [
-        lax.ppermute(part, "tgt", [(i, (i + k) % 4) for i in range(4)]) for k in (1, 3, 2)
+        lax.ppermute(part, "tgt", [(i, (i + k) % 4) for i in range(4)]) for k in (1, 2, 3)
     ]
     fine_f, sums = pl.pallas_call(
         column_kernel,

time: 54.7 us -> 53.9 us (0.985)
  waiting for transfers between devices: 6.98 us -> 7.78 us
  starting transfers between devices: 14.3 us -> 13.7 us
  Pallas kernels: 15.6 us -> 15 us
    ppermute x3, starting transfers between devices: 2.8 us -> 2.18 us  [on_device(): lax.ppermute(part, 'tgt', [(i, (i + k) % 4) for i in range(4)])]
  transfers between devices with their start and end apart: 4 -> 4, of which waited for: 3 -> 4; matrix products, arithmetic and copies ran while one was open for 0% -> 0% of each run, Pallas kernels for 11% -> 10%
where the time goes in v6:
time: 53.9 us; the launch traced here: 53.2 us
  blocking collectives  15.4 us (29%)
  Pallas kernels  15 us (28%)
  starting transfers between devices  13.7 us (25%)
  waiting for transfers between devices  7.78 us (14%)
  between operations  0.73 us (1%)
  local copies, waits for them, and re-layouts  0.67 us (1%)
    all_to_all x1, blocking collectives, on_device(): lax.all_to_all(sums, 'src', split_axis=0, concat_axis=0, tiled=True)  15.4 us
    all_to_all x1, starting transfers between devices, on_device(): lax.all_to_all(row, ('src', 'tgt'), split_axis=0, concat_axis=0, tiled=True)  11.5 us
    pallas_call x1, Pallas kernels, on_device(): pl.pallas_call(row_kernel, out_shape=(shape((BLOCKS, PTS), F32), shape((1...  5.54 us
    pallas_call x1, Pallas kernels, on_device(): pl.pallas_call(column_kernel, out_shape=(shape((CL, PTS), F32), shape((32...  5.01 us
    ppermute x3, waiting for transfers between devices, on_device(): lax.ppermute(part, 'tgt', [(i, (i + k) % 4) for i in range(4)])  4.09 us
    all_to_all x1, waiting for transfers between devices, on_device(): lax.all_to_all(row, ('src', 'tgt'), split_axis=0, concat_axis=0, tiled=True)  3.69 us
    pallas_call x1, Pallas kernels, on_device(): pl.pallas_call(centroid_kernel, out_shape=(shape((128, 128), F32), shape(...  2.26 us
    ppermute x3, starting transfers between devices, on_device(): lax.ppermute(part, 'tgt', [(i, (i + k) % 4) for i in range(4)])  2.18 us
  transfers between devices with their start and end apart: 4, of which 4 were waited for; matrix products, arithmetic and copies ran while one was open for 0% of the time, Pallas kernels for 10%

profile of v6, /device:TPU:1, one launch (start us, length us, event | category | flops | bytes accessed | tf_op | source)
XLA Modules:
  0.0 53.2 jit_solution(3900166059845288451)
XLA Ops:
  0.6 0.0 copy-start
  0.6 0.0 copy-start.1
  0.7 2.3 %centroids.1 = (f32[128,128]{1,0:T(8,128)}, f32[8,256]{1,0:T(8,128)}, f32[8,256]{1,0:T(8,128)}, s32[160]{0:T(256)}) custom-call(s32[8,16]{1,0:T(8,128)} %bitcast.10, s32[1,16]{1,0:T(1,128)} %bitcast.11, f32[3,16,256]{2,1,0:T(8,128)} %sp.5, f32[16,256]{1,0:T(8,128)} %sm.3, f32[3,256,256]{2,1,0:T(8,128)} %tp.5, f32[256,256]{1,0:T(8,128)} %tm.5), custom_call_target="tpu_custom_call" | custom-call | tf_op jit(solution)/shard_map/centroids/pallas_call | solution.py:310
  2.9 0.0 copy-start.2
  2.9 11.5 %all-to-all-start = ((f32[128,1,128]{2,1,0:T(1,128)}), f32[128,1,128]{2,1,0:T(1,128)S(1)}, u32[]{:S(2)}, u32[]{:S(2)}) async-start(f32[128,1,128]{2,1,0:T(1,128)} %bitcast.9), calls=%async_computation | async-start | bytes 131072 | tf_op jit(solution)/shard_map/all_to_all | solution.py:317
  14.4 0.0 copy-start.6
  14.4 0.0 copy-done
  14.5 0.0 copy-done.1
  14.5 0.0 copy-done.2
  14.5 0.6 %copy-done.6 = s32[160]{0:T(256)S(1)} copy-done((s32[160]{0:T(256)S(1)}, s32[160]{0:T(256)}, u32[]{:S(2)}) %copy-start.6) | copy-done | bytes 664
  15.1 0.0 copy-start.5
  15.1 5.5 %rows.1 = (f32[128,256]{1,0:T(8,128)S(1)}, f32[128,128]{1,0:T(8,128)S(1)}) custom-call(s32[160]{0:T(256)S(1)} %copy-done.6, f32[3,16,256]{2,1,0:T(8,128)S(1)} %copy-done.2, f32[3,256,256]{2,1,0:T(8,128)S(1)} %copy-done, f32[256,256]{1,0:T(8,128)S(1)} %copy-done.1), custom_call_target="tpu_custom_call" | custom-call | flops 100000000 | bytes 10000000 | tf_op jit(solution)/shard_map/rows/pallas_call | solution.py:318
  20.7 3.7 %all-to-all-done = f32[128,1,128]{2,1,0:T(1,128)S(1)} async-done(((f32[128,1,128]{2,1,0:T(1,128)}), f32[128,1,128]{2,1,0:T(1,128)S(1)}, u32[]{:S(2)}, u32[]{:S(2)}) %all-to-all-start) | async-done | bytes 65568 | tf_op jit(solution)/shard_map/all_to_all | solution.py:317
  24.4 0.0 copy-done.5
  24.4 0.0 copy-start.3
  24.4 1.5 %coarse.1 = (f32[8,256]{1,0:T(8,128)S(1)}, f32[16,256]{1,0:T(8,128)S(1)}) custom-call(f32[128,128]{1,0:T(8,128)S(1)} %bitcast.8, f32[8,256]{1,0:T(8,128)S(1)} %copy-done.5, f32[128,256]{1,0:T(8,128)S(1)} %get-tuple-element.15.r_in, f32[128,128]{1,0:T(8,128)S(1)} %get-tuple-element.16.l_in), custom_call_target="tpu_custom_call" | custom-call | tf_op jit(solution)/shard_map/coarse/pallas_call | solution.py:335
  25.9 0.9 %collective-permute-start.2 = (f32[16,256]{1,0:T(8,128)S(1)}, f32[16,256]{1,0:T(8,128)S(1)}, u32[]{:S(2)}, u32[]{:S(2)}) collective-permute-start(f32[16,256]{1,0:T(8,128)S(1)} %get-tuple-element.18.l0), channel_id=1, source_target_pairs={{0,3},{1,0},{2,1},{3,2},{4,7},{5,4},{6,5},{7,6},{8,11},{9,8},{10,9... | collective-permute-start | bytes 49160 | tf_op jit(solution)/shard_map/ppermute | solution.py:345
  26.7 1.3 %collective-permute-start.1 = (f32[16,256]{1,0:T(8,128)S(1)}, f32[16,256]{1,0:T(8,128)S(1)}, u32[]{:S(2)}, u32[]{:S(2)}) collective-permute-start(f32[16,256]{1,0:T(8,128)S(1)} %get-tuple-element.18.l0), channel_id=1, source_target_pairs={{0,2},{1,3},{2,0},{3,1},{4,6},{5,7},{6,4},{7,5},{8,10},{9,11},{10,... | collective-permute-start | bytes 49160 | tf_op jit(solution)/shard_map/ppermute | solution.py:345
  28.1 0.0 collective-permute-start
  28.1 0.5 collective-permute-done.2.l3
  28.5 2.3 %collective-permute-done.1.l2 = f32[16,256]{1,0:T(8,128)S(1)} collective-permute-done((f32[16,256]{1,0:T(8,128)S(1)}, f32[16,256]{1,0:T(8,128)S(1)}, u32[]{:S(2)}, u32[]{:S(2)}) %collective-permute-start.1) | collective-permute-done | bytes 16416 | tf_op jit(solution)/shard_map/ppermute | solution.py:345
  30.8 1.3 %collective-permute-done.l1 = f32[16,256]{1,0:T(8,128)S(1)} collective-permute-done((f32[16,256]{1,0:T(8,128)S(1)}, f32[16,256]{1,0:T(8,128)S(1)}, u32[]{:S(2)}, u32[]{:S(2)}) %collective-permute-start) | collective-permute-done | bytes 16416 | tf_op jit(solution)/shard_map/ppermute | solution.py:345
  32.2 0.0 copy-done.3
  32.2 5.0 %columns.1 = (f32[16,256]{1,0:T(8,128)}, f32[32,8,256]{2,1,0:T(8,128)S(1)}) custom-call(s32[160]{0:T(256)S(1)} %copy-done.6, f32[8,256]{1,0:T(8,128)S(1)} %get-tuple-element.17.g, f32[3,16,256]{2,1,0:T(8,128)S(1)} %copy-done.2, f32[16,256]{1,0:T(8,128)S(1)} %copy-done.3, f32[3,256,256]{2,1,0:T(8,128)S(1)} %copy-done, f32[256,256]{1,0:T(8,128)S(1)} %copy-done.1, ...), custom_call_target="tpu_custom_call" | custom-call | tf_op jit(solution)/shard_map/columns/pallas_call | solution.py:347
  37.2 0.0 copy-start.4
  37.2 15.4 %all_to_all.16.arrived = f32[32,8,256]{2,1,0:T(8,128)S(1)} all-to-all(f32[32,8,256]{2,1,0:T(8,128)S(1)} %get-tuple-element.20), channel_id=1, replica_groups=mesh['src'=32,'tgt'=4] {'src'}, dimensions={0} | all-to-all | bytes 524288 | tf_op jit(solution)/shard_map/all_to_all | solution.py:363
  52.6 0.0 copy-done.4
  52.6 0.6 %final.1 = f32[8,256]{1,0:T(8,128)} custom-call(f32[32,8,256]{2,1,0:T(8,128)S(1)} %all_to_all.16.arrived, f32[8,256]{1,0:T(8,128)S(1)} %copy-done.4, f32[8,256]{1,0:T(8,128)S(1)} %get-tuple-element.17.g), custom_call_target="tpu_custom_call" | custom-call | tf_op jit(solution)/shard_map/final/pallas_call | solution.py:364
Async XLA Ops:
  0.6 13.8 %copy-start = (f32[3,256,256]{2,1,0:T(8,128)S(1)}, f32[3,256,256]{2,1,0:T(8,128)}, u32[]{:S(2)}) copy-start(f32[3,256,256]{2,1,0:T(8,128)} %tp.5) | copy-start | bytes 2359300
  0.6 13.8 %copy-start.1 = (f32[256,256]{1,0:T(8,128)S(1)}, f32[256,256]{1,0:T(8,128)}, u32[]{:S(2)}) copy-start(f32[256,256]{1,0:T(8,128)} %tm.5) | copy-start | bytes 786436
  2.9 11.5 %copy-start.2 = (f32[3,16,256]{2,1,0:T(8,128)S(1)}, f32[3,16,256]{2,1,0:T(8,128)}, u32[]{:S(2)}) copy-start(f32[3,16,256]{2,1,0:T(8,128)} %sp.5) | copy-start | bytes 147460
  2.9 21.4 %all-to-all-start = ((f32[128,1,128]{2,1,0:T(1,128)}), f32[128,1,128]{2,1,0:T(1,128)S(1)}, u32[]{:S(2)}, u32[]{:S(2)}) async-start(f32[128,1,128]{2,1,0:T(1,128)} %bitcast.9), calls=%async_computation | async-start | bytes 131072 | tf_op jit(solution)/shard_map/all_to_all | solution.py:317
  14.4 0.7 %copy-start.6 = (s32[160]{0:T(256)S(1)}, s32[160]{0:T(256)}, u32[]{:S(2)}) copy-start(s32[160]{0:T(256)} %get-tuple-element.12.order) | copy-start | bytes 1924
  15.1 9.2 %copy-start.5 = (f32[8,256]{1,0:T(8,128)S(1)}, f32[8,256]{1,0:T(8,128)}, u32[]{:S(2)}) copy-start(f32[8,256]{1,0:T(8,128)} %get-tuple-element.14.own) | copy-start | bytes 24580
  24.4 7.8 %copy-start.3 = (f32[16,256]{1,0:T(8,128)S(1)}, f32[16,256]{1,0:T(8,128)}, u32[]{:S(2)}) copy-start(f32[16,256]{1,0:T(8,128)} %sm.3) | copy-start | bytes 49156
  25.9 2.7 %collective-permute-start.2 = (f32[16,256]{1,0:T(8,128)S(1)}, f32[16,256]{1,0:T(8,128)S(1)}, u32[]{:S(2)}, u32[]{:S(2)}) collective-permute-start(f32[16,256]{1,0:T(8,128)S(1)} %get-tuple-element.18.l0), channel_id=1, source_target_pairs={{0,3},{1,0},{2,1},{3,2},{4,7},{5,4},{6,5},{7,6},{8,11},{9,8},{10,9... | collective-permute-start | bytes 49160 | tf_op jit(solution)/shard_map/ppermute | solution.py:345
  26.7 4.1 %collective-permute-start.1 = (f32[16,256]{1,0:T(8,128)S(1)}, f32[16,256]{1,0:T(8,128)S(1)}, u32[]{:S(2)}, u32[]{:S(2)}) collective-permute-start(f32[16,256]{1,0:T(8,128)S(1)} %get-tuple-element.18.l0), channel_id=1, source_target_pairs={{0,2},{1,3},{2,0},{3,1},{4,6},{5,7},{6,4},{7,5},{8,10},{9,11},{10,... | collective-permute-start | bytes 49160 | tf_op jit(solution)/shard_map/ppermute | solution.py:345
  28.1 4.1 %collective-permute-start = (f32[16,256]{1,0:T(8,128)S(1)}, f32[16,256]{1,0:T(8,128)S(1)}, u32[]{:S(2)}, u32[]{:S(2)}) collective-permute-start(f32[16,256]{1,0:T(8,128)S(1)} %get-tuple-element.18.l0), channel_id=1, source_target_pairs={{0,1},{1,2},{2,3},{3,0},{4,5},{5,6},{6,7},{7,4},{8,9},{9,10},{10,1... | collective-permute-start | bytes 49160 | tf_op jit(solution)/shard_map/ppermute | solution.py:345
  37.2 15.4 %copy-start.4 = (f32[8,256]{1,0:T(8,128)S(1)}, f32[8,256]{1,0:T(8,128)}, u32[]{:S(2)}) copy-start(f32[8,256]{1,0:T(8,128)} %get-tuple-element.21.mass) | copy-start | bytes 24580

commit v7 on v6

--- a/solution.py
+++ b/solution.py
@@ -56,9 +56,8 @@
     order[LIST - 1] = n
 
 
-def centroid_kernel(listed, live, sp, sm, tp, tm, row_out, own_out, slice_out, order):
+def centroid_kernel(sp, sm, tp, tm, row_out, own_out, slice_out):
     s, t = lax.axis_index("src"), lax.axis_index("tgt")
-    fill_order(order, listed, live)
     mass = sm[...]
     total = jnp.sum(mass, axis=1, keepdims=True)
     inv = 1.0 / total
@@ -134,8 +133,9 @@
     return jnp.sum(total, axis=0, keepdims=True)
 
 
-def row_kernel(order, sp, tp, tm, r_out, l_out, tab, gt, gf, scol, lrow, *scratch):
+def row_kernel(listed, live, sp, tp, tm, r_out, l_out, order, tab, gt, gf, scol, lrow, *scratch):
     factors = [scratch[2 * u : 2 * u + 2] for u in range(BATCH)]
+    fill_order(order, listed, live)
     n = order[LIST - 1]
     zero = jnp.zeros((CL, PTS), F32)
     source_factors(gf, [sp[d] * ALPHA for d in range(3)], [zero] * 4)
@@ -307,19 +307,19 @@
     stages = [pltpu.VMEM((TGT, 16), BF16), pltpu.VMEM((16, PTS), BF16)] * BATCH
     slots = listed.transpose(1, 2, 0).reshape(SLOTS, CL)
     counts = live.transpose(1, 0)
-    row, own, mass, order = pl.pallas_call(
+    row, own, mass = pl.pallas_call(
         centroid_kernel,
-        out_shape=(shape((128, 128), F32), shape((8, 256), F32), shape((8, 256), F32), shape((LIST,), I32)),
-        in_specs=[SMEM, SMEM] + [VMEM] * 4,
-        out_specs=(VMEM, VMEM, VMEM, SMEM),
+        out_shape=(shape((128, 128), F32), shape((8, 256), F32), shape((8, 256), F32)),
+        in_specs=[VMEM] * 4,
+        out_specs=(VMEM, VMEM, VMEM),
         name="centroids",
-    )(slots, counts, src_pts, src_mass, tgt_pts, tgt_mass)
+    )(src_pts, src_mass, tgt_pts, tgt_mass)
     got = lax.all_to_all(row, ("src", "tgt"), split_axis=0, concat_axis=0, tiled=True)
-    r, where = pl.pallas_call(
+    r, where, order = pl.pallas_call(
         row_kernel,
-        out_shape=(shape((BLOCKS, PTS), F32), shape((128, 128), F32)),
-        in_specs=[SMEM, VMEM, VMEM, VMEM],
-        out_specs=(VMEM, VMEM),
+        out_shape=(shape((BLOCKS, PTS), F32), shape((128, 128), F32), shape((LIST,), I32)),
+        in_specs=[SMEM, SMEM, VMEM, VMEM, VMEM],
+        out_specs=(VMEM, VMEM, SMEM),
         scratch_shapes=[
             pltpu.VMEM((7, TGT, PTS), F32),
             pltpu.VMEM((CL, 16, PTS), F32),
@@ -331,7 +331,7 @@
         cost_estimate=pl.CostEstimate(flops=100_000_000, bytes_accessed=10_000_000, transcendentals=5_000_000),
         compiler_params=params,
         name="rows",
-    )(order, src_pts, tgt_pts, tgt_mass)
+    )(slots, counts, src_pts, tgt_pts, tgt_mass)
     g, part = pl.pallas_call(
         coarse_kernel,
         out_shape=(shape((8, 256), F32), shape((CL, PTS), F32)),

time: 53.9 us -> 54.7 us (1.015)
  blocking collectives: 15.4 us -> 16.1 us
  waiting for transfers between devices: 7.78 us -> 7.13 us
  Pallas kernels: 15 us -> 15.6 us
    all_to_all x1, blocking collectives: 15.4 us -> 16.1 us  [on_device(): lax.all_to_all(sums, 'src', split_axis=0, concat_axis=0, tiled=True)]
    all_to_all x1, waiting for transfers between devices: 3.69 us -> 3.04 us  [on_device(): lax.all_to_all(row, ('src', 'tgt'), split_axis=0, concat_axis=0, tiled=True)]
    pallas_call x1, Pallas kernels: 5.54 us -> 6.19 us  [on_device(): pl.pallas_call(row_kernel, out_shape=(shape((BLOCKS, PTS), F32), shape((1...]
  transfers between devices with their start and end apart: 4 -> 4, of which waited for: 4 -> 4; matrix products, arithmetic and copies ran while one was open for 0% -> 0% of each run, Pallas kernels for 10% -> 11%
where the time goes in v7:
time: 54.7 us; the launch traced here: 53.9 us
  blocking collectives  16.1 us (29%)
  Pallas kernels  15.6 us (29%)
  starting transfers between devices  13.7 us (25%)
  waiting for transfers between devices  7.13 us (13%)
  between operations  0.73 us (1%)
  local copies, waits for them, and re-layouts  0.64 us (1%)
    all_to_all x1, blocking collectives, on_device(): lax.all_to_all(sums, 'src', split_axis=0, concat_axis=0, tiled=True)  16.1 us
    all_to_all x1, starting transfers between devices, on_device(): lax.all_to_all(row, ('src', 'tgt'), split_axis=0, concat_axis=0, tiled=True)  11.5 us
    pallas_call x1, Pallas kernels, on_device(): pl.pallas_call(row_kernel, out_shape=(shape((BLOCKS, PTS), F32), shape((1...  6.19 us
    pallas_call x1, Pallas kernels, on_device(): pl.pallas_call(column_kernel, out_shape=(shape((CL, PTS), F32), shape((32...  5.01 us
    ppermute x3, waiting for transfers between devices, on_device(): lax.ppermute(part, 'tgt', [(i, (i + k) % 4) for i in range(4)])  4.09 us
    all_to_all x1, waiting for transfers between devices, on_device(): lax.all_to_all(row, ('src', 'tgt'), split_axis=0, concat_axis=0, tiled=True)  3.04 us
    pallas_call x1, Pallas kernels, on_device(): pl.pallas_call(centroid_kernel, out_shape=(shape((128, 128), F32), shape(...  2.25 us
    ppermute x3, starting transfers between devices, on_device(): lax.ppermute(part, 'tgt', [(i, (i + k) % 4) for i in range(4)])  2.23 us
  transfers between devices with their start and end apart: 4, of which 4 were waited for; matrix products, arithmetic and copies ran while one was open for 0% of the time, Pallas kernels for 11%

profile of v7, /device:TPU:1, one launch (start us, length us, event | category | flops | bytes accessed | tf_op | source)
XLA Modules:
  0.0 53.9 jit_solution(5650126684882813480)
XLA Ops:
  0.6 0.0 copy-start.1
  0.6 0.0 copy-start
  0.6 2.2 %centroids.1 = (f32[128,128]{1,0:T(8,128)}, f32[8,256]{1,0:T(8,128)}, f32[8,256]{1,0:T(8,128)}) custom-call(f32[3,16,256]{2,1,0:T(8,128)} %sp.5, f32[16,256]{1,0:T(8,128)} %sm.3, f32[3,256,256]{2,1,0:T(8,128)} %tp.5, f32[256,256]{1,0:T(8,128)} %tm.5), custom_call_target="tpu_custom_call" | custom-call | tf_op jit(solution)/shard_map/centroids/pallas_call | solution.py:310
  2.9 0.0 copy-start.2
  2.9 0.0 copy-start.6
  2.9 11.5 %all-to-all-start = ((f32[128,1,128]{2,1,0:T(1,128)}), f32[128,1,128]{2,1,0:T(1,128)S(1)}, u32[]{:S(2)}, u32[]{:S(2)}) async-start(f32[128,1,128]{2,1,0:T(1,128)} %bitcast.11), calls=%async_computation | async-start | bytes 131072 | tf_op jit(solution)/shard_map/all_to_all | solution.py:317
  14.4 0.0 copy-start.7
  14.4 0.0 copy-done.1
  14.4 0.0 copy-done
  14.4 0.0 copy-done.2
  14.4 0.0 copy-done.6
  14.4 0.6 %copy-done.7 = s32[16,1]{0,1:T(1,128)S(1)} copy-done((s32[16,1]{0,1:T(1,128)S(1)}, s32[16,1]{0,1:T(1,128)}, u32[]{:S(2)}) %copy-start.7) | copy-done | bytes 88
  15.1 0.0 copy-start.5
  15.1 6.2 %rows.1 = (f32[128,256]{1,0:T(8,128)S(1)}, f32[128,128]{1,0:T(8,128)S(1)}, s32[160]{0:T(256)S(1)}) custom-call(s32[8,16]{1,0:T(8,128)S(1)} %bitcast.9, s32[1,16]{1,0:T(1,128)S(1)} %bitcast.10, f32[3,16,256]{2,1,0:T(8,128)S(1)} %copy-done.2, f32[3,256,256]{2,1,0:T(8,128)S(1)} %copy-done, f32[256,256]{1,0:T(8,128)S(1)} %copy-done.1), custom_call_target="tpu_custom_call" | custom-call | flops 100000000 | bytes 10000000 | tf_op jit(solution)/shard_map/rows/pallas_call | solution.py:318
  21.2 3.0 %all-to-all-done = f32[128,1,128]{2,1,0:T(1,128)S(1)} async-done(((f32[128,1,128]{2,1,0:T(1,128)}), f32[128,1,128]{2,1,0:T(1,128)S(1)}, u32[]{:S(2)}, u32[]{:S(2)}) %all-to-all-start) | async-done | bytes 65568 | tf_op jit(solution)/shard_map/all_to_all | solution.py:317
  24.3 0.0 copy-done.5
  24.3 0.0 copy-start.3
  24.3 1.5 %coarse.1 = (f32[8,256]{1,0:T(8,128)S(1)}, f32[16,256]{1,0:T(8,128)S(1)}) custom-call(f32[128,128]{1,0:T(8,128)S(1)} %bitcast.8, f32[8,256]{1,0:T(8,128)S(1)} %copy-done.5, f32[128,256]{1,0:T(8,128)S(1)} %get-tuple-element.15.r_in, f32[128,128]{1,0:T(8,128)S(1)} %get-tuple-element.16.l_in), custom_call_target="tpu_custom_call" | custom-call | tf_op jit(solution)/shard_map/coarse/pallas_call | solution.py:335
  25.8 1.2 %collective-permute-start.2 = (f32[16,256]{1,0:T(8,128)S(1)}, f32[16,256]{1,0:T(8,128)S(1)}, u32[]{:S(2)}, u32[]{:S(2)}) collective-permute-start(f32[16,256]{1,0:T(8,128)S(1)} %get-tuple-element.18.l0), channel_id=1, source_target_pairs={{0,3},{1,0},{2,1},{3,2},{4,7},{5,4},{6,5},{7,6},{8,11},{9,8},{10,9... | collective-permute-start | bytes 49160 | tf_op jit(solution)/shard_map/ppermute | solution.py:345
  27.0 1.0 %collective-permute-start.1 = (f32[16,256]{1,0:T(8,128)S(1)}, f32[16,256]{1,0:T(8,128)S(1)}, u32[]{:S(2)}, u32[]{:S(2)}) collective-permute-start(f32[16,256]{1,0:T(8,128)S(1)} %get-tuple-element.18.l0), channel_id=1, source_target_pairs={{0,2},{1,3},{2,0},{3,1},{4,6},{5,7},{6,4},{7,5},{8,10},{9,11},{10,... | collective-permute-start | bytes 49160 | tf_op jit(solution)/shard_map/ppermute | solution.py:345
  28.0 0.0 collective-permute-start
  28.1 0.4 collective-permute-done.2.l3
  28.5 2.6 %collective-permute-done.1.l2 = f32[16,256]{1,0:T(8,128)S(1)} collective-permute-done((f32[16,256]{1,0:T(8,128)S(1)}, f32[16,256]{1,0:T(8,128)S(1)}, u32[]{:S(2)}, u32[]{:S(2)}) %collective-permute-start.1) | collective-permute-done | bytes 16416 | tf_op jit(solution)/shard_map/ppermute | solution.py:345
  31.1 1.0 %collective-permute-done.l1 = f32[16,256]{1,0:T(8,128)S(1)} collective-permute-done((f32[16,256]{1,0:T(8,128)S(1)}, f32[16,256]{1,0:T(8,128)S(1)}, u32[]{:S(2)}, u32[]{:S(2)}) %collective-permute-start) | collective-permute-done | bytes 16416 | tf_op jit(solution)/shard_map/ppermute | solution.py:345
  32.1 0.0 copy-done.3
  32.1 5.0 %columns.1 = (f32[16,256]{1,0:T(8,128)}, f32[32,8,256]{2,1,0:T(8,128)S(1)}) custom-call(s32[160]{0:T(256)S(1)} %get-tuple-element.12.order, f32[8,256]{1,0:T(8,128)S(1)} %get-tuple-element.17.g, f32[3,16,256]{2,1,0:T(8,128)S(1)} %copy-done.2, f32[16,256]{1,0:T(8,128)S(1)} %copy-done.3, f32[3,256,256]{2,1,0:T(8,128)S(1)} %copy-done, ...), custom_call_target="tpu_custom_call" | custom-call | tf_op jit(solution)/shard_map/columns/pallas_call | solution.py:347
  37.2 0.0 copy-start.4
  37.2 16.1 %all_to_all.16.arrived = f32[32,8,256]{2,1,0:T(8,128)S(1)} all-to-all(f32[32,8,256]{2,1,0:T(8,128)S(1)} %get-tuple-element.20), channel_id=1, replica_groups=mesh['src'=32,'tgt'=4] {'src'}, dimensions={0} | all-to-all | bytes 524288 | tf_op jit(solution)/shard_map/all_to_all | solution.py:363
  53.3 0.0 copy-done.4
  53.3 0.6 %final.1 = f32[8,256]{1,0:T(8,128)} custom-call(f32[32,8,256]{2,1,0:T(8,128)S(1)} %all_to_all.16.arrived, f32[8,256]{1,0:T(8,128)S(1)} %copy-done.4, f32[8,256]{1,0:T(8,128)S(1)} %get-tuple-element.17.g), custom_call_target="tpu_custom_call" | custom-call | tf_op jit(solution)/shard_map/final/pallas_call | solution.py:364
Async XLA Ops:
  0.6 13.8 %copy-start.1 = (f32[256,256]{1,0:T(8,128)S(1)}, f32[256,256]{1,0:T(8,128)}, u32[]{:S(2)}) copy-start(f32[256,256]{1,0:T(8,128)} %tm.5) | copy-start | bytes 786436
  0.6 13.8 %copy-start = (f32[3,256,256]{2,1,0:T(8,128)S(1)}, f32[3,256,256]{2,1,0:T(8,128)}, u32[]{:S(2)}) copy-start(f32[3,256,256]{2,1,0:T(8,128)} %tp.5) | copy-start | bytes 2359300
  2.9 11.5 %copy-start.2 = (f32[3,16,256]{2,1,0:T(8,128)S(1)}, f32[3,16,256]{2,1,0:T(8,128)}, u32[]{:S(2)}) copy-start(f32[3,16,256]{2,1,0:T(8,128)} %sp.5) | copy-start | bytes 147460
  2.9 11.5 %copy-start.6 = (s32[16,1,8]{0,2,1:T(8,128)S(1)}, s32[16,1,8]{0,2,1:T(8,128)}, u32[]{:S(2)}) copy-start(s32[16,1,8]{0,2,1:T(8,128)} %param.10) | copy-start | bytes 1540
  2.9 21.4 %all-to-all-start = ((f32[128,1,128]{2,1,0:T(1,128)}), f32[128,1,128]{2,1,0:T(1,128)S(1)}, u32[]{:S(2)}, u32[]{:S(2)}) async-start(f32[128,1,128]{2,1,0:T(1,128)} %bitcast.11), calls=%async_computation | async-start | bytes 131072 | tf_op jit(solution)/shard_map/all_to_all | solution.py:317
  14.4 0.7 %copy-start.7 = (s32[16,1]{0,1:T(1,128)S(1)}, s32[16,1]{0,1:T(1,128)}, u32[]{:S(2)}) copy-start(s32[16,1]{0,1:T(1,128)} %param.11) | copy-start | bytes 196
  15.1 9.2 %copy-start.5 = (f32[8,256]{1,0:T(8,128)S(1)}, f32[8,256]{1,0:T(8,128)}, u32[]{:S(2)}) copy-start(f32[8,256]{1,0:T(8,128)} %get-tuple-element.14.own) | copy-start | bytes 24580
  24.3 7.9 %copy-start.3 = (f32[16,256]{1,0:T(8,128)S(1)}, f32[16,256]{1,0:T(8,128)}, u32[]{:S(2)}) copy-start(f32[16,256]{1,0:T(8,128)} %sm.3) | copy-start | bytes 49156
  25.8 2.7 %collective-permute-start.2 = (f32[16,256]{1,0:T(8,128)S(1)}, f32[16,256]{1,0:T(8,128)S(1)}, u32[]{:S(2)}, u32[]{:S(2)}) collective-permute-start(f32[16,256]{1,0:T(8,128)S(1)} %get-tuple-element.18.l0), channel_id=1, source_target_pairs={{0,3},{1,0},{2,1},{3,2},{4,7},{5,4},{6,5},{7,6},{8,11},{9,8},{10,9... | collective-permute-start | bytes 49160 | tf_op jit(solution)/shard_map/ppermute | solution.py:345
  27.0 4.1 %collective-permute-start.1 = (f32[16,256]{1,0:T(8,128)S(1)}, f32[16,256]{1,0:T(8,128)S(1)}, u32[]{:S(2)}, u32[]{:S(2)}) collective-permute-start(f32[16,256]{1,0:T(8,128)S(1)} %get-tuple-element.18.l0), channel_id=1, source_target_pairs={{0,2},{1,3},{2,0},{3,1},{4,6},{5,7},{6,4},{7,5},{8,10},{9,11},{10,... | collective-permute-start | bytes 49160 | tf_op jit(solution)/shard_map/ppermute | solution.py:345
  28.0 4.1 %collective-permute-start = (f32[16,256]{1,0:T(8,128)S(1)}, f32[16,256]{1,0:T(8,128)S(1)}, u32[]{:S(2)}, u32[]{:S(2)}) collective-permute-start(f32[16,256]{1,0:T(8,128)S(1)} %get-tuple-element.18.l0), channel_id=1, source_target_pairs={{0,1},{1,2},{2,3},{3,0},{4,5},{5,6},{6,7},{7,4},{8,9},{9,10},{10,1... | collective-permute-start | bytes 49160 | tf_op jit(solution)/shard_map/ppermute | solution.py:345
  37.2 16.1 %copy-start.4 = (f32[8,256]{1,0:T(8,128)S(1)}, f32[8,256]{1,0:T(8,128)}, u32[]{:S(2)}) copy-start(f32[8,256]{1,0:T(8,128)} %get-tuple-element.21.mass) | copy-start | bytes 24580

commit v8 on v7

--- a/solution.py
+++ b/solution.py
@@ -15,10 +15,7 @@
 F32, BF16, I32 = jnp.float32, jnp.bfloat16, jnp.int32
 CL, SLOTS, PTS, TGT = 16, 8, 256, 256
 BLOCKS = CL * SLOTS
-SAMPLE = 32
-MARGIN = 90.0
-HUGE = 1e36
-BATCH = 8
+AHEAD = 4
 MANY = 16
 FEW = 4
 PAD = 16
@@ -133,59 +130,46 @@
     return jnp.sum(total, axis=0, keepdims=True)
 
 
-def row_kernel(listed, live, sp, tp, tm, r_out, l_out, order, tab, gt, gf, scol, lrow, *scratch):
-    factors = [scratch[2 * u : 2 * u + 2] for u in range(BATCH)]
+def row_kernel(listed, live, sp, tp, tm, r_out, l_out, order, tab, gt, gf, scol, lrow, *sets):
+    sets = [sets[3 * u : 3 * u + 3] for u in range(AHEAD)]
     fill_order(order, listed, live)
     n = order[LIST - 1]
     zero = jnp.zeros((CL, PTS), F32)
     source_factors(gf, [sp[d] * ALPHA for d in range(3)], [zero] * 4)
     for c in range(CL):
-        gt[c] = jnp.concatenate([gf[h, 16 * c : 16 * c + 16, :] for h in range(2)], axis=1)
+        gt[c] = jnp.concatenate([gf[h, 16 * c : 16 * c + 16, :] for h in range(2)], axis=1).astype(BF16)
     fill_tables(tab, tp, tm)
     lrow[...] = jnp.full((BLOCKS, 128), -1.0, F32)
-    scol[...] = jnp.zeros((BLOCKS, PTS), F32)
-    sub = iota((16, PTS), 0)
-
-    def prepare(i, lhs, rhs):
-        b, at = order[i] >> 8, order[i] & (TGT - 1)
-        left = target_factors(tab, at, None).T
-        right = gt[b & (CL - 1)]
-        seen = jnp.dot(left[:SAMPLE, :], right.astype(BF16), preferred_element_type=F32)
-        shift = jnp.max(seen, axis=0, keepdims=True) + MARGIN
-        for r, piece in enumerate(split3(-shift)):
-            right = jnp.where(sub == 12 + r, piece, right)
-        lhs[...] = left
-        rhs[...] = right.astype(BF16)
-        r_out[pl.ds(b, 1), :] = shift
-        lrow[pl.ds(b, 1), :] = jnp.broadcast_to(at.astype(F32), (1, 128))
-
-    for u in range(BATCH):
-        prepare(u, *factors[u])
+
+    def prepare(i, lhs):
+        at = order[i] & (TGT - 1)
+        lhs[...] = target_factors(tab, at, None).T
+        lrow[pl.ds(order[i] >> 8, 1), :] = jnp.broadcast_to(at.astype(F32), (1, 128))
+
+    for u in range(AHEAD):
+        prepare(u, sets[u][0])
 
     def batch(i, _):
-        at = BATCH * i
-        scores = [jnp.dot(lhs[...], rhs[...], preferred_element_type=F32) for lhs, rhs in factors]
-        for u in range(BATCH):
-            prepare(at + BATCH + u, *factors[u])
-        for u in range(BATCH):
-            scol[pl.ds(order[at + u] >> 8, 1), :] = exp_sum(scores[u])
+        at = AHEAD * i
+        v = [jnp.dot(sets[u][0][...], gt[(order[at + u] >> 8) & (CL - 1)], preferred_element_type=F32) for u in range(AHEAD)]
+        for u in range(AHEAD):
+            prepare(at + AHEAD + u, sets[u][0])
+        for u in range(AHEAD):
+            lhs, score, tops = sets[u]
+            top_old = tops[...]
+            total = jnp.zeros((8, PTS), F32)
+            top = jnp.full((8, PTS), NEG, F32)
+            for j in range(0, TGT, 8):
+                total = total + jnp.exp2(score[j : j + 8, :] - top_old)
+                score[j : j + 8, :] = v[u][j : j + 8, :]
+                top = jnp.maximum(top, v[u][j : j + 8, :])
+            tops[...] = jnp.broadcast_to(jnp.max(top, axis=0, keepdims=True), (8, PTS))
+            old = order[jnp.maximum(at - AHEAD + u, 0)] >> 8
+            r_out[pl.ds(old, 1), :] = top_old[0:1, :]
+            scol[pl.ds(old, 1), :] = jnp.sum(total, axis=0, keepdims=True)
         return 0
 
-    lax.fori_loop(0, (n + BATCH - 1) // BATCH, batch, 0)
-
-    @pl.when(jnp.max(scol[...]) > HUGE)
-    def _():
-        def exact(i, _):
-            b = order[i] >> 8
-            left = target_factors(tab, order[i] & (TGT - 1), None).T
-            v = jnp.dot(left, gt[b & (CL - 1)].astype(BF16), preferred_element_type=F32)
-            top = jnp.max(v, axis=0, keepdims=True)
-            r_out[pl.ds(b, 1), :] = top
-            scol[pl.ds(b, 1), :] = jnp.sum(jnp.exp2(v - top), axis=0, keepdims=True)
-            return 0
-
-        lax.fori_loop(0, n, exact, 0)
-
+    lax.fori_loop(0, (n + AHEAD - 1) // AHEAD + 1, batch, 0)
     xn = (-0.5 * ALPHA) * (sp[0] * sp[0] + sp[1] * sp[1] + sp[2] * sp[2])
     r = r_out[...] + jnp.log2(scol[...])
     r = (r.reshape(SLOTS, CL, PTS) + xn[None]).reshape(BLOCKS, PTS)
@@ -304,7 +288,7 @@
 def on_device(src_pts, src_mass, tgt_pts, tgt_mass, listed, live):
     shape = jax.ShapeDtypeStruct
     params = pltpu.CompilerParams(vmem_limit_bytes=LIMIT)
-    stages = [pltpu.VMEM((TGT, 16), BF16), pltpu.VMEM((16, PTS), BF16)] * BATCH
+    stages = [pltpu.VMEM((TGT, 16), BF16), pltpu.VMEM((TGT, PTS), F32), pltpu.VMEM((8, PTS), F32)] * AHEAD
     slots = listed.transpose(1, 2, 0).reshape(SLOTS, CL)
     counts = live.transpose(1, 0)
     row, own, mass = pl.pallas_call(
@@ -322,7 +306,7 @@
         out_specs=(VMEM, VMEM, SMEM),
         scratch_shapes=[
             pltpu.VMEM((7, TGT, PTS), F32),
-            pltpu.VMEM((CL, 16, PTS), F32),
+            pltpu.VMEM((CL, 16, PTS), BF16),
             pltpu.VMEM((2, CL * 16, 128), F32),
             pltpu.VMEM((BLOCKS, PTS), F32),
             pltpu.VMEM((BLOCKS, 128), F32),

time: 54.7 us -> 55.3 us (1.011)
  blocking collectives: 16.1 us -> 17.4 us
    all_to_all x1, blocking collectives: 16.1 us -> 17.4 us  [on_device(): lax.all_to_all(sums, 'src', split_axis=0, concat_axis=0, tiled=True)]
  transfers between devices with their start and end apart: 4 -> 4, of which waited for: 4 -> 4; matrix products, arithmetic and copies ran while one was open for 0% -> 0% of each run, Pallas kernels for 11% -> 12%
where the time goes in v8:
time: 55.3 us; the launch traced here: 55 us
  blocking collectives  17.4 us (31%)
  Pallas kernels  15.5 us (28%)
  starting transfers between devices  13.7 us (25%)
  waiting for transfers between devices  6.94 us (13%)
  between operations  0.73 us (1%)
  local copies, waits for them, and re-layouts  0.64 us (1%)
    all_to_all x1, blocking collectives, on_device(): lax.all_to_all(sums, 'src', split_axis=0, concat_axis=0, tiled=True)  17.4 us
    all_to_all x1, starting transfers between devices, on_device(): lax.all_to_all(row, ('src', 'tgt'), split_axis=0, concat_axis=0, tiled=True)  11.5 us
    pallas_call x1, Pallas kernels, on_device(): pl.pallas_call(row_kernel, out_shape=(shape((BLOCKS, PTS), F32), shape((1...  6.39 us
    pallas_call x1, Pallas kernels, on_device(): pl.pallas_call(column_kernel, out_shape=(shape((CL, PTS), F32), shape((32...  4.71 us
    ppermute x3, waiting for transfers between devices, on_device(): lax.ppermute(part, 'tgt', [(i, (i + k) % 4) for i in range(4)])  4.09 us
    all_to_all x1, waiting for transfers between devices, on_device(): lax.all_to_all(row, ('src', 'tgt'), split_axis=0, concat_axis=0, tiled=True)  2.84 us
    pallas_call x1, Pallas kernels, on_device(): pl.pallas_call(centroid_kernel, out_shape=(shape((128, 128), F32), shape(...  2.25 us
    ppermute x3, starting transfers between devices, on_device(): lax.ppermute(part, 'tgt', [(i, (i + k) % 4) for i in range(4)])  2.23 us
  transfers between devices with their start and end apart: 4, of which 4 were waited for; matrix products, arithmetic and copies ran while one was open for 0% of the time, Pallas kernels for 12%

profile of v8, /device:TPU:1, one launch (start us, length us, event | category | flops | bytes accessed | tf_op | source)
XLA Modules:
  0.0 55.0 jit_solution(14565920871604433079)
XLA Ops:
  0.6 0.0 copy-start.1
  0.6 0.0 copy-start
  0.6 2.2 %centroids.1 = (f32[128,128]{1,0:T(8,128)}, f32[8,256]{1,0:T(8,128)}, f32[8,256]{1,0:T(8,128)}) custom-call(f32[3,16,256]{2,1,0:T(8,128)} %sp.5, f32[16,256]{1,0:T(8,128)} %sm.3, f32[3,256,256]{2,1,0:T(8,128)} %tp.5, f32[256,256]{1,0:T(8,128)} %tm.5), custom_call_target="tpu_custom_call" | custom-call | tf_op jit(solution)/shard_map/centroids/pallas_call | solution.py:294
  2.9 0.0 copy-start.2
  2.9 0.0 copy-start.6
  2.9 11.5 %all-to-all-start = ((f32[128,1,128]{2,1,0:T(1,128)}), f32[128,1,128]{2,1,0:T(1,128)S(1)}, u32[]{:S(2)}, u32[]{:S(2)}) async-start(f32[128,1,128]{2,1,0:T(1,128)} %bitcast.11), calls=%async_computation | async-start | bytes 131072 | tf_op jit(solution)/shard_map/all_to_all | solution.py:301
  14.4 0.0 copy-start.7
  14.4 0.0 copy-done.1
  14.4 0.0 copy-done
  14.4 0.0 copy-done.2
  14.4 0.0 copy-done.6
  14.4 0.6 %copy-done.7 = s32[16,1]{0,1:T(1,128)S(1)} copy-done((s32[16,1]{0,1:T(1,128)S(1)}, s32[16,1]{0,1:T(1,128)}, u32[]{:S(2)}) %copy-start.7) | copy-done | bytes 88
  15.1 0.0 copy-start.5
  15.1 6.4 %rows.1 = (f32[128,256]{1,0:T(8,128)S(1)}, f32[128,128]{1,0:T(8,128)S(1)}, s32[160]{0:T(256)S(1)}) custom-call(s32[8,16]{1,0:T(8,128)S(1)} %bitcast.9, s32[1,16]{1,0:T(1,128)S(1)} %bitcast.10, f32[3,16,256]{2,1,0:T(8,128)S(1)} %copy-done.2, f32[3,256,256]{2,1,0:T(8,128)S(1)} %copy-done, f32[256,256]{1,0:T(8,128)S(1)} %copy-done.1), custom_call_target="tpu_custom_call" | custom-call | flops 100000000 | bytes 10000000 | tf_op jit(solution)/shard_map/rows/pallas_call | solution.py:302
  21.4 2.8 %all-to-all-done = f32[128,1,128]{2,1,0:T(1,128)S(1)} async-done(((f32[128,1,128]{2,1,0:T(1,128)}), f32[128,1,128]{2,1,0:T(1,128)S(1)}, u32[]{:S(2)}, u32[]{:S(2)}) %all-to-all-start) | async-done | bytes 65568 | tf_op jit(solution)/shard_map/all_to_all | solution.py:301
  24.3 0.0 copy-done.5
  24.3 0.0 copy-start.3
  24.3 1.5 %coarse.1 = (f32[8,256]{1,0:T(8,128)S(1)}, f32[16,256]{1,0:T(8,128)S(1)}) custom-call(f32[128,128]{1,0:T(8,128)S(1)} %bitcast.8, f32[8,256]{1,0:T(8,128)S(1)} %copy-done.5, f32[128,256]{1,0:T(8,128)S(1)} %get-tuple-element.15.r_in, f32[128,128]{1,0:T(8,128)S(1)} %get-tuple-element.16.l_in), custom_call_target="tpu_custom_call" | custom-call | tf_op jit(solution)/shard_map/coarse/pallas_call | solution.py:319
  25.8 0.9 %collective-permute-start.2 = (f32[16,256]{1,0:T(8,128)S(1)}, f32[16,256]{1,0:T(8,128)S(1)}, u32[]{:S(2)}, u32[]{:S(2)}) collective-permute-start(f32[16,256]{1,0:T(8,128)S(1)} %get-tuple-element.18.l0), channel_id=1, source_target_pairs={{0,3},{1,0},{2,1},{3,2},{4,7},{5,4},{6,5},{7,6},{8,11},{9,8},{10,9... | collective-permute-start | bytes 49160 | tf_op jit(solution)/shard_map/ppermute | solution.py:329
  26.7 1.4 %collective-permute-start.1 = (f32[16,256]{1,0:T(8,128)S(1)}, f32[16,256]{1,0:T(8,128)S(1)}, u32[]{:S(2)}, u32[]{:S(2)}) collective-permute-start(f32[16,256]{1,0:T(8,128)S(1)} %get-tuple-element.18.l0), channel_id=1, source_target_pairs={{0,2},{1,3},{2,0},{3,1},{4,6},{5,7},{6,4},{7,5},{8,10},{9,11},{10,... | collective-permute-start | bytes 49160 | tf_op jit(solution)/shard_map/ppermute | solution.py:329
  28.0 0.0 collective-permute-start
  28.1 0.4 collective-permute-done.2.l3
  28.5 2.3 %collective-permute-done.1.l2 = f32[16,256]{1,0:T(8,128)S(1)} collective-permute-done((f32[16,256]{1,0:T(8,128)S(1)}, f32[16,256]{1,0:T(8,128)S(1)}, u32[]{:S(2)}, u32[]{:S(2)}) %collective-permute-start.1) | collective-permute-done | bytes 16416 | tf_op jit(solution)/shard_map/ppermute | solution.py:329
  30.8 1.4 %collective-permute-done.l1 = f32[16,256]{1,0:T(8,128)S(1)} collective-permute-done((f32[16,256]{1,0:T(8,128)S(1)}, f32[16,256]{1,0:T(8,128)S(1)}, u32[]{:S(2)}, u32[]{:S(2)}) %collective-permute-start) | collective-permute-done | bytes 16416 | tf_op jit(solution)/shard_map/ppermute | solution.py:329
  32.1 0.0 copy-done.3
  32.1 4.7 %columns.1 = (f32[16,256]{1,0:T(8,128)}, f32[32,8,256]{2,1,0:T(8,128)S(1)}) custom-call(s32[160]{0:T(256)S(1)} %get-tuple-element.12.order, f32[8,256]{1,0:T(8,128)S(1)} %get-tuple-element.17.g, f32[3,16,256]{2,1,0:T(8,128)S(1)} %copy-done.2, f32[16,256]{1,0:T(8,128)S(1)} %copy-done.3, f32[3,256,256]{2,1,0:T(8,128)S(1)} %copy-done, ...), custom_call_target="tpu_custom_call" | custom-call | tf_op jit(solution)/shard_map/columns/pallas_call | solution.py:331
  36.9 0.0 copy-start.4
  36.9 17.4 %all_to_all.16.arrived = f32[32,8,256]{2,1,0:T(8,128)S(1)} all-to-all(f32[32,8,256]{2,1,0:T(8,128)S(1)} %get-tuple-element.20), channel_id=1, replica_groups=mesh['src'=32,'tgt'=4] {'src'}, dimensions={0} | all-to-all | bytes 524288 | tf_op jit(solution)/shard_map/all_to_all | solution.py:347
  54.3 0.0 copy-done.4
  54.3 0.6 %final.1 = f32[8,256]{1,0:T(8,128)} custom-call(f32[32,8,256]{2,1,0:T(8,128)S(1)} %all_to_all.16.arrived, f32[8,256]{1,0:T(8,128)S(1)} %copy-done.4, f32[8,256]{1,0:T(8,128)S(1)} %get-tuple-element.17.g), custom_call_target="tpu_custom_call" | custom-call | tf_op jit(solution)/shard_map/final/pallas_call | solution.py:348
Async XLA Ops:
  0.6 13.8 %copy-start.1 = (f32[256,256]{1,0:T(8,128)S(1)}, f32[256,256]{1,0:T(8,128)}, u32[]{:S(2)}) copy-start(f32[256,256]{1,0:T(8,128)} %tm.5) | copy-start | bytes 786436
  0.6 13.8 %copy-start = (f32[3,256,256]{2,1,0:T(8,128)S(1)}, f32[3,256,256]{2,1,0:T(8,128)}, u32[]{:S(2)}) copy-start(f32[3,256,256]{2,1,0:T(8,128)} %tp.5) | copy-start | bytes 2359300
  2.9 11.5 %copy-start.2 = (f32[3,16,256]{2,1,0:T(8,128)S(1)}, f32[3,16,256]{2,1,0:T(8,128)}, u32[]{:S(2)}) copy-start(f32[3,16,256]{2,1,0:T(8,128)} %sp.5) | copy-start | bytes 147460
  2.9 11.5 %copy-start.6 = (s32[16,1,8]{0,2,1:T(8,128)S(1)}, s32[16,1,8]{0,2,1:T(8,128)}, u32[]{:S(2)}) copy-start(s32[16,1,8]{0,2,1:T(8,128)} %param.10) | copy-start | bytes 1540
  2.9 21.4 %all-to-all-start = ((f32[128,1,128]{2,1,0:T(1,128)}), f32[128,1,128]{2,1,0:T(1,128)S(1)}, u32[]{:S(2)}, u32[]{:S(2)}) async-start(f32[128,1,128]{2,1,0:T(1,128)} %bitcast.11), calls=%async_computation | async-start | bytes 131072 | tf_op jit(solution)/shard_map/all_to_all | solution.py:301
  14.4 0.7 %copy-start.7 = (s32[16,1]{0,1:T(1,128)S(1)}, s32[16,1]{0,1:T(1,128)}, u32[]{:S(2)}) copy-start(s32[16,1]{0,1:T(1,128)} %param.11) | copy-start | bytes 196
  15.1 9.2 %copy-start.5 = (f32[8,256]{1,0:T(8,128)S(1)}, f32[8,256]{1,0:T(8,128)}, u32[]{:S(2)}) copy-start(f32[8,256]{1,0:T(8,128)} %get-tuple-element.14.own) | copy-start | bytes 24580
  24.3 7.9 %copy-start.3 = (f32[16,256]{1,0:T(8,128)S(1)}, f32[16,256]{1,0:T(8,128)}, u32[]{:S(2)}) copy-start(f32[16,256]{1,0:T(8,128)} %sm.3) | copy-start | bytes 49156
  25.8 2.7 %collective-permute-start.2 = (f32[16,256]{1,0:T(8,128)S(1)}, f32[16,256]{1,0:T(8,128)S(1)}, u32[]{:S(2)}, u32[]{:S(2)}) collective-permute-start(f32[16,256]{1,0:T(8,128)S(1)} %get-tuple-element.18.l0), channel_id=1, source_target_pairs={{0,3},{1,0},{2,1},{3,2},{4,7},{5,4},{6,5},{7,6},{8,11},{9,8},{10,9... | collective-permute-start | bytes 49160 | tf_op jit(solution)/shard_map/ppermute | solution.py:329
  26.7 4.1 %collective-permute-start.1 = (f32[16,256]{1,0:T(8,128)S(1)}, f32[16,256]{1,0:T(8,128)S(1)}, u32[]{:S(2)}, u32[]{:S(2)}) collective-permute-start(f32[16,256]{1,0:T(8,128)S(1)} %get-tuple-element.18.l0), channel_id=1, source_target_pairs={{0,2},{1,3},{2,0},{3,1},{4,6},{5,7},{6,4},{7,5},{8,10},{9,11},{10,... | collective-permute-start | bytes 49160 | tf_op jit(solution)/shard_map/ppermute | solution.py:329
  28.0 4.1 %collective-permute-start = (f32[16,256]{1,0:T(8,128)S(1)}, f32[16,256]{1,0:T(8,128)S(1)}, u32[]{:S(2)}, u32[]{:S(2)}) collective-permute-start(f32[16,256]{1,0:T(8,128)S(1)} %get-tuple-element.18.l0), channel_id=1, source_target_pairs={{0,1},{1,2},{2,3},{3,0},{4,5},{5,6},{6,7},{7,4},{8,9},{9,10},{10,1... | collective-permute-start | bytes 49160 | tf_op jit(solution)/shard_map/ppermute | solution.py:329
  36.9 17.4 %copy-start.4 = (f32[8,256]{1,0:T(8,128)S(1)}, f32[8,256]{1,0:T(8,128)}, u32[]{:S(2)}) copy-start(f32[8,256]{1,0:T(8,128)} %get-tuple-element.21.mass) | copy-start | bytes 24580

commit v9 on v8

--- a/solution.py
+++ b/solution.py
@@ -182,14 +182,14 @@
     turned = table.T
     high = bf16_part(ALPHA * table)
     mid = bf16_part(ALPHA * table - high)
-    lane = iota((256, 64), 1)
+    lane = iota((256, 128), 1)
     r = lane & 15
     d = (r >= 3).astype(I32) + (r >= 6).astype(I32)
     wanted = 4 * d + (lane >> 4) + jnp.where(r - 3 * d == 1, 128, 0)
-    pick = jnp.where((r < 9) & (iota((256, 64), 0) == wanted), 1.0, 0.0).astype(BF16)
+    pick = jnp.where((r < 9) & (lane < 64) & (iota((256, 128), 0) == wanted), 1.0, 0.0).astype(BF16)
     left = jnp.dot(jnp.concatenate([high, mid], axis=1).astype(BF16), pick, preferred_element_type=F32)
-    r = iota((128, 64), 1) & 15
-    left = jnp.where((r >= 9) & (r < 12), 1.0, left).astype(BF16)
+    r = iota((128, 128), 1) & 15
+    left = jnp.where((r >= 9) & (r < 12), 1.0, left)
 
     def target_rows(y, mass):
         rows = []
@@ -208,12 +208,11 @@
     tiles = target_rows([turned[16 + 8 * d : 24 + 8 * d, :] for d in range(3)], turned[40:48, :])
     rights = [jnp.concatenate([stacked(tiles, 2 * p), stacked(tiles, 2 * p + 1)], axis=1) for p in range(4)]
     mine = stacked(target_rows([own[d : d + 1, :] for d in range(3)], own[3:4, :]), 0)
-    zero = jnp.zeros((16, TGT), BF16)
     for ci in range(4):
-
-        def score(right):
-            placed = jnp.concatenate([right if k == ci else zero for k in range(4)], axis=0)
-            return jnp.dot(left, placed, preferred_element_type=F32)
+        own_lanes = (left if ci == 0 else pltpu.roll(left, 128 - 16 * ci, 1))[:, :16].astype(BF16)
+
+        def score(right, own_lanes=own_lanes):
+            return jnp.dot(own_lanes, right, preferred_element_type=F32)
 
         peak = None
         for p, right in enumerate(rights):

time: 55.3 us -> 54.9 us (level)
  Pallas kernels: 15.5 us -> 16.8 us
  waiting for transfers between devices: 6.94 us -> 6.07 us
  blocking collectives: 17.4 us -> 16.6 us
    pallas_call x1, Pallas kernels: 6.39 us -> 7.25 us  [on_device(): pl.pallas_call(row_kernel, out_shape=(shape((BLOCKS, PTS), F32), shape((1...]
    all_to_all x1, waiting for transfers between devices: 2.84 us -> 1.98 us  [on_device(): lax.all_to_all(row, ('src', 'tgt'), split_axis=0, concat_axis=0, tiled=True)]
    all_to_all x1, blocking collectives: 17.4 us -> 16.6 us  [on_device(): lax.all_to_all(sums, 'src', split_axis=0, concat_axis=0, tiled=True)]
  transfers between devices with their start and end apart: 4 -> 4, of which waited for: 4 -> 4; matrix products, arithmetic and copies ran while one was open for 0% -> 0% of each run, Pallas kernels for 12% -> 13%
where the time goes in v9:
time: 54.9 us; the launch traced here: 54.6 us
  Pallas kernels  16.8 us (31%)
  blocking collectives  16.6 us (30%)
  starting transfers between devices  13.7 us (25%)
  waiting for transfers between devices  6.07 us (11%)
  between operations  0.73 us (1%)
  local copies, waits for them, and re-layouts  0.64 us (1%)
    all_to_all x1, blocking collectives, on_device(): lax.all_to_all(sums, 'src', split_axis=0, concat_axis=0, tiled=True)  16.6 us
    all_to_all x1, starting transfers between devices, on_device(): lax.all_to_all(row, ('src', 'tgt'), split_axis=0, concat_axis=0, tiled=True)  11.5 us
    pallas_call x1, Pallas kernels, on_device(): pl.pallas_call(row_kernel, out_shape=(shape((BLOCKS, PTS), F32), shape((1...  7.25 us
    pallas_call x1, Pallas kernels, on_device(): pl.pallas_call(column_kernel, out_shape=(shape((CL, PTS), F32), shape((32...  5.12 us
    ppermute x3, waiting for transfers between devices, on_device(): lax.ppermute(part, 'tgt', [(i, (i + k) % 4) for i in range(4)])  4.09 us
    pallas_call x1, Pallas kernels, on_device(): pl.pallas_call(centroid_kernel, out_shape=(shape((128, 128), F32), shape(...  2.25 us
    ppermute x3, starting transfers between devices, on_device(): lax.ppermute(part, 'tgt', [(i, (i + k) % 4) for i in range(4)])  2.23 us
    all_to_all x1, waiting for transfers between devices, on_device(): lax.all_to_all(row, ('src', 'tgt'), split_axis=0, concat_axis=0, tiled=True)  1.98 us
  transfers between devices with their start and end apart: 4, of which 4 were waited for; matrix products, arithmetic and copies ran while one was open for 0% of the time, Pallas kernels for 13%

profile of v9, /device:TPU:1, one launch (start us, length us, event | category | flops | bytes accessed | tf_op | source)
XLA Modules:
  0.0 54.6 jit_solution(8726266838813315468)
XLA Ops:
  0.6 0.0 copy-start.1
  0.6 0.0 copy-start
  0.6 2.2 %centroids.1 = (f32[128,128]{1,0:T(8,128)}, f32[8,256]{1,0:T(8,128)}, f32[8,256]{1,0:T(8,128)}) custom-call(f32[3,16,256]{2,1,0:T(8,128)} %sp.5, f32[16,256]{1,0:T(8,128)} %sm.3, f32[3,256,256]{2,1,0:T(8,128)} %tp.5, f32[256,256]{1,0:T(8,128)} %tm.5), custom_call_target="tpu_custom_call" | custom-call | tf_op jit(solution)/shard_map/centroids/pallas_call | solution.py:293
  2.9 0.0 copy-start.2
  2.9 0.0 copy-start.6
  2.9 11.5 %all-to-all-start = ((f32[128,1,128]{2,1,0:T(1,128)}), f32[128,1,128]{2,1,0:T(1,128)S(1)}, u32[]{:S(2)}, u32[]{:S(2)}) async-start(f32[128,1,128]{2,1,0:T(1,128)} %bitcast.11), calls=%async_computation | async-start | bytes 131072 | tf_op jit(solution)/shard_map/all_to_all | solution.py:300
  14.4 0.0 copy-start.7
  14.4 0.0 copy-done.1
  14.4 0.0 copy-done
  14.4 0.0 copy-done.2
  14.4 0.0 copy-done.6
  14.4 0.6 %copy-done.7 = s32[16,1]{0,1:T(1,128)S(1)} copy-done((s32[16,1]{0,1:T(1,128)S(1)}, s32[16,1]{0,1:T(1,128)}, u32[]{:S(2)}) %copy-start.7) | copy-done | bytes 88
  15.1 0.0 copy-start.5
  15.1 7.3 %rows.1 = (f32[128,256]{1,0:T(8,128)S(1)}, f32[128,128]{1,0:T(8,128)S(1)}, s32[160]{0:T(256)S(1)}) custom-call(s32[8,16]{1,0:T(8,128)S(1)} %bitcast.9, s32[1,16]{1,0:T(1,128)S(1)} %bitcast.10, f32[3,16,256]{2,1,0:T(8,128)S(1)} %copy-done.2, f32[3,256,256]{2,1,0:T(8,128)S(1)} %copy-done, f32[256,256]{1,0:T(8,128)S(1)} %copy-done.1), custom_call_target="tpu_custom_call" | custom-call | flops 100000000 | bytes 10000000 | tf_op jit(solution)/shard_map/rows/pallas_call | solution.py:301
  22.3 2.0 %all-to-all-done = f32[128,1,128]{2,1,0:T(1,128)S(1)} async-done(((f32[128,1,128]{2,1,0:T(1,128)}), f32[128,1,128]{2,1,0:T(1,128)S(1)}, u32[]{:S(2)}, u32[]{:S(2)}) %all-to-all-start) | async-done | bytes 65568 | tf_op jit(solution)/shard_map/all_to_all | solution.py:300
  24.3 0.0 copy-done.5
  24.3 0.0 copy-start.3
  24.3 1.5 %coarse.1 = (f32[8,256]{1,0:T(8,128)S(1)}, f32[16,256]{1,0:T(8,128)S(1)}) custom-call(f32[128,128]{1,0:T(8,128)S(1)} %bitcast.8, f32[8,256]{1,0:T(8,128)S(1)} %copy-done.5, f32[128,256]{1,0:T(8,128)S(1)} %get-tuple-element.15.r_in, f32[128,128]{1,0:T(8,128)S(1)} %get-tuple-element.16.l_in), custom_call_target="tpu_custom_call" | custom-call | tf_op jit(solution)/shard_map/coarse/pallas_call | solution.py:318
  25.8 0.9 %collective-permute-start.2 = (f32[16,256]{1,0:T(8,128)S(1)}, f32[16,256]{1,0:T(8,128)S(1)}, u32[]{:S(2)}, u32[]{:S(2)}) collective-permute-start(f32[16,256]{1,0:T(8,128)S(1)} %get-tuple-element.18.l0), channel_id=1, source_target_pairs={{0,3},{1,0},{2,1},{3,2},{4,7},{5,4},{6,5},{7,6},{8,11},{9,8},{10,9... | collective-permute-start | bytes 49160 | tf_op jit(solution)/shard_map/ppermute | solution.py:328
  26.7 1.4 %collective-permute-start.1 = (f32[16,256]{1,0:T(8,128)S(1)}, f32[16,256]{1,0:T(8,128)S(1)}, u32[]{:S(2)}, u32[]{:S(2)}) collective-permute-start(f32[16,256]{1,0:T(8,128)S(1)} %get-tuple-element.18.l0), channel_id=1, source_target_pairs={{0,2},{1,3},{2,0},{3,1},{4,6},{5,7},{6,4},{7,5},{8,10},{9,11},{10,... | collective-permute-start | bytes 49160 | tf_op jit(solution)/shard_map/ppermute | solution.py:328
  28.1 0.0 collective-permute-start
  28.1 0.4 collective-permute-done.2.l3
  28.5 2.3 %collective-permute-done.1.l2 = f32[16,256]{1,0:T(8,128)S(1)} collective-permute-done((f32[16,256]{1,0:T(8,128)S(1)}, f32[16,256]{1,0:T(8,128)S(1)}, u32[]{:S(2)}, u32[]{:S(2)}) %collective-permute-start.1) | collective-permute-done | bytes 16416 | tf_op jit(solution)/shard_map/ppermute | solution.py:328
  30.8 1.4 %collective-permute-done.l1 = f32[16,256]{1,0:T(8,128)S(1)} collective-permute-done((f32[16,256]{1,0:T(8,128)S(1)}, f32[16,256]{1,0:T(8,128)S(1)}, u32[]{:S(2)}, u32[]{:S(2)}) %collective-permute-start) | collective-permute-done | bytes 16416 | tf_op jit(solution)/shard_map/ppermute | solution.py:328
  32.2 0.0 copy-done.3
  32.2 5.1 %columns.1 = (f32[16,256]{1,0:T(8,128)}, f32[32,8,256]{2,1,0:T(8,128)S(1)}) custom-call(s32[160]{0:T(256)S(1)} %get-tuple-element.12.order, f32[8,256]{1,0:T(8,128)S(1)} %get-tuple-element.17.g, f32[3,16,256]{2,1,0:T(8,128)S(1)} %copy-done.2, f32[16,256]{1,0:T(8,128)S(1)} %copy-done.3, f32[3,256,256]{2,1,0:T(8,128)S(1)} %copy-done, ...), custom_call_target="tpu_custom_call" | custom-call | tf_op jit(solution)/shard_map/columns/pallas_call | solution.py:330
  37.3 0.0 copy-start.4
  37.3 16.6 %all_to_all.16.arrived = f32[32,8,256]{2,1,0:T(8,128)S(1)} all-to-all(f32[32,8,256]{2,1,0:T(8,128)S(1)} %get-tuple-element.20), channel_id=1, replica_groups=mesh['src'=32,'tgt'=4] {'src'}, dimensions={0} | all-to-all | bytes 524288 | tf_op jit(solution)/shard_map/all_to_all | solution.py:346
  53.9 0.0 copy-done.4
  53.9 0.6 %final.1 = f32[8,256]{1,0:T(8,128)} custom-call(f32[32,8,256]{2,1,0:T(8,128)S(1)} %all_to_all.16.arrived, f32[8,256]{1,0:T(8,128)S(1)} %copy-done.4, f32[8,256]{1,0:T(8,128)S(1)} %get-tuple-element.17.g), custom_call_target="tpu_custom_call" | custom-call | tf_op jit(solution)/shard_map/final/pallas_call | solution.py:347
Async XLA Ops:
  0.6 13.8 %copy-start.1 = (f32[256,256]{1,0:T(8,128)S(1)}, f32[256,256]{1,0:T(8,128)}, u32[]{:S(2)}) copy-start(f32[256,256]{1,0:T(8,128)} %tm.5) | copy-start | bytes 786436
  0.6 13.8 %copy-start = (f32[3,256,256]{2,1,0:T(8,128)S(1)}, f32[3,256,256]{2,1,0:T(8,128)}, u32[]{:S(2)}) copy-start(f32[3,256,256]{2,1,0:T(8,128)} %tp.5) | copy-start | bytes 2359300
  2.9 11.5 %copy-start.2 = (f32[3,16,256]{2,1,0:T(8,128)S(1)}, f32[3,16,256]{2,1,0:T(8,128)}, u32[]{:S(2)}) copy-start(f32[3,16,256]{2,1,0:T(8,128)} %sp.5) | copy-start | bytes 147460
  2.9 11.5 %copy-start.6 = (s32[16,1,8]{0,2,1:T(8,128)S(1)}, s32[16,1,8]{0,2,1:T(8,128)}, u32[]{:S(2)}) copy-start(s32[16,1,8]{0,2,1:T(8,128)} %param.10) | copy-start | bytes 1540
  2.9 21.4 %all-to-all-start = ((f32[128,1,128]{2,1,0:T(1,128)}), f32[128,1,128]{2,1,0:T(1,128)S(1)}, u32[]{:S(2)}, u32[]{:S(2)}) async-start(f32[128,1,128]{2,1,0:T(1,128)} %bitcast.11), calls=%async_computation | async-start | bytes 131072 | tf_op jit(solution)/shard_map/all_to_all | solution.py:300
  14.4 0.7 %copy-start.7 = (s32[16,1]{0,1:T(1,128)S(1)}, s32[16,1]{0,1:T(1,128)}, u32[]{:S(2)}) copy-start(s32[16,1]{0,1:T(1,128)} %param.11) | copy-start | bytes 196
  15.1 9.2 %copy-start.5 = (f32[8,256]{1,0:T(8,128)S(1)}, f32[8,256]{1,0:T(8,128)}, u32[]{:S(2)}) copy-start(f32[8,256]{1,0:T(8,128)} %get-tuple-element.14.own) | copy-start | bytes 24580
  24.3 7.9 %copy-start.3 = (f32[16,256]{1,0:T(8,128)S(1)}, f32[16,256]{1,0:T(8,128)}, u32[]{:S(2)}) copy-start(f32[16,256]{1,0:T(8,128)} %sm.3) | copy-start | bytes 49156
  25.8 2.7 %collective-permute-start.2 = (f32[16,256]{1,0:T(8,128)S(1)}, f32[16,256]{1,0:T(8,128)S(1)}, u32[]{:S(2)}, u32[]{:S(2)}) collective-permute-start(f32[16,256]{1,0:T(8,128)S(1)} %get-tuple-element.18.l0), channel_id=1, source_target_pairs={{0,3},{1,0},{2,1},{3,2},{4,7},{5,4},{6,5},{7,6},{8,11},{9,8},{10,9... | collective-permute-start | bytes 49160 | tf_op jit(solution)/shard_map/ppermute | solution.py:328
  26.7 4.1 %collective-permute-start.1 = (f32[16,256]{1,0:T(8,128)S(1)}, f32[16,256]{1,0:T(8,128)S(1)}, u32[]{:S(2)}, u32[]{:S(2)}) collective-permute-start(f32[16,256]{1,0:T(8,128)S(1)} %get-tuple-element.18.l0), channel_id=1, source_target_pairs={{0,2},{1,3},{2,0},{3,1},{4,6},{5,7},{6,4},{7,5},{8,10},{9,11},{10,... | collective-permute-start | bytes 49160 | tf_op jit(solution)/shard_map/ppermute | solution.py:328
  28.1 4.1 %collective-permute-start = (f32[16,256]{1,0:T(8,128)S(1)}, f32[16,256]{1,0:T(8,128)S(1)}, u32[]{:S(2)}, u32[]{:S(2)}) collective-permute-start(f32[16,256]{1,0:T(8,128)S(1)} %get-tuple-element.18.l0), channel_id=1, source_target_pairs={{0,1},{1,2},{2,3},{3,0},{4,5},{5,6},{6,7},{7,4},{8,9},{9,10},{10,1... | collective-permute-start | bytes 49160 | tf_op jit(solution)/shard_map/ppermute | solution.py:328
  37.3 16.6 %copy-start.4 = (f32[8,256]{1,0:T(8,128)S(1)}, f32[8,256]{1,0:T(8,128)}, u32[]{:S(2)}) copy-start(f32[8,256]{1,0:T(8,128)} %get-tuple-element.21.mass) | copy-start | bytes 24580
